TPU v7x, 128 devices: a whole 4x4x4 slice. The times are simulated.
128 devices in a mesh: dp: 2 (over y_hi), ctx: 16 (over z, y_lo, core), tp: 4 (over x).
Axes of the slice: x: 4, y: 4 (y_hi: 2, y_lo: 2; y = y_hi * 2 + y_lo), z: 4, core: 2. Of those that a mesh axis runs over, the one named last changes fastest.
Arguments:
- activations: bfloat16 [16384, 5120], P(('dp', 'ctx')), parts along dimension 0, may hold values from -48 to 48
- residual: bfloat16 [16384, 5120], P(('dp', 'ctx', 'tp')), parts along dimension 0, may hold values from -1.5 to 1.5
- w_query: bfloat16 [5120, 2560], P(None, 'tp'), may hold values from -0.078125 to 0.078125
- w_key: bfloat16 [5120, 512], P(None, 'tp'), may hold values from -0.078125 to 0.078125
- w_value: bfloat16 [5120, 512], P(None, 'tp'), may hold values from -0.078125 to 0.078125
- w_out: bfloat16 [2560, 5120], P('tp'), may hold values from -0.47265625 to 0.47265625
- gain: float32 [5120], replicated, may hold values from 0.5 to 1.5
- ancestors: int32 [128, 16], P(('dp', 'ctx')), parts along dimension 0, may hold values from -1 to 62, as said below
- kept: int32 [128], P(('dp', 'ctx')), parts along dimension 0, may hold values 0 or 1
Outputs:
- normed_out: bfloat16 [16384, 5120], P(('dp', 'ctx', 'tp')), parts along dimension 0
There are 2 independent parts, one for each index of `dp`. A program takes and returns all parts, laid end to end along the dimension named above; an argument that names none is the same for every part. Nothing has to cross between parts.
Inputs may be any that keep to these rules, and one draw needn't show every extreme that they name: Entry l of a block's list is its ancestor block at depth l, earlier in the order; the list holds as many entries as the block's depth and -1 after them; some block has a full list; blocks 0 to 7 are ancestors of every later block.
All inputs are finite; a program needn't handle non-finite values. No bound on the sum of `kept` on one device may be relied on, other than what follows from the above.
Results may differ from a plain program's by a relative error of at most 0.015.
The roundings to bfloat16 on the way count: a program that leaves them out, or rounds other values in their place, can miss the bound.
Values may be sent and summed in bfloat16 or wider, within the bound.
No kernel may reach another device: no remote copies, remote signals or barrier semaphores. Data moves between devices by JAX's collectives and lax.ppermute only.
A program may use at most 256 MiB of HBM per device.

v0:
```python
import math

import jax
import jax.numpy as jnp
from jax import lax
from jax.sharding import PartitionSpec as P

HD = 128
BLK = 128


def attend_block(query_block, key_block, value_block, listed_ok, score_scale):
    slot_count = listed_ok.shape[0]
    blk_rows = query_block.shape[0]
    scores = (
        jnp.einsum("qkgd,nkd->kgqn", query_block, key_block, preferred_element_type=jnp.float32)
        * score_scale
    )
    column = jnp.arange(slot_count * blk_rows, dtype=jnp.int32)
    own_cols = column >= (slot_count - 1) * blk_rows
    offset = column - (slot_count - 1) * blk_rows
    row_ids = jnp.arange(blk_rows, dtype=jnp.int32)
    allowed = jnp.repeat(listed_ok, blk_rows)[None, :] & (
        jnp.logical_not(own_cols)[None, :] | (offset[None, :] <= row_ids[:, None])
    )
    scores = jnp.where(allowed, scores, -jnp.inf)
    row_max = jnp.max(scores, axis=-1, keepdims=True)
    weights = jnp.where(allowed, jnp.exp(scores - row_max), 0.0)
    row_total = jnp.sum(weights, axis=-1, keepdims=True)
    prob_bf = weights.astype(jnp.bfloat16)
    summed = jnp.einsum("kgqn,nkd->qkgd", prob_bf, value_block, preferred_element_type=jnp.float32)
    return summed / jnp.transpose(row_total, (2, 0, 1, 3))


def on_device(activations, residual, w_query, w_key, w_value, w_out, gain, ancestors, kept):
    tok_dev = activations.shape[0]
    blk_dev = ancestors.shape[0]
    kv_local = w_key.shape[1] // HD
    heads_local = w_query.shape[1] // HD
    group_size = heads_local // kv_local
    score_scale = 1.0 / math.sqrt(HD)
    queries = jnp.dot(activations, w_query, preferred_element_type=jnp.float32).astype(jnp.bfloat16)
    key_rows = jnp.dot(activations, w_key, preferred_element_type=jnp.float32).astype(jnp.bfloat16)
    value_rows = jnp.dot(activations, w_value, preferred_element_type=jnp.float32).astype(
        jnp.bfloat16
    )
    position = lax.axis_index("ctx")
    all_keys, all_values = (
        lax.all_gather(key_rows, "ctx", axis=0, tiled=True),
        lax.all_gather(value_rows, "ctx", axis=0, tiled=True),
    )
    key_blocks = all_keys.reshape(-1, BLK, kv_local, HD)
    value_blocks = all_values.reshape(-1, BLK, kv_local, HD)
    own_ids = position * blk_dev + jnp.arange(blk_dev, dtype=jnp.int32)
    key_lists = jnp.concatenate([ancestors, own_ids[:, None]], axis=1)
    query_blocks = queries.reshape(blk_dev, BLK, kv_local, group_size, HD)

    def one_block(block_pair):
        query_block, id_list = block_pair
        listed_ok = id_list >= 0
        safe_ids = jnp.maximum(id_list, 0)
        chosen_keys = key_blocks[safe_ids].reshape(-1, kv_local, HD)
        chosen_values = value_blocks[safe_ids].reshape(-1, kv_local, HD)
        return attend_block(query_block, chosen_keys, chosen_values, listed_ok, score_scale)

    attended = lax.map(one_block, (query_blocks, key_lists))
    head_out = attended.astype(jnp.bfloat16).reshape(tok_dev, heads_local * HD)
    out_rows = residual.shape[0]
    projected = lax.psum_scatter(
        jnp.dot(head_out, w_out, preferred_element_type=jnp.float32).astype(jnp.bfloat16),
        "tp",
        scatter_dimension=0,
        tiled=True,
    ).astype(jnp.float32)
    mixed_rows = residual.astype(jnp.float32) + projected
    mean_square = jnp.mean(mixed_rows * mixed_rows, axis=-1, keepdims=True)
    row_start = lax.axis_index("tp") * out_rows
    keep_rows = lax.dynamic_slice_in_dim(jnp.repeat(kept, BLK), row_start, out_rows, 0).astype(
        jnp.float32
    )
    normed = mixed_rows * lax.rsqrt(mean_square + 1e-06) * gain[None, :] * keep_rows[:, None]
    return normed.astype(jnp.bfloat16)


def solution(mesh):
    in_specs = (
        P(("dp", "ctx"), None),
        P(("dp", "ctx", "tp"), None),
        P(None, "tp"),
        P(None, "tp"),
        P(None, "tp"),
        P("tp", None),
        P(),
        P(("dp", "ctx"), None),
        P(("dp", "ctx")),
    )
    out_specs = P(("dp", "ctx", "tp"), None)
    return jax.shard_map(
        on_device, mesh=mesh, in_specs=in_specs, out_specs=out_specs, check_vma=False
    )
```

profile of v0, /device:TPU:24, one launch (start us, length us, event | category | flops | bytes accessed | tf_op | source)
XLA Modules:
  0.0 217.6 jit_solution(5983307769722376903)
XLA Ops:
  6.5 1.3 copy-done
  7.9 4.7 %convolution_convert_fusion.3 = bf16[512,128]{1,0:T(8,128)(2,1)} fusion(bf16[512,5120]{1,0:T(8,128)(2,1)} %param.11, bf16[5120,128]{1,0:T(8,128)(2,1)S(1)} %copy-done), kind=kOutput, calls=%fused_computation.36 | convolution fusion | flops 671154176 | bytes 6684672 | tf_op jit(solution)/shard_map/dot_general | solution.py:44
  12.6 4.7 %convolution_convert_fusion.2 = bf16[512,128]{1,0:T(8,128)(2,1)} fusion(bf16[512,5120]{1,0:T(8,128)(2,1)} %param.11, bf16[5120,128]{1,0:T(8,128)(2,1)S(1)} %copy-done.7), kind=kOutput, calls=%fused_computation.35 | convolution fusion | flops 671154176 | bytes 6684672 | tf_op jit(solution)/shard_map/dot_general | solution.py:43
  17.3 8.7 %convolution_convert_fusion.1 = bf16[512,640]{1,0:T(8,128)(2,1)S(1)} fusion(bf16[512,5120]{1,0:T(8,128)(2,1)} %param.11, bf16[5120,640]{1,0:T(8,128)(2,1)} %param.13), kind=kOutput, calls=%fused_computation.34 | convolution fusion | flops 3355770880 | bytes 12451840 | tf_op jit(solution)/shard_map/dot_general | solution.py:42
  27.0 21.5 %all-gather.3.cloned.1.call-done = bf16[8192,128]{1,0:T(8,128)(2,1)} async-done(((bf16[512,128]{1,0:T(8,128)(2,1)}), bf16[8192,128]{1,0:T(8,128)(2,1)}) %all-gather.3.cloned.1.call-update) | async-done | bytes 2097168 | tf_op jit(solution)/shard_map/all_gather | solution.py:50
  48.6 35.8 %all-gather.5.cloned.1.call-done = bf16[8192,128]{1,0:T(8,128)(2,1)} async-done(((bf16[512,128]{1,0:T(8,128)(2,1)}), bf16[8192,128]{1,0:T(8,128)(2,1)}) %all-gather.5.cloned.1.call-update) | async-done | bytes 2097168 | tf_op jit(solution)/shard_map/all_gather | solution.py:49
  84.3 56.8 %while.12 = (s32[]{:T(128)}, bf16[4,128,1,5,128]{1,4,3,2,0:T(8,128)(2,1)}, s32[4,17]{1,0:T(4,128)S(1)}, bf16[64,128,1,128]{3,1,0,2:T(8,128)(2,1)}, bf16[64,128,1...) while((s32[]{:T(128)}, bf16[4,128,1,5,128]{1,4,3,2,0:T(8,128)(2,1)}, ...), condition=%wide.region_3.4_spmd, body=%wide.region_0.3_spmd.sunk | while | flops 726489216 | bytes 43985968 | solution.py:66
  84.3 2.2 %gather_fusion.1 = bf16[17,128,128]{2,1,0:T(8,128)(2,1)S(1)} fusion(bf16[64,128,128]{2,1,0:T(8,128)(2,1)} %bitcast.106, s32[1024]{0:T(1024)S(1)} %pad_clamp_fusion.2), kind=kCustom, calls=%fused_computation.1.clone.1 | custom fusion | bytes 1114180 | tf_op jit(solution)/shard_map/while/body/eval_jaxpr/gather | solution.py:62
  86.7 1.8 fusion.51
  90.4 1.4 copy-done.1
  91.9 2.2 %gather_fusion = bf16[17,128,128]{2,1,0:T(8,128)(2,1)S(1)} fusion(bf16[64,128,128]{2,1,0:T(8,128)(2,1)} %bitcast.104, s32[1024]{0:T(1024)S(1)} %pad_clamp_fusion.2), kind=kCustom, calls=%fused_computation.clone.1 | custom fusion | bytes 1114180 | tf_op jit(solution)/shard_map/while/body/eval_jaxpr/gather | solution.py:63
  94.1 4.4 %fusion.54 = bf16[4,128,1,5,128]{1,4,3,2,0:T(8,128)(2,1)} fusion(bf16[4,128,1,5,128]{1,4,3,2,0:T(8,128)(2,1)} %get-tuple-element.158, s32[]{:T(128)} %get-tuple-element.157, bf16[2176,128,1]{1,0,2:T(8,128)(2,1)S(1)} %bitcast.102, f32[1,5,128,2176]{2,3,1,0:T(8,128)} %copy-done.1, f32[5,128]{1,0:T(8,128)S(1)} %get-tuple-element.149, ...), kind=kOutput, calls=%fused_computation.17.clone.1 | convolution fusion | flops 360775680 | bytes 6739456 | tf_op jit(solution)/shard_map/while/body/eval_jaxpr/kgqn,nkd->qkgd/dot_general | solution.py:31
  98.5 2.2 %gather_fusion.1 = bf16[17,128,128]{2,1,0:T(8,128)(2,1)S(1)} fusion(bf16[64,128,128]{2,1,0:T(8,128)(2,1)} %bitcast.106, s32[1024]{0:T(1024)S(1)} %pad_clamp_fusion.2), kind=kCustom, calls=%fused_computation.1.clone.1 | custom fusion | bytes 1114180 | tf_op jit(solution)/shard_map/while/body/eval_jaxpr/gather | solution.py:62
  100.9 1.8 fusion.51
  104.6 1.4 copy-done.1
  106.1 2.2 %gather_fusion = bf16[17,128,128]{2,1,0:T(8,128)(2,1)S(1)} fusion(bf16[64,128,128]{2,1,0:T(8,128)(2,1)} %bitcast.104, s32[1024]{0:T(1024)S(1)} %pad_clamp_fusion.2), kind=kCustom, calls=%fused_computation.clone.1 | custom fusion | bytes 1114180 | tf_op jit(solution)/shard_map/while/body/eval_jaxpr/gather | solution.py:63
  108.3 4.4 %fusion.54 = bf16[4,128,1,5,128]{1,4,3,2,0:T(8,128)(2,1)} fusion(bf16[4,128,1,5,128]{1,4,3,2,0:T(8,128)(2,1)} %get-tuple-element.158, s32[]{:T(128)} %get-tuple-element.157, bf16[2176,128,1]{1,0,2:T(8,128)(2,1)S(1)} %bitcast.102, f32[1,5,128,2176]{2,3,1,0:T(8,128)} %copy-done.1, f32[5,128]{1,0:T(8,128)S(1)} %get-tuple-element.149, ...), kind=kOutput, calls=%fused_computation.17.clone.1 | convolution fusion | flops 360775680 | bytes 6739456 | tf_op jit(solution)/shard_map/while/body/eval_jaxpr/kgqn,nkd->qkgd/dot_general | solution.py:31
  112.7 2.2 %gather_fusion.1 = bf16[17,128,128]{2,1,0:T(8,128)(2,1)S(1)} fusion(bf16[64,128,128]{2,1,0:T(8,128)(2,1)} %bitcast.106, s32[1024]{0:T(1024)S(1)} %pad_clamp_fusion.2), kind=kCustom, calls=%fused_computation.1.clone.1 | custom fusion | bytes 1114180 | tf_op jit(solution)/shard_map/while/body/eval_jaxpr/gather | solution.py:62
  115.1 1.8 fusion.51
  118.8 1.4 copy-done.1
  120.3 2.2 %gather_fusion = bf16[17,128,128]{2,1,0:T(8,128)(2,1)S(1)} fusion(bf16[64,128,128]{2,1,0:T(8,128)(2,1)} %bitcast.104, s32[1024]{0:T(1024)S(1)} %pad_clamp_fusion.2), kind=kCustom, calls=%fused_computation.clone.1 | custom fusion | bytes 1114180 | tf_op jit(solution)/shard_map/while/body/eval_jaxpr/gather | solution.py:63
  122.5 4.4 %fusion.54 = bf16[4,128,1,5,128]{1,4,3,2,0:T(8,128)(2,1)} fusion(bf16[4,128,1,5,128]{1,4,3,2,0:T(8,128)(2,1)} %get-tuple-element.158, s32[]{:T(128)} %get-tuple-element.157, bf16[2176,128,1]{1,0,2:T(8,128)(2,1)S(1)} %bitcast.102, f32[1,5,128,2176]{2,3,1,0:T(8,128)} %copy-done.1, f32[5,128]{1,0:T(8,128)S(1)} %get-tuple-element.149, ...), kind=kOutput, calls=%fused_computation.17.clone.1 | convolution fusion | flops 360775680 | bytes 6739456 | tf_op jit(solution)/shard_map/while/body/eval_jaxpr/kgqn,nkd->qkgd/dot_general | solution.py:31
  126.9 2.2 %gather_fusion.1 = bf16[17,128,128]{2,1,0:T(8,128)(2,1)S(1)} fusion(bf16[64,128,128]{2,1,0:T(8,128)(2,1)} %bitcast.106, s32[1024]{0:T(1024)S(1)} %pad_clamp_fusion.2), kind=kCustom, calls=%fused_computation.1.clone.1 | custom fusion | bytes 1114180 | tf_op jit(solution)/shard_map/while/body/eval_jaxpr/gather | solution.py:62
  129.3 1.8 fusion.51
  133.0 1.4 copy-done.1
  134.5 2.2 %gather_fusion = bf16[17,128,128]{2,1,0:T(8,128)(2,1)S(1)} fusion(bf16[64,128,128]{2,1,0:T(8,128)(2,1)} %bitcast.104, s32[1024]{0:T(1024)S(1)} %pad_clamp_fusion.2), kind=kCustom, calls=%fused_computation.clone.1 | custom fusion | bytes 1114180 | tf_op jit(solution)/shard_map/while/body/eval_jaxpr/gather | solution.py:63
  136.7 4.4 %fusion.54 = bf16[4,128,1,5,128]{1,4,3,2,0:T(8,128)(2,1)} fusion(bf16[4,128,1,5,128]{1,4,3,2,0:T(8,128)(2,1)} %get-tuple-element.158, s32[]{:T(128)} %get-tuple-element.157, bf16[2176,128,1]{1,0,2:T(8,128)(2,1)S(1)} %bitcast.102, f32[1,5,128,2176]{2,3,1,0:T(8,128)} %copy-done.1, f32[5,128]{1,0:T(8,128)S(1)} %get-tuple-element.149, ...), kind=kOutput, calls=%fused_computation.17.clone.1 | convolution fusion | flops 360775680 | bytes 6739456 | tf_op jit(solution)/shard_map/while/body/eval_jaxpr/kgqn,nkd->qkgd/dot_general | solution.py:31
  141.1 1.6 copy.19
  142.7 8.9 %convolution_convert_fusion = bf16[512,5120]{1,0:T(8,128)(2,1)} fusion(bf16[640,5120]{1,0:T(8,128)(2,1)} %param.16, bf16[80,8,4,128]{3,2,1,0:T(4,128)(2,1)S(1)} %bitcast.107), kind=kOutput, calls=%fused_computation.30 | convolution fusion | flops 3358064640 | bytes 12451840 | tf_op jit(solution)/shard_map/dot_general | solution.py:70
  152.4 55.0 %reduce-scatter.2.cloned.1.call-done = bf16[128,5120]{1,0:T(8,128)(2,1)} async-done(((bf16[512,5120]{1,0:T(8,128)(2,1)}), bf16[128,5120]{1,0:T(8,128)(2,1)}) %reduce-scatter.2.cloned.1.call-update) | async-done | bytes 1310736 | tf_op jit(solution)/shard_map/reduce_scatter | solution.py:69
  207.4 1.9 multiply_reduce_fusion
  209.4 1.6 multiply_convert_fusion
  (63 shorter events, 10.1 us)
Async XLA Ops:
  6.5 1.3 copy-start
  6.5 6.0 %copy-start.7 = (bf16[5120,128]{1,0:T(8,128)(2,1)S(1)}, bf16[5120,128]{1,0:T(8,128)(2,1)}, u32[]{:S(2)}) copy-start(bf16[5120,128]{1,0:T(8,128)(2,1)} %param.14) | copy-start | bytes 3932164
  6.5 42.0 %all-gather.3.cloned.1.call-start = ((), (), s32[]{:S(2)}) async-start(), calls=%async_computation.1 | async-start | bytes 2228224 | tf_op jit(solution)/shard_map/all_gather | solution.py:50
  12.5 71.8 %all-gather.5.cloned.1.call-start = ((), (), s32[]{:S(2)}) async-start(), calls=%async_computation.2 | async-start | bytes 2228224 | tf_op jit(solution)/shard_map/all_gather | solution.py:49
  17.3 190.2 %reduce-scatter.2.cloned.1.call-start = ((), (), s32[]{:S(2)}) async-start(), calls=%async_computation.3 | async-start | bytes 6553600 | tf_op jit(solution)/shard_map/reduce_scatter | solution.py:69
  26.0 0.9 copy-start.5
  89.4 2.4 %copy-start.1 = (f32[1,5,128,2176]{2,3,1,0:T(8,128)}, f32[1,5,128,2176]{2,3,1,0:T(8,128)S(1)}, u32[]{:S(2)}) copy-start(f32[1,5,128,2176]{2,3,1,0:T(8,128)S(1)} %get-tuple-element.148) | copy-start | bytes 16711684 | tf_op jit(solution)/shard_map/while
  103.6 2.4 %copy-start.1 = (f32[1,5,128,2176]{2,3,1,0:T(8,128)}, f32[1,5,128,2176]{2,3,1,0:T(8,128)S(1)}, u32[]{:S(2)}) copy-start(f32[1,5,128,2176]{2,3,1,0:T(8,128)S(1)} %get-tuple-element.148) | copy-start | bytes 16711684 | tf_op jit(solution)/shard_map/while
  117.8 2.4 %copy-start.1 = (f32[1,5,128,2176]{2,3,1,0:T(8,128)}, f32[1,5,128,2176]{2,3,1,0:T(8,128)S(1)}, u32[]{:S(2)}) copy-start(f32[1,5,128,2176]{2,3,1,0:T(8,128)S(1)} %get-tuple-element.148) | copy-start | bytes 16711684 | tf_op jit(solution)/shard_map/while
  132.0 2.4 %copy-start.1 = (f32[1,5,128,2176]{2,3,1,0:T(8,128)}, f32[1,5,128,2176]{2,3,1,0:T(8,128)S(1)}, u32[]{:S(2)}) copy-start(f32[1,5,128,2176]{2,3,1,0:T(8,128)S(1)} %get-tuple-element.148) | copy-start | bytes 16711684 | tf_op jit(solution)/shard_map/while
  151.6 0.7 copy-start.6
  151.6 55.8 %copy-start.2 = (bf16[128,5120]{1,0:T(8,128)(2,1)S(1)}, bf16[128,5120]{1,0:T(8,128)(2,1)}, u32[]{:S(2)}) copy-start(bf16[128,5120]{1,0:T(8,128)(2,1)} %param.12) | copy-start | bytes 3932164
  151.6 57.7 %copy-start.4 = (f32[5120]{0:T(1024)S(1)}, f32[5120]{0:T(1024)}, u32[]{:S(2)}) copy-start(f32[5120]{0:T(1024)} %param.17) | copy-start | bytes 61444
  207.4 1.9 copy-start.3
Sparse Core Ops, SparseCore 0:
  12.7 35.8 all-gather.2
  50.3 34.0 all-gather.4
  151.8 55.6 reduce-scatter.1
where the time goes:
time: 219 us; the launch traced here: 218 us
  waiting for transfers between devices  112 us (51%)
  matrix products  48.3 us (22%)
  local copies, waits for them, and re-layouts  28.5 us (13%)
  other arithmetic  15 us (7%)
  between operations  13.2 us (6%)
    reduce_scatter x1, waiting for transfers between devices, on_device(): lax.psum_scatter(jnp.dot(head_out, w_out, preferred_element_type=jnp.floa...  55 us
    all_gather x1, waiting for transfers between devices, on_device(): lax.all_gather(key_rows, 'ctx', axis=0, tiled=True)  35.8 us
    all_gather x1, waiting for transfers between devices, on_device(): lax.all_gather(value_rows, 'ctx', axis=0, tiled=True)  21.5 us
    dot_general x4, matrix products, attend_block(): jnp.einsum('kgqn,nkd->qkgd', prob_bf, value_block, preferred_element_type...  17.5 us
    gather x4, local copies, waits for them, and re-layouts, one_block(): chosen_keys = key_blocks[safe_ids].reshape(-1, kv_local, HD)  8.97 us
    gather x4, local copies, waits for them, and re-layouts, one_block(): chosen_values = value_blocks[safe_ids].reshape(-1, kv_local, HD)  8.97 us
    dot_general x1, matrix products, on_device(): jnp.dot(head_out, w_out, preferred_element_type=jnp.float32)  8.93 us
    dot_general x1, matrix products, on_device(): jnp.dot(activations, w_query, preferred_element_type=jnp.float32)  8.66 us
  transfers between devices with their start and end apart: 3, of which 3 were waited for; matrix products, arithmetic and copies ran while one was open for 7% of the time, Pallas kernels for 0%

commit v1 on v0

v1 whole, which is shorter than its diff:
```python
import math

import jax
import jax.numpy as jnp
from jax import lax
from jax.experimental import pallas as pl
from jax.experimental.pallas import tpu as pltpu
from jax.sharding import Mesh, PartitionSpec as P

HD = 128
BLK = 128
CHUNK = 4
CTX = ("z", "y", "core")
F32 = jnp.float32
BF16 = jnp.bfloat16
SCALE2 = math.log2(math.e) / math.sqrt(HD)
NT = (((1,), (1,)), ((), ()))


def kv_kernel(x_ref, wk_ref, wv_ref, o_ref, acc_ref):
    step = pl.program_id(0)

    @pl.when(step == 0)
    def _():
        acc_ref[...] = jnp.zeros_like(acc_ref)

    w = jnp.concatenate([wk_ref[...], wv_ref[...]], axis=1)
    acc_ref[...] += jnp.dot(x_ref[...], w, preferred_element_type=F32)

    @pl.when(step == pl.num_programs(0) - 1)
    def _():
        o_ref[...] = acc_ref[...].astype(BF16)


def kv_project(x, wk, wv):
    rows, depth = x.shape
    tile = 640
    return pl.pallas_call(
        kv_kernel,
        name="kv_project",
        out_shape=jax.ShapeDtypeStruct((rows, 2 * HD), BF16),
        grid=(depth // tile,),
        in_specs=[
            pl.BlockSpec((rows, tile), lambda k: (0, k)),
            pl.BlockSpec((tile, HD), lambda k: (k, 0)),
            pl.BlockSpec((tile, HD), lambda k: (k, 0)),
        ],
        out_specs=pl.BlockSpec((rows, 2 * HD), lambda k: (0, 0)),
        scratch_shapes=[pltpu.VMEM((rows, 2 * HD), F32)],
        cost_estimate=pl.CostEstimate(
            flops=2 * rows * depth * 2 * HD,
            bytes_accessed=2 * depth * (rows + 2 * HD),
            transcendentals=0,
        ),
    )(x, wk, wv)


def block_kernel(
    meta_ref, anc_ref, q_ref, kv_ref, w_ref, o_ref,
    kvbuf, kvown, wbuf, sbuf, mbuf, lbuf, abuf, sems, wsem,
):
    local, own = meta_ref[0], meta_ref[1]
    slots = anc_ref.shape[1]
    heads = q_ref.shape[1] // HD
    wide = CHUNK * BLK

    own_copy = pltpu.make_async_copy(
        kv_ref.at[pl.ds(pl.multiple_of(own * BLK, BLK), BLK)], kvown, sems.at[slots]
    )
    own_copy.start()
    count = jnp.int32(0)
    for l in range(slots):
        entry = anc_ref[local, l]
        count += jnp.where(entry >= 0, 1, 0).astype(jnp.int32)
        src = pl.multiple_of(jnp.maximum(entry, 0) * BLK, BLK)
        pltpu.make_async_copy(
            kv_ref.at[pl.ds(src, BLK)], kvbuf.at[pl.ds(l * BLK, BLK)], sems.at[l]
        ).start()
    w_copy = pltpu.make_async_copy(w_ref, wbuf, wsem.at[0])
    w_copy.start()

    q_all = q_ref[...]
    q = jnp.concatenate([q_all[:, h * HD:(h + 1) * HD] for h in range(heads)], axis=0)
    own_copy.wait()
    s_own = lax.dot_general(q, kvown[:, :HD], NT, preferred_element_type=F32)
    row = lax.broadcasted_iota(jnp.int32, s_own.shape, 0) % BLK
    col = lax.broadcasted_iota(jnp.int32, s_own.shape, 1)
    s_own = jnp.where(col <= row, s_own, -jnp.inf)
    mbuf[...] = s_own
    for l in range(slots):
        pltpu.make_async_copy(
            kv_ref.at[pl.ds(0, BLK)], kvbuf.at[pl.ds(l * BLK, BLK)], sems.at[l]
        ).wait()
    chunks = (count + CHUNK - 1) // CHUNK

    def score(c, _):
        base = pl.multiple_of(c * wide, wide)
        s = lax.dot_general(q, kvbuf[pl.ds(base, wide), :HD], NT, preferred_element_type=F32)
        m = mbuf[...]
        for j in range(CHUNK):
            piece = s[:, j * BLK:(j + 1) * BLK]
            piece = jnp.where(c * CHUNK + j < count, piece, -jnp.inf)
            sbuf[c, :, j * BLK:(j + 1) * BLK] = piece
            m = jnp.maximum(m, piece)
        mbuf[...] = m
        return 0

    lax.fori_loop(0, chunks, score, 0)
    m = jnp.max(mbuf[...], axis=1, keepdims=True)
    p = jnp.exp2((s_own - m) * SCALE2)
    lbuf[...] = p
    abuf[...] = jnp.dot(p.astype(BF16), kvown[:, HD:], preferred_element_type=F32)

    def weigh(c, _):
        base = pl.multiple_of(c * wide, wide)
        w = jnp.exp2((sbuf[c] - m) * SCALE2)
        total = lbuf[...]
        for j in range(CHUNK):
            total += w[:, j * BLK:(j + 1) * BLK]
        lbuf[...] = total
        abuf[...] += jnp.dot(
            w.astype(BF16), kvbuf[pl.ds(base, wide), HD:], preferred_element_type=F32
        )
        return 0

    lax.fori_loop(0, chunks, weigh, 0)
    total = jnp.sum(lbuf[...], axis=1, keepdims=True)
    out = (abuf[...] / total).astype(BF16)
    head_out = jnp.concatenate([out[h * BLK:(h + 1) * BLK] for h in range(heads)], axis=1)
    w_copy.wait()
    cols = w_ref.shape[1]
    step = 1280
    for c in range(0, cols, step):
        o_ref[:, c:c + step] = jnp.dot(
            head_out, wbuf[:, c:c + step], preferred_element_type=F32
        ).astype(BF16)


def block_term(meta, anc, q, kv, w_out):
    slots = anc.shape[1]
    width = q.shape[1]
    rows = BLK * (width // HD)
    cols = w_out.shape[1]
    keys = (slots + 1) * BLK
    return pl.pallas_call(
        block_kernel,
        name="block_term",
        out_shape=jax.ShapeDtypeStruct((BLK, cols), BF16),
        grid_spec=pltpu.PrefetchScalarGridSpec(
            num_scalar_prefetch=2,
            grid=(1,),
            in_specs=[
                pl.BlockSpec((BLK, width), lambda i, meta, anc: (meta[0], 0)),
                pl.BlockSpec(memory_space=pl.ANY),
                pl.BlockSpec(memory_space=pl.ANY),
            ],
            out_specs=pl.BlockSpec((BLK, cols), lambda i, meta, anc: (0, 0)),
            scratch_shapes=[
                pltpu.VMEM((slots * BLK, 2 * HD), BF16),
                pltpu.VMEM((BLK, 2 * HD), BF16),
                pltpu.VMEM(w_out.shape, BF16),
                pltpu.VMEM((slots // CHUNK, rows, CHUNK * BLK), F32),
                pltpu.VMEM((rows, BLK), F32),
                pltpu.VMEM((rows, BLK), F32),
                pltpu.VMEM((rows, HD), F32),
                pltpu.SemaphoreType.DMA((slots + 1,)),
                pltpu.SemaphoreType.DMA((1,)),
            ],
        ),
        compiler_params=pltpu.CompilerParams(vmem_limit_bytes=40 << 20),
        cost_estimate=pl.CostEstimate(
            flops=4 * rows * keys * HD + 2 * BLK * width * cols,
            bytes_accessed=2 * (keys * 2 * HD + w_out.size + BLK * (width + cols)),
            transcendentals=rows * keys,
        ),
    )(meta, anc, q, kv, w_out)


def norm_kernel(res_ref, own_ref, u1_ref, u2_ref, v1_ref, v2_ref, gain_ref, keep_ref, o_ref):
    half = u1_ref.shape[1]
    total = []
    for lo, u, v in ((0, u1_ref, v1_ref), (half, u2_ref, v2_ref)):
        total.append(
            res_ref[:, lo:lo + half].astype(F32)
            + own_ref[:, lo:lo + half].astype(F32)
            + u[...].astype(F32)
            + v[...].astype(F32)
        )
    square = sum(jnp.sum(x * x, axis=1, keepdims=True) for x in total)
    factor = lax.rsqrt(square * (1.0 / (2 * half)) + 1e-06) * keep_ref[0].astype(F32)
    for lo, x in zip((0, half), total):
        o_ref[:, lo:lo + half] = (x * factor * gain_ref[:, lo:lo + half]).astype(BF16)


def final_norm(residual, own, u, v, gain, keep):
    rows, cols = residual.shape
    vm = pl.BlockSpec(memory_space=pltpu.VMEM)
    return pl.pallas_call(
        norm_kernel,
        name="final_norm",
        out_shape=jax.ShapeDtypeStruct((rows, cols), BF16),
        in_specs=[vm] * 7 + [pl.BlockSpec(memory_space=pltpu.SMEM)],
        out_specs=vm,
        compiler_params=pltpu.CompilerParams(vmem_limit_bytes=30 << 20),
    )(residual, own, *u, *v, gain[None, :], keep)


def ring(n, s):
    return [(i, (i + s) % n) for i in range(n)]


def on_device(activations, residual, w_query, w_key, w_value, w_out, gain, ancestors, kept):
    blk_dev = ancestors.shape[0]
    kv_own = kv_project(activations, w_key, w_value)
    kv = lax.all_gather(kv_own, CTX, axis=0, tiled=True)
    queries = jnp.dot(activations, w_query, preferred_element_type=F32).astype(BF16)

    t = lax.axis_index("tp").astype(jnp.int32)
    position = lax.axis_index(CTX).astype(jnp.int32)

    def term(s):
        local = (t + s) % 4
        meta = jnp.stack([local, position * blk_dev + local])
        return block_term(meta, ancestors, queries, kv, w_out)

    def send(x, s):
        return lax.ppermute(x, "tp", ring(4, s))

    half = w_out.shape[1] // 2
    p2 = term(2)
    a = send(p2[:, :half], 1)
    b = send(p2[:, half:], 3)
    p1 = term(1)
    u2 = send(p1[:, half:], 1)
    p3 = term(3)
    v1 = send(p3[:, :half], 3)
    p0 = term(0)
    u1 = send(p1[:, :half] + a, 1)
    v2 = send(p3[:, half:] + b, 3)
    keep = lax.dynamic_slice_in_dim(kept, t, 1, 0)
    return final_norm(residual, p0, (u1, u2), (v1, v2), gain, keep)


def solution(mesh):
    fine = Mesh(mesh.devices.reshape(2, 4, 2, 2, 4), ("dp", "z", "y", "core", "tp"))
    ctx = ("dp",) + CTX
    in_specs = (
        P(ctx, None),
        P(ctx + ("tp",), None),
        P(None, "tp"),
        P(None, "tp"),
        P(None, "tp"),
        P("tp", None),
        P(),
        P(ctx, None),
        P(ctx),
    )
    out_specs = P(ctx + ("tp",), None)
    return jax.shard_map(
        on_device, mesh=fine, in_specs=in_specs, out_specs=out_specs, check_vma=False
    )
```

time: 219 us -> 136 us (0.62)
  waiting for transfers between devices: 112 us -> 49.6 us
  matrix products: 48.3 us -> 8.67 us
  Pallas kernels: 0 us -> 36.8 us
  local copies, waits for them, and re-layouts: 28.5 us -> 15.9 us
  other arithmetic: 15 us -> 2.68 us
  starting transfers between devices: 0.09 us -> 7.33 us
    reduce_scatter x1 -> x0, waiting for transfers between devices: 55 us -> none  [on_device(): lax.psum_scatter(jnp.dot(head_out, w_out, preferred_element_type=jnp.floa...]
    dot_general x12 -> x1, matrix products: 48.3 us -> 8.67 us  [on_device(): jnp.dot(activations, w_query, preferred_element_type=F32).astype(BF16)]
    pallas_call x0 -> x6, Pallas kernels: none -> 36.8 us  [the longest x4 26.2 us: block_term(): pl.pallas_call(block_kernel, name='block_term', out_shape=jax.ShapeDtypeS...]
    all_gather x2 -> x1, waiting for transfers between devices: 57.3 us -> 30.9 us  [on_device(): kv = lax.all_gather(kv_own, CTX, axis=0, tiled=True)]
    ppermute x0 -> x6, waiting for transfers between devices: none -> 18.7 us  [send(): return lax.ppermute(x, 'tp', ring(4, s))]
    gather x8 -> x0, local copies, waits for them, and re-layouts: 17.9 us -> none  [the longest x4 8.97 us: one_block(): chosen_keys = key_blocks[safe_ids].reshape(-1, kv_local, HD)]
    unnamed x14 -> x20, local copies, waits for them, and re-layouts: 1.95 us -> 15.2 us
    ppermute x0 -> x6, starting transfers between devices: none -> 7.33 us  [send(): return lax.ppermute(x, 'tp', ring(4, s))]
  transfers between devices with their start and end apart: 3 -> 7, of which waited for: 3 -> 3; matrix products, arithmetic and copies ran while one was open for 7% -> 9% of each run, Pallas kernels for 0% -> 14%
where the time goes in v1:
time: 136 us; the launch traced here: 134 us
  waiting for transfers between devices  49.6 us (36%)
  Pallas kernels  36.8 us (27%)
  local copies, waits for them, and re-layouts  15.9 us (12%)
  between operations  13.5 us (10%)
  matrix products  8.67 us (6%)
  starting transfers between devices  7.33 us (5%)
  other arithmetic  2.68 us (2%)
    all_gather x1, waiting for transfers between devices, on_device(): kv = lax.all_gather(kv_own, CTX, axis=0, tiled=True)  30.9 us
    pallas_call x4, Pallas kernels, block_term(): pl.pallas_call(block_kernel, name='block_term', out_shape=jax.ShapeDtypeS...  26.2 us
    ppermute x6, waiting for transfers between devices, send(): return lax.ppermute(x, 'tp', ring(4, s))  18.7 us
    unnamed x20, local copies, waits for them, and re-layouts  15.2 us
    dot_general x1, matrix products, on_device(): jnp.dot(activations, w_query, preferred_element_type=F32).astype(BF16)  8.67 us
    pallas_call x1, Pallas kernels, kv_project(): pl.pallas_call(kv_kernel, name='kv_project', out_shape=jax.ShapeDtypeStru...  7.63 us
    ppermute x6, starting transfers between devices, send(): return lax.ppermute(x, 'tp', ring(4, s))  7.33 us
    pallas_call x1, Pallas kernels, final_norm(): pl.pallas_call(norm_kernel, name='final_norm', out_shape=jax.ShapeDtypeSt...  2.95 us
  transfers between devices with their start and end apart: 7, of which 3 were waited for; matrix products, arithmetic and copies ran while one was open for 9% of the time, Pallas kernels for 14%

profile of v1, /device:TPU:24, one launch (start us, length us, event | category | flops | bytes accessed | tf_op | source)
XLA Modules:
  0.0 134.5 jit_solution(163295982704409525)
XLA Ops:
  6.5 7.6 %kv_project.1 = bf16[512,256]{1,0:T(8,128)(2,1)} custom-call(bf16[512,5120]{1,0:T(8,128)(2,1)} %x_ref.1, bf16[5120,128]{1,0:T(8,128)(2,1)} %wk_ref.1, bf16[5120,128]{1,0:T(8,128)(2,1)} %wv_ref.1), custom_call_target="tpu_custom_call" | custom-call | flops 1342177280 | bytes 7864320 | tf_op jit(solution)/shard_map/kv_project/pallas_call | solution.py:38
  14.2 0.0 all-gather.2.cloned.1.call-update
  14.2 0.1 pad_add_fusion.2.meta_ref
  14.3 8.7 %convolution_convert_fusion.q_ref = bf16[512,640]{1,0:T(8,128)(2,1)S(1)} fusion(bf16[512,5120]{1,0:T(8,128)(2,1)} %x_ref.1, bf16[5120,640]{1,0:T(8,128)(2,1)} %param.11), kind=kOutput, calls=%fused_computation | convolution fusion | flops 3355770880 | bytes 12451840 | tf_op jit(solution)/shard_map/dot_general | solution.py:216
  23.0 30.9 %all-gather.2.cloned.1.call-done.kv_ref = bf16[8192,256]{1,0:T(8,128)(2,1)} async-done(((bf16[512,256]{1,0:T(8,128)(2,1)}), bf16[8192,256]{1,0:T(8,128)(2,1)}) %all-gather.2.cloned.1.call-update) | async-done | bytes 4194320 | tf_op jit(solution)/shard_map/all_gather | solution.py:215
  53.8 2.9 %copy-done = bf16[640,5120]{1,0:T(8,128)(2,1)S(1)} copy-done((bf16[640,5120]{1,0:T(8,128)(2,1)S(1)}, bf16[640,5120]{1,0:T(8,128)(2,1)}, u32[]{:S(2)}) %copy-start) | copy-done | bytes 6553624
  56.7 2.2 %copy-done.3 = bf16[8192,256]{1,0:T(8,128)(2,1)S(1)} copy-done((bf16[8192,256]{1,0:T(8,128)(2,1)S(1)}, bf16[8192,256]{1,0:T(8,128)(2,1)}, u32[]{:S(2)}) %copy-start.3) | copy-done | bytes 4194328
  58.9 6.7 %block_term.6 = bf16[128,5120]{1,0:T(8,128)(2,1)S(1)} custom-call(s32[2]{0:T(128)S(1)} %pad_add_fusion.2.meta_ref, s32[4,16]{1,0:T(4,128)S(1)} %copy-done.7, bf16[512,640]{1,0:T(8,128)(2,1)S(1)} %convolution_convert_fusion.q_ref, bf16[8192,256]{1,0:T(8,128)(2,1)S(1)} %copy-done.3, bf16[640,5120]{1,0:T(8,128)(2,1)S(1)} %copy-done), custom_call_target="tpu_custom_call" | custom-call | flops 1551892480 | bytes 9142272 | tf_op jit(solution)/shard_map/block_term/pallas_call | solution.py:145
  65.6 0.1 fusion
  65.7 2.8 %collective-permute-start.4 = (bf16[128,2560]{1,0:T(8,128)(2,1)S(1)}, bf16[128,2560]{1,0:T(8,128)(2,1)S(1)}, u32[]{:S(2)}, u32[]{:S(2)}) collective-permute-start(bf16[128,2560]{1,0:T(8,128)(2,1)S(1)} %get-tuple-element.7), channel_id=1, source_target_pairs={{0,3},{1,0},{2,1},{3,2},{4,7},{5,4},{6,5},{7,6},{8,11},{9,8},{10,9... | collective-permute-start | bytes 1966088 | tf_op jit(solution)/shard_map/ppermute | solution.py:227
  68.5 0.1 pad_add_fusion.1.meta_ref
  68.5 0.1 pad_add_fusion.3.meta_ref
  68.6 0.0 copy-start.1
  68.6 2.9 %copy-done.1 = bf16[640,5120]{1,0:T(8,128)(2,1)S(1)} copy-done((bf16[640,5120]{1,0:T(8,128)(2,1)S(1)}, bf16[640,5120]{1,0:T(8,128)(2,1)}, u32[]{:S(2)}) %copy-start.1) | copy-done | bytes 6553624
  71.5 2.2 %copy-done.4 = bf16[8192,256]{1,0:T(8,128)(2,1)S(1)} copy-done((bf16[8192,256]{1,0:T(8,128)(2,1)S(1)}, bf16[8192,256]{1,0:T(8,128)(2,1)}, u32[]{:S(2)}) %copy-start.4) | copy-done | bytes 4194328
  73.7 6.7 %block_term.7 = bf16[128,5120]{1,0:T(8,128)(2,1)S(1)} custom-call(s32[2]{0:T(128)S(1)} %pad_add_fusion.3.meta_ref, s32[4,16]{1,0:T(4,128)S(1)} %copy-done.7, bf16[512,640]{1,0:T(8,128)(2,1)S(1)} %convolution_convert_fusion.q_ref, bf16[8192,256]{1,0:T(8,128)(2,1)S(1)} %copy-done.4, bf16[640,5120]{1,0:T(8,128)(2,1)S(1)} %copy-done.1), custom_call_target="tpu_custom_call" | custom-call | flops 1551892480 | bytes 9142272 | tf_op jit(solution)/shard_map/block_term/pallas_call | solution.py:145
  80.4 6.7 %block_term.5 = bf16[128,5120]{1,0:T(8,128)(2,1)S(1)} custom-call(s32[2]{0:T(128)S(1)} %pad_add_fusion.1.meta_ref, s32[4,16]{1,0:T(4,128)S(1)} %copy-done.7, bf16[512,640]{1,0:T(8,128)(2,1)S(1)} %convolution_convert_fusion.q_ref, bf16[8192,256]{1,0:T(8,128)(2,1)S(1)} %copy-done.4, bf16[640,5120]{1,0:T(8,128)(2,1)S(1)} %copy-done.1), custom_call_target="tpu_custom_call" | custom-call | flops 1551892480 | bytes 9142272 | tf_op jit(solution)/shard_map/block_term/pallas_call | solution.py:145
  87.1 0.0 collective-permute-done.4
  87.1 1.2 slice_add_fusion
  88.3 2.5 %collective-permute-start.5 = (bf16[128,2560]{1,0:T(8,128)(2,1)}, bf16[128,2560]{1,0:T(8,128)(2,1)S(1)}, u32[]{:S(2)}, u32[]{:S(2)}) collective-permute-start(bf16[128,2560]{1,0:T(8,128)(2,1)} %get-tuple-element.5), channel_id=1, source_target_pairs={{0,3},{1,0},{2,1},{3,2},{4,7},{5,4},{6,5},{7,6},{8,11},{9,8},{10,9... | collective-permute-start | bytes 1966088 | tf_op jit(solution)/shard_map/ppermute | solution.py:227
  90.9 0.0 collective-permute-start.3
  90.9 1.2 fusion.1
  92.1 2.0 %collective-permute-start.2 = (bf16[128,2560]{1,0:T(8,128)(2,1)}, bf16[128,2560]{1,0:T(8,128)(2,1)S(1)}, u32[]{:S(2)}, u32[]{:S(2)}) collective-permute-start(bf16[128,2560]{1,0:T(8,128)(2,1)} %get-tuple-element.9), channel_id=1, source_target_pairs={{0,1},{1,2},{2,3},{3,0},{4,5},{5,6},{6,7},{7,4},{8,9},{9,10},{10,1... | collective-permute-start | bytes 1966088 | tf_op jit(solution)/shard_map/ppermute | solution.py:227
  94.1 0.0 collective-permute-start.1
  94.1 0.7 dynamic_slice.3.keep_ref
  94.8 0.1 pad_add_fusion.meta_ref
  94.8 2.9 %copy-done.2 = bf16[640,5120]{1,0:T(8,128)(2,1)S(1)} copy-done((bf16[640,5120]{1,0:T(8,128)(2,1)S(1)}, bf16[640,5120]{1,0:T(8,128)(2,1)}, u32[]{:S(2)}) %copy-start.2) | copy-done | bytes 6553624
  97.7 2.2 %copy-done.5 = bf16[8192,256]{1,0:T(8,128)(2,1)S(1)} copy-done((bf16[8192,256]{1,0:T(8,128)(2,1)S(1)}, bf16[8192,256]{1,0:T(8,128)(2,1)}, u32[]{:S(2)}) %copy-start.5) | copy-done | bytes 4194328
  99.9 6.0 %block_term.4.own_ref = bf16[128,5120]{1,0:T(8,128)(2,1)S(1)} custom-call(s32[2]{0:T(128)S(1)} %pad_add_fusion.meta_ref, s32[4,16]{1,0:T(4,128)S(1)} %copy-done.7, bf16[512,640]{1,0:T(8,128)(2,1)S(1)} %convolution_convert_fusion.q_ref, bf16[8192,256]{1,0:T(8,128)(2,1)S(1)} %copy-done.5, bf16[640,5120]{1,0:T(8,128)(2,1)S(1)} %copy-done.2), custom_call_target="tpu_custom_call" | custom-call | flops 1551892480 | bytes 9142272 | tf_op jit(solution)/shard_map/block_term/pallas_call | solution.py:145
  105.9 13.6 %collective-permute-done.3.v1_ref = bf16[128,2560]{1,0:T(8,128)(2,1)S(1)} collective-permute-done((bf16[128,2560]{1,0:T(8,128)(2,1)}, bf16[128,2560]{1,0:T(8,128)(2,1)S(1)}, u32[]{:S(2)}, u32[]{:S(2)}) %collective-permute-start.3) | collective-permute-done | bytes 655392 | tf_op jit(solution)/shard_map/ppermute | solution.py:227
  119.5 5.1 %collective-permute-done.1.u1_ref = bf16[128,2560]{1,0:T(8,128)(2,1)S(1)} collective-permute-done((bf16[128,2560]{1,0:T(8,128)(2,1)}, bf16[128,2560]{1,0:T(8,128)(2,1)S(1)}, u32[]{:S(2)}, u32[]{:S(2)}) %collective-permute-start.1) | collective-permute-done | bytes 655392 | tf_op jit(solution)/shard_map/ppermute | solution.py:227
  124.7 3.0 %final_norm.1 = bf16[128,5120]{1,0:T(8,128)(2,1)} custom-call(bf16[128,5120]{1,0:T(8,128)(2,1)S(1)} %copy-done.6, bf16[128,5120]{1,0:T(8,128)(2,1)S(1)} %block_term.4.own_ref, bf16[128,2560]{1,0:T(8,128)(2,1)S(1)} %collective-permute-done.1.u1_ref, bf16[128,2560]{1,0:T(8,128)(2,1)S(1)} %collective-permute-done.2.u2_ref, ...), custom_call_target="tpu_custom_call" | custom-call | tf_op jit(solution)/shard_map/final_norm/pallas_call | solution.py:198
  (18 shorter events, 0.0 us)
Async XLA Ops:
  6.5 47.3 %all-gather.2.cloned.1.call-start = ((), (), s32[]{:S(2)}) async-start(), calls=%async_computation | async-start | bytes 4456448 | tf_op jit(solution)/shard_map/all_gather | solution.py:215
  14.3 39.5 %copy-start.7 = (s32[4,16]{1,0:T(4,128)S(1)}, s32[4,16]{1,0:T(4,128)}, u32[]{:S(2)}) copy-start(s32[4,16]{1,0:T(4,128)} %anc_ref.7) | copy-start | bytes 772
  53.8 2.9 %copy-start = (bf16[640,5120]{1,0:T(8,128)(2,1)S(1)}, bf16[640,5120]{1,0:T(8,128)(2,1)}, u32[]{:S(2)}) copy-start(bf16[640,5120]{1,0:T(8,128)(2,1)} %w_ref.7) | copy-start | bytes 19660804
  56.7 2.2 %copy-start.3 = (bf16[8192,256]{1,0:T(8,128)(2,1)S(1)}, bf16[8192,256]{1,0:T(8,128)(2,1)}, u32[]{:S(2)}) copy-start(bf16[8192,256]{1,0:T(8,128)(2,1)} %all-gather.2.cloned.1.call-done.kv_ref) | copy-start | bytes 12582916
  65.7 21.4 %collective-permute-start.4 = (bf16[128,2560]{1,0:T(8,128)(2,1)S(1)}, bf16[128,2560]{1,0:T(8,128)(2,1)S(1)}, u32[]{:S(2)}, u32[]{:S(2)}) collective-permute-start(bf16[128,2560]{1,0:T(8,128)(2,1)S(1)} %get-tuple-element.7), channel_id=1, source_target_pairs={{0,3},{1,0},{2,1},{3,2},{4,7},{5,4},{6,5},{7,6},{8,11},{9,8},{10,9... | collective-permute-start | bytes 1966088 | tf_op jit(solution)/shard_map/ppermute | solution.py:227
  68.6 22.3 %collective-permute-start = (bf16[128,2560]{1,0:T(8,128)(2,1)S(1)}, bf16[128,2560]{1,0:T(8,128)(2,1)S(1)}, u32[]{:S(2)}, u32[]{:S(2)}) collective-permute-start(bf16[128,2560]{1,0:T(8,128)(2,1)S(1)} %get-tuple-element.8), channel_id=1, source_target_pairs={{0,1},{1,2},{2,3},{3,0},{4,5},{5,6},{6,7},{7,4},{8,9},{9,10},{10,1... | collective-permute-start | bytes 1966088 | tf_op jit(solution)/shard_map/ppermute | solution.py:227
  68.6 2.9 %copy-start.1 = (bf16[640,5120]{1,0:T(8,128)(2,1)S(1)}, bf16[640,5120]{1,0:T(8,128)(2,1)}, u32[]{:S(2)}) copy-start(bf16[640,5120]{1,0:T(8,128)(2,1)} %w_ref.7) | copy-start | bytes 19660804
  71.5 2.2 %copy-start.4 = (bf16[8192,256]{1,0:T(8,128)(2,1)S(1)}, bf16[8192,256]{1,0:T(8,128)(2,1)}, u32[]{:S(2)}) copy-start(bf16[8192,256]{1,0:T(8,128)(2,1)} %all-gather.2.cloned.1.call-done.kv_ref) | copy-start | bytes 12582916
  88.3 17.6 %collective-permute-start.5 = (bf16[128,2560]{1,0:T(8,128)(2,1)}, bf16[128,2560]{1,0:T(8,128)(2,1)S(1)}, u32[]{:S(2)}, u32[]{:S(2)}) collective-permute-start(bf16[128,2560]{1,0:T(8,128)(2,1)} %get-tuple-element.5), channel_id=1, source_target_pairs={{0,3},{1,0},{2,1},{3,2},{4,7},{5,4},{6,5},{7,6},{8,11},{9,8},{10,9... | collective-permute-start | bytes 1966088 | tf_op jit(solution)/shard_map/ppermute | solution.py:227
  90.9 3.2 %copy-start.9 = (s32[4]{0:T(128)S(1)}, s32[4]{0:T(128)}, u32[]{:S(2)}) copy-start(s32[4]{0:T(128)} %param.17) | copy-start | bytes 52
  90.9 28.7 %collective-permute-start.3 = (bf16[128,2560]{1,0:T(8,128)(2,1)}, bf16[128,2560]{1,0:T(8,128)(2,1)S(1)}, u32[]{:S(2)}, u32[]{:S(2)}) collective-permute-start(bf16[128,2560]{1,0:T(8,128)(2,1)} %get-tuple-element.6), channel_id=1, source_target_pairs={{0,3},{1,0},{2,1},{3,2},{4,7},{5,4},{6,5},{7,6},{8,11},{9,8},{10,9... | collective-permute-start | bytes 1966088 | tf_op jit(solution)/shard_map/ppermute | solution.py:227
  92.1 27.5 %collective-permute-start.2 = (bf16[128,2560]{1,0:T(8,128)(2,1)}, bf16[128,2560]{1,0:T(8,128)(2,1)S(1)}, u32[]{:S(2)}, u32[]{:S(2)}) collective-permute-start(bf16[128,2560]{1,0:T(8,128)(2,1)} %get-tuple-element.9), channel_id=1, source_target_pairs={{0,1},{1,2},{2,3},{3,0},{4,5},{5,6},{6,7},{7,4},{8,9},{9,10},{10,1... | collective-permute-start | bytes 1966088 | tf_op jit(solution)/shard_map/ppermute | solution.py:227
  94.1 30.6 %collective-permute-start.1 = (bf16[128,2560]{1,0:T(8,128)(2,1)}, bf16[128,2560]{1,0:T(8,128)(2,1)S(1)}, u32[]{:S(2)}, u32[]{:S(2)}) collective-permute-start(bf16[128,2560]{1,0:T(8,128)(2,1)} %get-tuple-element.10), channel_id=1, source_target_pairs={{0,1},{1,2},{2,3},{3,0},{4,5},{5,6},{6,7},{7,4},{8,9},{9,10},{10,1... | collective-permute-start | bytes 1966088 | tf_op jit(solution)/shard_map/ppermute | solution.py:227
  94.8 2.9 %copy-start.2 = (bf16[640,5120]{1,0:T(8,128)(2,1)S(1)}, bf16[640,5120]{1,0:T(8,128)(2,1)}, u32[]{:S(2)}) copy-start(bf16[640,5120]{1,0:T(8,128)(2,1)} %w_ref.7) | copy-start | bytes 19660804
  97.7 2.2 %copy-start.5 = (bf16[8192,256]{1,0:T(8,128)(2,1)S(1)}, bf16[8192,256]{1,0:T(8,128)(2,1)}, u32[]{:S(2)}) copy-start(bf16[8192,256]{1,0:T(8,128)(2,1)} %all-gather.2.cloned.1.call-done.kv_ref) | copy-start | bytes 12582916
  99.9 24.8 %copy-start.6 = (bf16[128,5120]{1,0:T(8,128)(2,1)S(1)}, bf16[128,5120]{1,0:T(8,128)(2,1)}, u32[]{:S(2)}) copy-start(bf16[128,5120]{1,0:T(8,128)(2,1)} %res_ref.1) | copy-start | bytes 3932164
  99.9 24.8 %copy-start.8 = (f32[5120]{0:T(1024)S(1)}, f32[5120]{0:T(1024)}, u32[]{:S(2)}) copy-start(f32[5120]{0:T(1024)} %param.15) | copy-start | bytes 61444
Sparse Core Ops, SparseCore 0:
  14.3 39.4 all-gather.1

commit v2 on v1

--- a/solution.py
+++ b/solution.py
@@ -17,36 +17,44 @@
 NT = (((1,), (1,)), ((), ()))
 
 
-def kv_kernel(x_ref, wk_ref, wv_ref, o_ref, acc_ref):
-    step = pl.program_id(0)
-
-    @pl.when(step == 0)
-    def _():
-        acc_ref[...] = jnp.zeros_like(acc_ref)
-
-    w = jnp.concatenate([wk_ref[...], wv_ref[...]], axis=1)
-    acc_ref[...] += jnp.dot(x_ref[...], w, preferred_element_type=F32)
-
-    @pl.when(step == pl.num_programs(0) - 1)
-    def _():
-        o_ref[...] = acc_ref[...].astype(BF16)
+def kv_kernel(x_ref, wk_ref, wv_ref, o_ref, xbuf, wbuf, sems):
+    parts, _, tile = xbuf.shape
+    copies = []
+    for k in range(parts):
+        cut = pl.ds(k * tile, tile)
+        group = [
+            pltpu.make_async_copy(x_ref.at[:, cut], xbuf.at[k], sems.at[0, k]),
+            pltpu.make_async_copy(wk_ref.at[cut], wbuf.at[k, :, pl.ds(0, HD)], sems.at[1, k]),
+            pltpu.make_async_copy(wv_ref.at[cut], wbuf.at[k, :, pl.ds(HD, HD)], sems.at[2, k]),
+        ]
+        for copy in group:
+            copy.start()
+        copies.append(group)
+    total = None
+    for k in range(parts):
+        for copy in copies[k]:
+            copy.wait()
+        part = jnp.dot(xbuf[k], wbuf[k], preferred_element_type=F32)
+        total = part if total is None else total + part
+    o_ref[...] = total.astype(BF16)
 
 
 def kv_project(x, wk, wv):
     rows, depth = x.shape
-    tile = 640
+    parts = 10
+    tile = depth // parts
+    hbm = pl.BlockSpec(memory_space=pltpu.HBM)
     return pl.pallas_call(
         kv_kernel,
         name="kv_project",
         out_shape=jax.ShapeDtypeStruct((rows, 2 * HD), BF16),
-        grid=(depth // tile,),
-        in_specs=[
-            pl.BlockSpec((rows, tile), lambda k: (0, k)),
-            pl.BlockSpec((tile, HD), lambda k: (k, 0)),
-            pl.BlockSpec((tile, HD), lambda k: (k, 0)),
+        in_specs=[hbm] * 3,
+        out_specs=pl.BlockSpec(memory_space=pltpu.VMEM),
+        scratch_shapes=[
+            pltpu.VMEM((parts, rows, tile), BF16),
+            pltpu.VMEM((parts, tile, 2 * HD), BF16),
+            pltpu.SemaphoreType.DMA((3, parts)),
         ],
-        out_specs=pl.BlockSpec((rows, 2 * HD), lambda k: (0, 0)),
-        scratch_shapes=[pltpu.VMEM((rows, 2 * HD), F32)],
         cost_estimate=pl.CostEstimate(
             flops=2 * rows * depth * 2 * HD,
             bytes_accessed=2 * depth * (rows + 2 * HD),
@@ -56,7 +64,7 @@
 
 
 def block_kernel(
-    meta_ref, anc_ref, q_ref, kv_ref, w_ref, o_ref,
+    meta_ref, anc_ref, q_ref, kv_ref, w_ref, lo_ref, hi_ref,
     kvbuf, kvown, wbuf, sbuf, mbuf, lbuf, abuf, sems, wsem,
 ):
     local, own = meta_ref[0], meta_ref[1]
@@ -128,12 +136,13 @@
     out = (abuf[...] / total).astype(BF16)
     head_out = jnp.concatenate([out[h * BLK:(h + 1) * BLK] for h in range(heads)], axis=1)
     w_copy.wait()
-    cols = w_ref.shape[1]
-    step = 1280
-    for c in range(0, cols, step):
-        o_ref[:, c:c + step] = jnp.dot(
-            head_out, wbuf[:, c:c + step], preferred_element_type=F32
-        ).astype(BF16)
+    half = lo_ref.shape[1]
+    step = half // 2
+    for o_ref, start in ((lo_ref, 0), (hi_ref, half)):
+        for c in range(0, half, step):
+            o_ref[:, c:c + step] = jnp.dot(
+                head_out, wbuf[:, start + c:start + c + step], preferred_element_type=F32
+            ).astype(BF16)
 
 
 def block_term(meta, anc, q, kv, w_out):
@@ -145,16 +154,16 @@
     return pl.pallas_call(
         block_kernel,
         name="block_term",
-        out_shape=jax.ShapeDtypeStruct((BLK, cols), BF16),
+        out_shape=[jax.ShapeDtypeStruct((BLK, cols // 2), BF16)] * 2,
         grid_spec=pltpu.PrefetchScalarGridSpec(
             num_scalar_prefetch=2,
             grid=(1,),
             in_specs=[
                 pl.BlockSpec((BLK, width), lambda i, meta, anc: (meta[0], 0)),
-                pl.BlockSpec(memory_space=pl.ANY),
-                pl.BlockSpec(memory_space=pl.ANY),
+                pl.BlockSpec(memory_space=pltpu.HBM),
+                pl.BlockSpec(memory_space=pltpu.HBM),
             ],
-            out_specs=pl.BlockSpec((BLK, cols), lambda i, meta, anc: (0, 0)),
+            out_specs=[pl.BlockSpec((BLK, cols // 2), lambda i, meta, anc: (0, 0))] * 2,
             scratch_shapes=[
                 pltpu.VMEM((slots * BLK, 2 * HD), BF16),
                 pltpu.VMEM((BLK, 2 * HD), BF16),
@@ -167,22 +176,17 @@
                 pltpu.SemaphoreType.DMA((1,)),
             ],
         ),
-        compiler_params=pltpu.CompilerParams(vmem_limit_bytes=40 << 20),
-        cost_estimate=pl.CostEstimate(
-            flops=4 * rows * keys * HD + 2 * BLK * width * cols,
-            bytes_accessed=2 * (keys * 2 * HD + w_out.size + BLK * (width + cols)),
-            transcendentals=rows * keys,
-        ),
+        cost_estimate=pl.CostEstimate(flops=1 << 20, bytes_accessed=1 << 20, transcendentals=0),
     )(meta, anc, q, kv, w_out)
 
 
-def norm_kernel(res_ref, own_ref, u1_ref, u2_ref, v1_ref, v2_ref, gain_ref, keep_ref, o_ref):
+def norm_kernel(res_ref, o1_ref, o2_ref, u1_ref, u2_ref, v1_ref, v2_ref, gain_ref, keep_ref, o_ref):
     half = u1_ref.shape[1]
     total = []
-    for lo, u, v in ((0, u1_ref, v1_ref), (half, u2_ref, v2_ref)):
+    for lo, o, u, v in ((0, o1_ref, u1_ref, v1_ref), (half, o2_ref, u2_ref, v2_ref)):
         total.append(
             res_ref[:, lo:lo + half].astype(F32)
-            + own_ref[:, lo:lo + half].astype(F32)
+            + o[...].astype(F32)
             + u[...].astype(F32)
             + v[...].astype(F32)
         )
@@ -199,10 +203,10 @@
         norm_kernel,
         name="final_norm",
         out_shape=jax.ShapeDtypeStruct((rows, cols), BF16),
-        in_specs=[vm] * 7 + [pl.BlockSpec(memory_space=pltpu.SMEM)],
+        in_specs=[vm] * 8 + [pl.BlockSpec(memory_space=pltpu.SMEM)],
         out_specs=vm,
         compiler_params=pltpu.CompilerParams(vmem_limit_bytes=30 << 20),
-    )(residual, own, *u, *v, gain[None, :], keep)
+    )(residual, *own, *u, *v, gain[None, :], keep)
 
 
 def ring(n, s):
@@ -226,19 +230,18 @@
     def send(x, s):
         return lax.ppermute(x, "tp", ring(4, s))
 
-    half = w_out.shape[1] // 2
-    p2 = term(2)
-    a = send(p2[:, :half], 1)
-    b = send(p2[:, half:], 3)
-    p1 = term(1)
-    u2 = send(p1[:, half:], 1)
-    p3 = term(3)
-    v1 = send(p3[:, :half], 3)
-    p0 = term(0)
-    u1 = send(p1[:, :half] + a, 1)
-    v2 = send(p3[:, half:] + b, 3)
+    lo2, hi2 = term(2)
+    a = send(lo2, 1)
+    b = send(hi2, 3)
+    lo1, hi1 = term(1)
+    u2 = send(hi1, 1)
+    lo3, hi3 = term(3)
+    v1 = send(lo3, 3)
+    own = term(0)
+    u1 = send(lo1 + a, 1)
+    v2 = send(hi3 + b, 3)
     keep = lax.dynamic_slice_in_dim(kept, t, 1, 0)
-    return final_norm(residual, p0, (u1, u2), (v1, v2), gain, keep)
+    return final_norm(residual, own, (u1, u2), (v1, v2), gain, keep)
 
 
 def solution(mesh):

time: 136 us -> 133 us (0.978)
  local copies, waits for them, and re-layouts: 15.9 us -> 2.84 us
  Pallas kernels: 36.8 us -> 47.4 us
  waiting for transfers between devices: 49.6 us -> 41.9 us
  other arithmetic: 2.68 us -> 5.46 us
  starting transfers between devices: 7.33 us -> 9.92 us
    unnamed x20 -> x12, local copies, waits for them, and re-layouts: 15.2 us -> 2.19 us
    pallas_call x4, Pallas kernels: 26.2 us -> 37.9 us  [block_term(): pl.pallas_call(block_kernel, name='block_term', out_shape=[jax.ShapeDtype...]
    ppermute x6, waiting for transfers between devices: 18.7 us -> 12.3 us  [send(): return lax.ppermute(x, 'tp', ring(4, s))]
    ppermute x6, starting transfers between devices: 7.33 us -> 9.92 us  [send(): return lax.ppermute(x, 'tp', ring(4, s))]
    another operation x4, other arithmetic: 0.3 us -> 2.4 us  [term(): meta = jnp.stack([local, position * blk_dev + local])]
    pallas_call x1, Pallas kernels: 7.63 us -> 5.58 us  [kv_project(): pl.pallas_call(kv_kernel, name='kv_project', out_shape=jax.ShapeDtypeStru...]
    add x1 -> x2, other arithmetic: 1.21 us -> 3.06 us  [the longest x1 2.07 us: on_device(): v2 = send(hi3 + b, 3)]
  transfers between devices with their start and end apart: 7 -> 7, of which waited for: 3 -> 3; matrix products, arithmetic and copies ran while one was open for 9% -> 12% of each run, Pallas kernels for 14% -> 22%
where the time goes in v2:
time: 133 us; the launch traced here: 131 us
  Pallas kernels  47.4 us (36%)
  waiting for transfers between devices  41.9 us (32%)
  between operations  13.5 us (10%)
  starting transfers between devices  9.92 us (7%)
  matrix products  9.5 us (7%)
  other arithmetic  5.46 us (4%)
  local copies, waits for them, and re-layouts  2.84 us (2%)
    pallas_call x4, Pallas kernels, block_term(): pl.pallas_call(block_kernel, name='block_term', out_shape=[jax.ShapeDtype...  37.9 us
    all_gather x1, waiting for transfers between devices, on_device(): kv = lax.all_gather(kv_own, CTX, axis=0, tiled=True)  29.5 us
    ppermute x6, waiting for transfers between devices, send(): return lax.ppermute(x, 'tp', ring(4, s))  12.3 us
    ppermute x6, starting transfers between devices, send(): return lax.ppermute(x, 'tp', ring(4, s))  9.92 us
    dot_general x1, matrix products, on_device(): jnp.dot(activations, w_query, preferred_element_type=F32).astype(BF16)  9.5 us
    pallas_call x1, Pallas kernels, kv_project(): pl.pallas_call(kv_kernel, name='kv_project', out_shape=jax.ShapeDtypeStru...  5.58 us
    pallas_call x1, Pallas kernels, final_norm(): pl.pallas_call(norm_kernel, name='final_norm', out_shape=jax.ShapeDtypeSt...  3.98 us
  transfers between devices with their start and end apart: 7, of which 3 were waited for; matrix products, arithmetic and copies ran while one was open for 12% of the time, Pallas kernels for 22%

profile of v2, /device:TPU:24, one launch (start us, length us, event | category | flops | bytes accessed | tf_op | source)
XLA Modules:
  0.0 130.5 jit_solution(15288265633182170876)
XLA Ops:
  6.5 0.0 all-gather.2.cloned.1.call-start
  6.5 5.6 %kv_project.1 = bf16[512,256]{1,0:T(8,128)(2,1)} custom-call(bf16[512,5120]{1,0:T(8,128)(2,1)} %x_ref.1, bf16[5120,128]{1,0:T(8,128)(2,1)} %wk_ref.1, bf16[5120,128]{1,0:T(8,128)(2,1)} %wv_ref.1), custom_call_target="tpu_custom_call" | custom-call | flops 1342177280 | bytes 7864320 | tf_op jit(solution)/shard_map/kv_project/pallas_call | solution.py:47
  12.1 0.0 all-gather.2.cloned.1.call-update
  12.2 0.6 pad_add_fusion.2.meta_ref
  12.8 9.5 %convolution_convert_fusion.q_ref = bf16[512,640]{1,0:T(8,128)(2,1)} fusion(bf16[512,5120]{1,0:T(8,128)(2,1)} %x_ref.1, bf16[5120,640]{1,0:T(8,128)(2,1)} %param.11), kind=kOutput, calls=%fused_computation | convolution fusion | flops 3355770880 | bytes 12451840 | tf_op jit(solution)/shard_map/dot_general | solution.py:220
  22.3 29.5 %all-gather.2.cloned.1.call-done.kv_ref = bf16[8192,256]{1,0:T(8,128)(2,1)} async-done(((bf16[512,256]{1,0:T(8,128)(2,1)}), bf16[8192,256]{1,0:T(8,128)(2,1)}) %all-gather.2.cloned.1.call-update) | async-done | bytes 4194320 | tf_op jit(solution)/shard_map/all_gather | solution.py:219
  51.8 9.5 %block_term.6 = (bf16[128,2560]{1,0:T(8,128)(2,1)}, bf16[128,2560]{1,0:T(8,128)(2,1)}) custom-call(s32[2]{0:T(128)} %pad_add_fusion.2.meta_ref, s32[4,16]{1,0:T(4,128)} %anc_ref.7, bf16[512,640]{1,0:T(8,128)(2,1)} %convolution_convert_fusion.q_ref, bf16[8192,256]{1,0:T(8,128)(2,1)} %all-gather.2.cloned.1.call-done.kv_ref, bf16[640,5120]{1,0:T(8,128)(2,1)} %w_ref.7), custom_call_target="tpu_custom_call" | custom-call | flops 1048576 | bytes 1048576 | tf_op jit(solution)/shard_map/block_term/pallas_call | solution.py:154
  61.3 1.5 %collective-permute-start = (bf16[128,2560]{1,0:T(8,128)(2,1)}, bf16[128,2560]{1,0:T(8,128)(2,1)S(1)}, u32[]{:S(2)}, u32[]{:S(2)}) collective-permute-start(bf16[128,2560]{1,0:T(8,128)(2,1)} %get-tuple-element.16), channel_id=1, source_target_pairs={{0,1},{1,2},{2,3},{3,0},{4,5},{5,6},{6,7},{7,4},{8,9},{9,10},{10,1... | collective-permute-start | bytes 1966088 | tf_op jit(solution)/shard_map/ppermute | solution.py:231
  62.9 1.8 %collective-permute-start.4 = (bf16[128,2560]{1,0:T(8,128)(2,1)}, bf16[128,2560]{1,0:T(8,128)(2,1)S(1)}, u32[]{:S(2)}, u32[]{:S(2)}) collective-permute-start(bf16[128,2560]{1,0:T(8,128)(2,1)} %get-tuple-element.20), channel_id=1, source_target_pairs={{0,3},{1,0},{2,1},{3,2},{4,7},{5,4},{6,5},{7,6},{8,11},{9,8},{10,9... | collective-permute-start | bytes 1966088 | tf_op jit(solution)/shard_map/ppermute | solution.py:231
  64.6 0.6 pad_add_fusion.1.meta_ref
  65.2 0.6 pad_add_fusion.3.meta_ref
  65.8 9.5 %block_term.5 = (bf16[128,2560]{1,0:T(8,128)(2,1)}, bf16[128,2560]{1,0:T(8,128)(2,1)}) custom-call(s32[2]{0:T(128)} %pad_add_fusion.1.meta_ref, s32[4,16]{1,0:T(4,128)} %anc_ref.7, bf16[512,640]{1,0:T(8,128)(2,1)} %convolution_convert_fusion.q_ref, bf16[8192,256]{1,0:T(8,128)(2,1)} %all-gather.2.cloned.1.call-done.kv_ref, bf16[640,5120]{1,0:T(8,128)(2,1)} %w_ref.7), custom_call_target="tpu_custom_call" | custom-call | flops 1048576 | bytes 1048576 | tf_op jit(solution)/shard_map/block_term/pallas_call | solution.py:154
  75.4 0.0 copy-start.5
  75.4 0.3 collective-permute-start.2
  75.7 9.7 %block_term.7 = (bf16[128,2560]{1,0:T(8,128)(2,1)}, bf16[128,2560]{1,0:T(8,128)(2,1)}) custom-call(s32[2]{0:T(128)} %pad_add_fusion.3.meta_ref, s32[4,16]{1,0:T(4,128)} %anc_ref.7, bf16[512,640]{1,0:T(8,128)(2,1)} %convolution_convert_fusion.q_ref, bf16[8192,256]{1,0:T(8,128)(2,1)} %all-gather.2.cloned.1.call-done.kv_ref, bf16[640,5120]{1,0:T(8,128)(2,1)} %w_ref.7), custom_call_target="tpu_custom_call" | custom-call | flops 1048576 | bytes 1048576 | tf_op jit(solution)/shard_map/block_term/pallas_call | solution.py:154
  85.4 3.1 %collective-permute-start.3 = (bf16[128,2560]{1,0:T(8,128)(2,1)}, bf16[128,2560]{1,0:T(8,128)(2,1)S(1)}, u32[]{:S(2)}, u32[]{:S(2)}) collective-permute-start(bf16[128,2560]{1,0:T(8,128)(2,1)} %get-tuple-element.18), channel_id=1, source_target_pairs={{0,3},{1,0},{2,1},{3,2},{4,7},{5,4},{6,5},{7,6},{8,11},{9,8},{10,9... | collective-permute-start | bytes 1966088 | tf_op jit(solution)/shard_map/ppermute | solution.py:231
  88.5 0.0 collective-permute-done
  88.5 1.0 add.59
  89.5 0.0 collective-permute-start.1
  89.5 0.0 collective-permute-done.4
  89.5 2.1 %add.63 = bf16[128,2560]{1,0:T(8,128)(2,1)} add(bf16[128,2560]{1,0:T(8,128)(2,1)} %get-tuple-element.19, bf16[128,2560]{1,0:T(8,128)(2,1)S(1)} %collective-permute-done.4) | non-fusion elementwise | flops 327680 | bytes 1966080 | tf_op jit(solution)/shard_map/add | solution.py:242
  91.6 3.2 %collective-permute-start.5 = (bf16[128,2560]{1,0:T(8,128)(2,1)}, bf16[128,2560]{1,0:T(8,128)(2,1)}, u32[]{:S(2)}, u32[]{:S(2)}) collective-permute-start(bf16[128,2560]{1,0:T(8,128)(2,1)} %add.63), channel_id=1, source_target_pairs={{0,3},{1,0},{2,1},{3,2},{4,7},{5,4},{6,5},{7,6},{8,11},{9,8},{10,9... | collective-permute-start | bytes 1966088 | tf_op jit(solution)/shard_map/ppermute | solution.py:231
  94.8 0.6 dynamic_slice.3.keep_ref
  95.4 0.7 pad_add_fusion.meta_ref
  96.1 9.1 %block_term.4 = (bf16[128,2560]{1,0:T(8,128)(2,1)}, bf16[128,2560]{1,0:T(8,128)(2,1)}) custom-call(s32[2]{0:T(128)} %pad_add_fusion.meta_ref, s32[4,16]{1,0:T(4,128)} %anc_ref.7, bf16[512,640]{1,0:T(8,128)(2,1)} %convolution_convert_fusion.q_ref, bf16[8192,256]{1,0:T(8,128)(2,1)} %all-gather.2.cloned.1.call-done.kv_ref, bf16[640,5120]{1,0:T(8,128)(2,1)} %w_ref.7), custom_call_target="tpu_custom_call" | custom-call | flops 1048576 | bytes 1048576 | tf_op jit(solution)/shard_map/block_term/pallas_call | solution.py:154
  105.2 0.0 collective-permute-done.2.u2_ref
  105.2 0.0 collective-permute-done.3.v1_ref
  105.2 3.1 %collective-permute-done.1.u1_ref = bf16[128,2560]{1,0:T(8,128)(2,1)S(1)} collective-permute-done((bf16[128,2560]{1,0:T(8,128)(2,1)}, bf16[128,2560]{1,0:T(8,128)(2,1)S(1)}, u32[]{:S(2)}, u32[]{:S(2)}) %collective-permute-start.1) | collective-permute-done | bytes 655392 | tf_op jit(solution)/shard_map/ppermute | solution.py:231
  108.3 9.2 %collective-permute-done.5.v2_ref = bf16[128,2560]{1,0:T(8,128)(2,1)} collective-permute-done((bf16[128,2560]{1,0:T(8,128)(2,1)}, bf16[128,2560]{1,0:T(8,128)(2,1)}, u32[]{:S(2)}, u32[]{:S(2)}) %collective-permute-start.5) | collective-permute-done | bytes 655392 | tf_op jit(solution)/shard_map/ppermute | solution.py:231
  117.5 1.1 copy-done.1
  118.6 1.1 copy-done.2
  119.7 4.0 %final_norm.1 = bf16[128,5120]{1,0:T(8,128)(2,1)} custom-call(bf16[128,5120]{1,0:T(8,128)(2,1)S(1)} %copy-done, bf16[128,2560]{1,0:T(8,128)(2,1)S(1)} %copy-done.1, bf16[128,2560]{1,0:T(8,128)(2,1)S(1)} %copy-done.2, bf16[128,2560]{1,0:T(8,128)(2,1)S(1)} %collective-permute-done.1.u1_ref, bf16[128,2560]{1,0:T(8,128)(2,1)S(1)} %collective-permute-done.2.u2_ref, ...), custom_call_target="tpu_custom_call" | custom-call | tf_op jit(solution)/shard_map/final_norm/pallas_call | solution.py:202
  (9 shorter events, 0.0 us)
Async XLA Ops:
  6.5 45.3 %all-gather.2.cloned.1.call-start = ((), (), s32[]{:S(2)}) async-start(), calls=%async_computation | async-start | bytes 4456448 | tf_op jit(solution)/shard_map/all_gather | solution.py:219
  61.3 27.1 %collective-permute-start = (bf16[128,2560]{1,0:T(8,128)(2,1)}, bf16[128,2560]{1,0:T(8,128)(2,1)S(1)}, u32[]{:S(2)}, u32[]{:S(2)}) collective-permute-start(bf16[128,2560]{1,0:T(8,128)(2,1)} %get-tuple-element.16), channel_id=1, source_target_pairs={{0,1},{1,2},{2,3},{3,0},{4,5},{5,6},{6,7},{7,4},{8,9},{9,10},{10,1... | collective-permute-start | bytes 1966088 | tf_op jit(solution)/shard_map/ppermute | solution.py:231
  62.9 26.6 %collective-permute-start.4 = (bf16[128,2560]{1,0:T(8,128)(2,1)}, bf16[128,2560]{1,0:T(8,128)(2,1)S(1)}, u32[]{:S(2)}, u32[]{:S(2)}) collective-permute-start(bf16[128,2560]{1,0:T(8,128)(2,1)} %get-tuple-element.20), channel_id=1, source_target_pairs={{0,3},{1,0},{2,1},{3,2},{4,7},{5,4},{6,5},{7,6},{8,11},{9,8},{10,9... | collective-permute-start | bytes 1966088 | tf_op jit(solution)/shard_map/ppermute | solution.py:231
  75.4 13.1 %copy-start.4 = (bf16[128,2560]{1,0:T(8,128)(2,1)S(1)}, bf16[128,2560]{1,0:T(8,128)(2,1)}, u32[]{:S(2)}) copy-start(bf16[128,2560]{1,0:T(8,128)(2,1)} %get-tuple-element.15) | copy-start | bytes 1966084
  75.4 19.4 %copy-start.5 = (s32[4]{0:T(128)S(1)}, s32[4]{0:T(128)}, u32[]{:S(2)}) copy-start(s32[4]{0:T(128)} %param.17) | copy-start | bytes 52
  75.4 29.8 %collective-permute-start.2 = (bf16[128,2560]{1,0:T(8,128)(2,1)}, bf16[128,2560]{1,0:T(8,128)(2,1)S(1)}, u32[]{:S(2)}, u32[]{:S(2)}) collective-permute-start(bf16[128,2560]{1,0:T(8,128)(2,1)} %get-tuple-element.17), channel_id=1, source_target_pairs={{0,1},{1,2},{2,3},{3,0},{4,5},{5,6},{6,7},{7,4},{8,9},{9,10},{10,1... | collective-permute-start | bytes 1966088 | tf_op jit(solution)/shard_map/ppermute | solution.py:231
  85.4 19.8 %collective-permute-start.3 = (bf16[128,2560]{1,0:T(8,128)(2,1)}, bf16[128,2560]{1,0:T(8,128)(2,1)S(1)}, u32[]{:S(2)}, u32[]{:S(2)}) collective-permute-start(bf16[128,2560]{1,0:T(8,128)(2,1)} %get-tuple-element.18), channel_id=1, source_target_pairs={{0,3},{1,0},{2,1},{3,2},{4,7},{5,4},{6,5},{7,6},{8,11},{9,8},{10,9... | collective-permute-start | bytes 1966088 | tf_op jit(solution)/shard_map/ppermute | solution.py:231
  89.5 18.8 %collective-permute-start.1 = (bf16[128,2560]{1,0:T(8,128)(2,1)}, bf16[128,2560]{1,0:T(8,128)(2,1)S(1)}, u32[]{:S(2)}, u32[]{:S(2)}) collective-permute-start(bf16[128,2560]{1,0:T(8,128)(2,1)} %add.59), channel_id=1, source_target_pairs={{0,1},{1,2},{2,3},{3,0},{4,5},{5,6},{6,7},{7,4},{8,9},{9,10},{10,1... | collective-permute-start | bytes 1966088 | tf_op jit(solution)/shard_map/ppermute | solution.py:231
  91.6 26.0 %collective-permute-start.5 = (bf16[128,2560]{1,0:T(8,128)(2,1)}, bf16[128,2560]{1,0:T(8,128)(2,1)}, u32[]{:S(2)}, u32[]{:S(2)}) collective-permute-start(bf16[128,2560]{1,0:T(8,128)(2,1)} %add.63), channel_id=1, source_target_pairs={{0,3},{1,0},{2,1},{3,2},{4,7},{5,4},{6,5},{7,6},{8,11},{9,8},{10,9... | collective-permute-start | bytes 1966088 | tf_op jit(solution)/shard_map/ppermute | solution.py:231
  96.1 21.4 %copy-start = (bf16[128,5120]{1,0:T(8,128)(2,1)S(1)}, bf16[128,5120]{1,0:T(8,128)(2,1)}, u32[]{:S(2)}) copy-start(bf16[128,5120]{1,0:T(8,128)(2,1)} %res_ref.1) | copy-start | bytes 3932164
  96.1 21.4 %copy-start.3 = (f32[5120]{0:T(1024)S(1)}, f32[5120]{0:T(1024)}, u32[]{:S(2)}) copy-start(f32[5120]{0:T(1024)} %param.15) | copy-start | bytes 61444
  117.5 1.1 copy-start.1
  118.6 1.1 copy-start.2
Sparse Core Ops, SparseCore 0:
  12.3 39.4 all-gather.1

commit v3 on v2

v3 whole, which is shorter than its diff:
```python
import functools
import math

import jax
import jax.numpy as jnp
from jax import lax
from jax.experimental import pallas as pl
from jax.experimental.pallas import tpu as pltpu
from jax.sharding import Mesh, PartitionSpec as P

HD = 128
BLK = 128
CHUNK = 4
CTX = ("z", "y", "core")
F32 = jnp.float32
BF16 = jnp.bfloat16
SCALE2 = math.log2(math.e) / math.sqrt(HD)
SPLIT = ((0, 3), (3, 5))
KERNEL_VMEM = 54 << 20
NT = (((1,), (1,)), ((), ()))


def kv_kernel(x_ref, wk_ref, wv_ref, o_ref, xbuf, wbuf, sems):
    parts, _, tile = xbuf.shape
    copies = []
    for k in range(parts):
        cut = pl.ds(k * tile, tile)
        group = [
            pltpu.make_async_copy(x_ref.at[:, cut], xbuf.at[k], sems.at[0, k]),
            pltpu.make_async_copy(wk_ref.at[cut], wbuf.at[k, :, pl.ds(0, HD)], sems.at[1, k]),
            pltpu.make_async_copy(wv_ref.at[cut], wbuf.at[k, :, pl.ds(HD, HD)], sems.at[2, k]),
        ]
        for copy in group:
            copy.start()
        copies.append(group)
    total = None
    for k in range(parts):
        for copy in copies[k]:
            copy.wait()
        part = jnp.dot(xbuf[k], wbuf[k], preferred_element_type=F32)
        total = part if total is None else total + part
    o_ref[...] = total.astype(BF16)


def kv_project(x, wk, wv):
    rows, depth = x.shape
    parts = 10
    tile = depth // parts
    hbm = pl.BlockSpec(memory_space=pltpu.HBM)
    return pl.pallas_call(
        kv_kernel,
        name="kv_project",
        out_shape=jax.ShapeDtypeStruct((rows, 2 * HD), BF16),
        in_specs=[hbm] * 3,
        out_specs=pl.BlockSpec(memory_space=pltpu.VMEM),
        scratch_shapes=[
            pltpu.VMEM((parts, rows, tile), BF16),
            pltpu.VMEM((parts, tile, 2 * HD), BF16),
            pltpu.SemaphoreType.DMA((3, parts)),
        ],
        cost_estimate=pl.CostEstimate(
            flops=2 * rows * depth * 2 * HD,
            bytes_accessed=2 * depth * (rows + 2 * HD),
            transcendentals=0,
        ),
    )(x, wk, wv)


def attend(q, kv_ref, own_row, rows, count):
    slots = len(rows)
    take = [kv_ref[pl.ds(pl.multiple_of(r, BLK), BLK), :] for r in rows]
    own = kv_ref[pl.ds(pl.multiple_of(own_row, BLK), BLK), :]
    groups = [take[c:c + CHUNK] for c in range(0, slots, CHUNK)]
    keys = [jnp.concatenate([x[:, :HD] for x in g], axis=0) for g in groups]
    values = [jnp.concatenate([x[:, HD:] for x in g], axis=0) for g in groups]
    results = []
    for lo, hi in SPLIT:
        part = q[lo * BLK:hi * BLK]
        s = lax.dot_general(part, own[:, :HD], NT, preferred_element_type=F32)
        row = lax.broadcasted_iota(jnp.int32, s.shape, 0) % BLK
        col = lax.broadcasted_iota(jnp.int32, s.shape, 1)
        pieces = [jnp.where(col <= row, s, -jnp.inf)]
        for c, key in enumerate(keys):
            s = lax.dot_general(part, key, NT, preferred_element_type=F32)
            for j in range(CHUNK):
                pieces.append(
                    jnp.where(c * CHUNK + j < count, s[:, j * BLK:(j + 1) * BLK], -jnp.inf)
                )
        top = pieces[0]
        for piece in pieces[1:]:
            top = jnp.maximum(top, piece)
        top = jnp.max(top, axis=1, keepdims=True)
        weights = [jnp.exp2((piece - top) * SCALE2) for piece in pieces]
        total = weights[0]
        for w in weights[1:]:
            total = total + w
        out = jnp.dot(weights[0].astype(BF16), own[:, HD:], preferred_element_type=F32)
        for c, value in enumerate(values):
            w = jnp.concatenate(
                [x.astype(BF16) for x in weights[1 + c * CHUNK:1 + (c + 1) * CHUNK]], axis=1
            )
            out = out + jnp.dot(w, value, preferred_element_type=F32)
        out = (out / jnp.sum(total, axis=1, keepdims=True)).astype(BF16)
        results += [out[h * BLK:(h + 1) * BLK] for h in range(hi - lo)]
    return jnp.concatenate(results, axis=1)


def block_kernel(places, order_ref, rows_ref, q_ref, w_ref, *rest):
    pieces, outs = rest[:len(places)], rest[len(places):-4]
    kvbuf, wbuf, sems, wsem = rest[-4:]
    step = pl.program_id(0)
    w_copy = pltpu.make_async_copy(w_ref, wbuf, wsem.at[0])

    copies = []
    for piece, spots in zip(pieces, places):
        size = piece.shape[0] // len(spots)
        for k, spot in enumerate(spots):
            copies.append(
                pltpu.make_async_copy(
                    piece.at[pl.ds(k * size, size)],
                    kvbuf.at[pl.ds(spot, size)],
                    sems.at[len(copies)],
                )
            )

    @pl.when(step == 0)
    def _():
        for copy in copies:
            copy.start()
        w_copy.start()
        for copy in copies:
            copy.wait()

    local = order_ref[step]
    slots = rows_ref.shape[1]
    rows, count = [], jnp.int32(0)
    for l in range(slots):
        entry = rows_ref[local, l]
        count += jnp.where(entry >= 0, 1, 0).astype(jnp.int32)
        rows.append(jnp.maximum(entry, 0))
    q_all = q_ref[...]
    heads = q_all.shape[1] // HD
    q = jnp.concatenate([q_all[:, h * HD:(h + 1) * HD] for h in range(heads)], axis=0)
    head_out = attend(q, kvbuf, local * BLK, rows, count)

    @pl.when(step == 0)
    def _():
        w_copy.wait()

    half = outs[0].shape[1]
    tile = half // 2
    for side in range(2):
        for c in range(0, half, tile):
            start = side * half + c
            part = jnp.dot(
                head_out, wbuf[:, start:start + tile], preferred_element_type=F32
            ).astype(BF16)
            for k in range(len(outs) // 2):
                @pl.when(step == k)
                def _():
                    outs[2 * k + side][:, c:c + tile] = part


def block_terms(order, rows, q, kv, w_out):
    pieces, places = zip(*kv)
    keys = sum(x.shape[0] for x in pieces)
    moves = sum(len(x) for x in places)
    count = order.shape[0]
    width = q.shape[1]
    cols = w_out.shape[1]
    outs = pl.pallas_call(
        functools.partial(block_kernel, places),
        name="block_terms",
        out_shape=[jax.ShapeDtypeStruct((BLK, cols // 2), BF16)] * (2 * count),
        grid_spec=pltpu.PrefetchScalarGridSpec(
            num_scalar_prefetch=2,
            grid=(count,),
            in_specs=[
                pl.BlockSpec((BLK, width), lambda i, order, rows: (order[i], 0)),
                pl.BlockSpec(memory_space=pltpu.HBM),
            ]
            + [pl.BlockSpec(memory_space=pl.ANY)] * len(pieces),
            out_specs=[pl.BlockSpec((BLK, cols // 2), lambda i, order, rows: (0, 0))]
            * (2 * count),
            scratch_shapes=[
                pltpu.VMEM((keys, 2 * HD), BF16),
                pltpu.VMEM(w_out.shape, BF16),
                pltpu.SemaphoreType.DMA((moves,)),
                pltpu.SemaphoreType.DMA((1,)),
            ],
        ),
        compiler_params=pltpu.CompilerParams(vmem_limit_bytes=KERNEL_VMEM),
        cost_estimate=pl.CostEstimate(flops=1 << 20, bytes_accessed=1 << 20, transcendentals=0),
    )(order, rows, q, w_out, *pieces)
    return [(outs[2 * k], outs[2 * k + 1]) for k in range(count)]


def norm_kernel(res_ref, o1_ref, o2_ref, u1_ref, u2_ref, v1_ref, v2_ref, gain_ref, keep_ref, o_ref):
    half = u1_ref.shape[1]
    total = []
    for lo, o, u, v in ((0, o1_ref, u1_ref, v1_ref), (half, o2_ref, u2_ref, v2_ref)):
        total.append(
            res_ref[:, lo:lo + half].astype(F32)
            + o[...].astype(F32)
            + u[...].astype(F32)
            + v[...].astype(F32)
        )
    square = sum(jnp.sum(x * x, axis=1, keepdims=True) for x in total)
    factor = lax.rsqrt(square * (1.0 / (2 * half)) + 1e-06) * keep_ref[0].astype(F32)
    for lo, x in zip((0, half), total):
        o_ref[:, lo:lo + half] = (x * factor * gain_ref[:, lo:lo + half]).astype(BF16)


def final_norm(residual, own, u, v, gain, keep):
    rows, cols = residual.shape
    vm = pl.BlockSpec(memory_space=pltpu.VMEM)
    return pl.pallas_call(
        norm_kernel,
        name="final_norm",
        out_shape=jax.ShapeDtypeStruct((rows, cols), BF16),
        in_specs=[vm] * 8 + [pl.BlockSpec(memory_space=pltpu.SMEM)],
        out_specs=vm,
        compiler_params=pltpu.CompilerParams(vmem_limit_bytes=30 << 20),
    )(residual, *own, *u, *v, gain[None, :], keep)


def ring(n, s):
    return [(i, (i + s) % n) for i in range(n)]


def shift(x, axis, s):
    return lax.ppermute(x, axis, ring({"y": 2, "core": 2, "z": 4, "tp": 4}[axis], s))


def gather_blocks(own, queries_of):
    rows = own.shape[0]
    half = rows // 2
    own_c = shift(own, "core", 1)
    y = shift(own, "y", 1)
    up = shift(own, "z", 3)
    down = shift(own, "z", 1)
    queries, y, up, down = lax.optimization_barrier((queries_of(), y, up, down))
    y_up = shift(y, "z", 3)
    y_down = shift(y, "z", 1)
    far_a = shift(up[:half], "z", 3)
    far_b = shift(down[half:], "z", 1)
    y_far = shift(y, "z", 2)
    first = shift(jnp.concatenate([y, up, down], axis=0), "core", 1)
    second = shift(jnp.concatenate([y_up, y_down, far_a, far_b, y_far], axis=0), "core", 1)
    spot = lambda dz, dy, dc: (dz * 4 + dy * 2 + dc) * rows
    return queries, [
        (own, (spot(0, 0, 0),)),
        (own_c, (spot(0, 0, 1),)),
        (y, (spot(0, 1, 0),)),
        (up, (spot(1, 0, 0),)),
        (down, (spot(3, 0, 0),)),
        (first, (spot(0, 1, 1), spot(1, 0, 1), spot(3, 0, 1))),
        (y_up, (spot(1, 1, 0),)),
        (y_down, (spot(3, 1, 0),)),
        (far_a, (spot(2, 0, 0),)),
        (far_b, (spot(2, 0, 0) + half,)),
        (y_far, (spot(2, 1, 0),)),
        (second, (spot(1, 1, 1), spot(3, 1, 1), spot(2, 0, 1), spot(2, 1, 1))),
    ]


def block_rows(ancestors):
    per = ancestors.shape[0]
    owner = ancestors // per
    dz = (owner // 4 - lax.axis_index("z")) % 4
    dy = (owner // 2 - lax.axis_index("y")) % 2
    dc = (owner - lax.axis_index("core")) % 2
    row = ((dz * 4 + dy * 2 + dc) * per + ancestors % per) * BLK
    return jnp.where(ancestors >= 0, row, -1).astype(jnp.int32)


def on_device(activations, residual, w_query, w_key, w_value, w_out, gain, ancestors, kept):
    kv_own = kv_project(activations, w_key, w_value)
    queries, kv = gather_blocks(
        kv_own,
        lambda: jnp.dot(activations, w_query, preferred_element_type=F32).astype(BF16),
    )
    rows = block_rows(ancestors)
    t = lax.axis_index("tp").astype(jnp.int32)
    order = (t + jnp.array([2, 1, 3, 0], jnp.int32)) % 4

    def send(x, s):
        return shift(x, "tp", s % 4)

    ((lo2, hi2),) = block_terms(order[:1], rows, queries, kv, w_out)
    a = send(lo2, 1)
    b = send(hi2, 3)
    (lo1, hi1), (lo3, hi3), own = block_terms(order[1:], rows, queries, kv, w_out)
    u2 = send(hi1, 1)
    v1 = send(lo3, 3)
    u1 = send(lo1 + a, 1)
    v2 = send(hi3 + b, 3)
    keep = lax.dynamic_slice_in_dim(kept, t, 1, 0)
    return final_norm(residual, own, (u1, u2), (v1, v2), gain, keep)


def solution(mesh):
    fine = Mesh(mesh.devices.reshape(2, 4, 2, 2, 4), ("dp", "z", "y", "core", "tp"))
    ctx = ("dp",) + CTX
    in_specs = (
        P(ctx, None),
        P(ctx + ("tp",), None),
        P(None, "tp"),
        P(None, "tp"),
        P(None, "tp"),
        P("tp", None),
        P(),
        P(ctx, None),
        P(ctx),
    )
    out_specs = P(ctx + ("tp",), None)
    return jax.shard_map(
        on_device, mesh=fine, in_specs=in_specs, out_specs=out_specs, check_vma=False
    )
```

time: 133 us -> 115 us (0.86); the launches traced: 131 us -> 114 us
  between operations: 13.5 us -> 0.2 us
  starting transfers between devices: 9.92 us -> 22.8 us
  waiting for transfers between devices: 41.9 us -> 31.8 us
  Pallas kernels: 47.4 us -> 38.2 us
  local copies, waits for them, and re-layouts: 2.84 us -> 6.3 us
    all_gather x1 -> x0, waiting for transfers between devices: 29.5 us -> none  [on_device(): kv = lax.all_gather(kv_own, CTX, axis=0, tiled=True)]
    ppermute x6 -> x17, waiting for transfers between devices: 12.3 us -> 31.8 us  [shift(): lax.ppermute(x, axis, ring({'y': 2, 'core': 2, 'z': 4, 'tp': 4}[axis], s))]
    ppermute x6 -> x17, starting transfers between devices: 9.92 us -> 22.8 us  [shift(): lax.ppermute(x, axis, ring({'y': 2, 'core': 2, 'z': 4, 'tp': 4}[axis], s))]
    pallas_call x4 -> x2, Pallas kernels: 37.9 us -> 28.2 us  [block_terms(): pl.pallas_call(functools.partial(block_kernel, places), name='block_terms...]
    another operation x4 -> x0, other arithmetic: 2.4 us -> none  [term(): meta = jnp.stack([local, position * blk_dev + local])]
    unnamed x12 -> x46, local copies, waits for them, and re-layouts: 2.19 us -> 4.27 us
  transfers between devices with their start and end apart: 7 -> 17, of which waited for: 3 -> 5; matrix products, arithmetic and copies ran while one was open for 12% -> 17% of each run, Pallas kernels for 22% -> 17%
where the time goes in v3:
time: 115 us; the launch traced here: 114 us
  Pallas kernels  38.2 us (33%)
  waiting for transfers between devices  31.8 us (28%)
  starting transfers between devices  22.8 us (20%)
  matrix products  9.5 us (8%)
  local copies, waits for them, and re-layouts  6.3 us (5%)
  other arithmetic  5.32 us (5%)
    ppermute x17, waiting for transfers between devices, shift(): lax.ppermute(x, axis, ring({'y': 2, 'core': 2, 'z': 4, 'tp': 4}[axis], s))  31.8 us
    pallas_call x2, Pallas kernels, block_terms(): pl.pallas_call(functools.partial(block_kernel, places), name='block_terms...  28.2 us
    ppermute x17, starting transfers between devices, shift(): lax.ppermute(x, axis, ring({'y': 2, 'core': 2, 'z': 4, 'tp': 4}[axis], s))  22.8 us
    dot_general x1, matrix products, on_device(): jnp.dot(activations, w_query, preferred_element_type=F32).astype(BF16)  9.5 us
    pallas_call x1, Pallas kernels, kv_project(): pl.pallas_call(kv_kernel, name='kv_project', out_shape=jax.ShapeDtypeStru...  5.58 us
    pallas_call x1, Pallas kernels, final_norm(): pl.pallas_call(norm_kernel, name='final_norm', out_shape=jax.ShapeDtypeSt...  4.37 us
    unnamed x46, local copies, waits for them, and re-layouts  4.27 us
  transfers between devices with their start and end apart: 17, of which 5 were waited for; matrix products, arithmetic and copies ran while one was open for 17% of the time, Pallas kernels for 17%

profile of v3, /device:TPU:24, one launch (start us, length us, event | category | flops | bytes accessed | tf_op | source)
XLA Modules:
  0.0 114.1 jit_solution(2600635643892438335)
XLA Ops:
  0.0 5.6 %kv_project.1.rest_0_ = bf16[512,256]{1,0:T(8,128)(2,1)} custom-call(bf16[512,5120]{1,0:T(8,128)(2,1)} %x_ref.1, bf16[5120,128]{1,0:T(8,128)(2,1)} %wk_ref.1, bf16[5120,128]{1,0:T(8,128)(2,1)} %wv_ref.1), custom_call_target="tpu_custom_call" | custom-call | flops 1342177280 | bytes 7864320 | tf_op jit(solution)/shard_map/kv_project/pallas_call | solution.py:50
  5.6 2.0 %collective-permute-start.2 = (bf16[512,256]{1,0:T(8,128)(2,1)}, bf16[512,256]{1,0:T(8,128)(2,1)S(1)}, u32[]{:S(2)}, u32[]{:S(2)}) collective-permute-start(bf16[512,256]{1,0:T(8,128)(2,1)} %kv_project.1.rest_0_), channel_id=1, source_target_pairs={{0,16},{16,32},{32,48},{48,0},{1,17},{17,33},{33,49},{49,1},{2,18}... | collective-permute-start | bytes 786440 | tf_op jit(solution)/shard_map/ppermute | solution.py:232
  7.6 2.2 %collective-permute-start.1 = (bf16[512,256]{1,0:T(8,128)(2,1)}, bf16[512,256]{1,0:T(8,128)(2,1)S(1)}, u32[]{:S(2)}, u32[]{:S(2)}) collective-permute-start(bf16[512,256]{1,0:T(8,128)(2,1)} %kv_project.1.rest_0_), channel_id=1, source_target_pairs={{0,48},{16,0},{32,16},{48,32},{1,49},{17,1},{33,17},{49,33},{2,50}... | collective-permute-start | bytes 786440 | tf_op jit(solution)/shard_map/ppermute | solution.py:232
  9.8 0.7 collective-permute-start
  10.5 9.5 %convolution_convert_fusion.q_ref = bf16[512,640]{1,0:T(8,128)(2,1)} fusion(bf16[512,5120]{1,0:T(8,128)(2,1)} %x_ref.1, bf16[5120,640]{1,0:T(8,128)(2,1)} %param.12), kind=kOutput, calls=%fused_computation | convolution fusion | flops 3355770880 | bytes 12451840 | tf_op jit(solution)/shard_map/dot_general | solution.py:281
  20.1 2.0 %collective-permute-start.5 = (bf16[512,256]{1,0:T(8,128)(2,1)S(1)}, bf16[512,256]{1,0:T(8,128)(2,1)S(1)}, u32[]{:S(2)}, u32[]{:S(2)}) collective-permute-start(bf16[512,256]{1,0:T(8,128)(2,1)S(1)} %collective-permute-done.rest_2_), channel_id=1, source_target_pairs={{0,48},{16,0},{32,16},{48,32},{1,49},{17,1},{33,17},{49,33},{2,50}... | collective-permute-start | bytes 786440 | tf_op jit(solution)/shard_map/ppermute | solution.py:232
  22.2 1.8 %collective-permute-start.9 = (bf16[512,256]{1,0:T(8,128)(2,1)S(1)}, bf16[512,256]{1,0:T(8,128)(2,1)S(1)}, u32[]{:S(2)}, u32[]{:S(2)}) collective-permute-start(bf16[512,256]{1,0:T(8,128)(2,1)S(1)} %collective-permute-done.rest_2_), channel_id=1, source_target_pairs={{0,32},{16,48},{32,0},{48,16},{1,33},{17,49},{33,1},{49,17},{2,34}... | collective-permute-start | bytes 786440 | tf_op jit(solution)/shard_map/ppermute | solution.py:232
  24.0 2.3 %collective-permute-start.8 = (bf16[256,256]{1,0:T(8,128)(2,1)S(1)}, bf16[256,256]{1,0:T(8,128)(2,1)S(1)}, u32[]{:S(2)}, u32[]{:S(2)}) collective-permute-start(bf16[256,256]{1,0:T(8,128)(2,1)S(1)} %slice.14), channel_id=1, source_target_pairs={{0,16},{16,32},{32,48},{48,0},{1,17},{17,33},{33,49},{49,1},{2,18}... | collective-permute-start | bytes 393224 | tf_op jit(solution)/shard_map/ppermute | solution.py:232
  26.3 1.0 collective-permute-start.7
  27.3 6.2 %collective-permute-done.5.rest_6_ = bf16[512,256]{1,0:T(8,128)(2,1)S(1)} collective-permute-done((bf16[512,256]{1,0:T(8,128)(2,1)S(1)}, bf16[512,256]{1,0:T(8,128)(2,1)S(1)}, u32[]{:S(2)}, u32[]{:S(2)}) %collective-permute-start.5) | collective-permute-done | bytes 262176 | tf_op jit(solution)/shard_map/ppermute | solution.py:232
  33.5 0.8 constant_dynamic-update-slice_fusion.4
  34.3 3.0 %collective-permute-done.6.rest_7_ = bf16[512,256]{1,0:T(8,128)(2,1)S(1)} collective-permute-done((bf16[512,256]{1,0:T(8,128)(2,1)S(1)}, bf16[512,256]{1,0:T(8,128)(2,1)S(1)}, u32[]{:S(2)}, u32[]{:S(2)}) %collective-permute-start.6) | collective-permute-done | bytes 262176 | tf_op jit(solution)/shard_map/ppermute | solution.py:232
  37.2 0.8 constant_dynamic-update-slice_fusion.3
  38.0 0.7 constant_dynamic-update-slice_fusion.2
  38.7 0.7 constant_dynamic-update-slice_fusion.1
  39.4 0.8 constant_dynamic-update-slice_fusion
  40.2 0.9 pad_maximum_fusion
  42.5 0.6 fusion.9.rows_ref
  43.2 1.2 %collective-permute-done.3.rest_1_ = bf16[512,256]{1,0:T(8,128)(2,1)S(1)} collective-permute-done((bf16[512,256]{1,0:T(8,128)(2,1)S(1)}, bf16[512,256]{1,0:T(8,128)(2,1)S(1)}, u32[]{:S(2)}, u32[]{:S(2)}) %collective-permute-start.3) | collective-permute-done | bytes 262176 | tf_op jit(solution)/shard_map/ppermute | solution.py:232
  44.4 0.7 copy-done.15
  45.6 9.0 %block_terms.3 = (bf16[128,2560]{1,0:T(8,128)(2,1)}, bf16[128,2560]{1,0:T(8,128)(2,1)}) custom-call(s32[1]{0:T(128)} %bitcast.5, s32[4,16]{1,0:T(4,128)} %fusion.9.rows_ref, bf16[512,640]{1,0:T(8,128)(2,1)} %convolution_convert_fusion.q_ref, bf16[640,5120]{1,0:T(8,128)(2,1)} %w_ref.3, bf16[512,256]{1,0:T(8,128)(2,1)} %kv_project.1.rest_0_, ...), custom_call_target="tpu_custom_call" | custom-call | flops 1048576 | bytes 1048576 | tf_op jit(solution)/shard_map/block_terms/pallas_call | solution.py:171
  54.7 1.6 %collective-permute-start.11 = (bf16[128,2560]{1,0:T(8,128)(2,1)}, bf16[128,2560]{1,0:T(8,128)(2,1)S(1)}, u32[]{:S(2)}, u32[]{:S(2)}) collective-permute-start(bf16[128,2560]{1,0:T(8,128)(2,1)} %get-tuple-element.24), channel_id=1, source_target_pairs={{0,1},{1,2},{2,3},{3,0},{4,5},{5,6},{6,7},{7,4},{8,9},{9,10},{10,1... | collective-permute-start | bytes 1966088 | tf_op jit(solution)/shard_map/ppermute | solution.py:232
  56.2 1.7 %collective-permute-start.15 = (bf16[128,2560]{1,0:T(8,128)(2,1)}, bf16[128,2560]{1,0:T(8,128)(2,1)S(1)}, u32[]{:S(2)}, u32[]{:S(2)}) collective-permute-start(bf16[128,2560]{1,0:T(8,128)(2,1)} %get-tuple-element.28), channel_id=1, source_target_pairs={{0,3},{1,0},{2,1},{3,2},{4,7},{5,4},{6,5},{7,6},{8,11},{9,8},{10,9... | collective-permute-start | bytes 1966088 | tf_op jit(solution)/shard_map/ppermute | solution.py:232
  58.0 0.6 slice.12.order_ref
  58.6 19.2 %block_terms.2 = (bf16[128,2560]{1,0:T(8,128)(2,1)}, bf16[128,2560]{1,0:T(8,128)(2,1)}, bf16[128,2560]{1,0:T(8,128)(2,1)}, bf16[128,2560]{1,0:T(8,128)(2,1)}, bf...) custom-call(s32[3]{0:T(128)} %slice.12.order_ref, s32[4,16]{1,0:T(4,128)} %fusion.9.rows_ref, ...), custom_call_target="tpu_custom_call" | custom-call | flops 1048576 | bytes 1048576 | tf_op jit(solution)/shard_map/block_terms/pallas_call | solution.py:171
  78.2 3.0 %collective-permute-start.14 = (bf16[128,2560]{1,0:T(8,128)(2,1)}, bf16[128,2560]{1,0:T(8,128)(2,1)}, u32[]{:S(2)}, u32[]{:S(2)}) collective-permute-start(bf16[128,2560]{1,0:T(8,128)(2,1)} %get-tuple-element.26), channel_id=1, source_target_pairs={{0,3},{1,0},{2,1},{3,2},{4,7},{5,4},{6,5},{7,6},{8,11},{9,8},{10,9... | collective-permute-start | bytes 1966088 | tf_op jit(solution)/shard_map/ppermute | solution.py:232
  81.2 2.2 %add.61 = bf16[128,2560]{1,0:T(8,128)(2,1)} add(bf16[128,2560]{1,0:T(8,128)(2,1)} %get-tuple-element.23, bf16[128,2560]{1,0:T(8,128)(2,1)S(1)} %collective-permute-done.11) | non-fusion elementwise | flops 327680 | bytes 1966080 | tf_op jit(solution)/shard_map/add | solution.py:296
  83.4 1.0 add.62
  84.4 3.2 %collective-permute-start.16 = (bf16[128,2560]{1,0:T(8,128)(2,1)}, bf16[128,2560]{1,0:T(8,128)(2,1)}, u32[]{:S(2)}, u32[]{:S(2)}) collective-permute-start(bf16[128,2560]{1,0:T(8,128)(2,1)} %add.62), channel_id=1, source_target_pairs={{0,3},{1,0},{2,1},{3,2},{4,7},{5,4},{6,5},{7,6},{8,11},{9,8},{10,9... | collective-permute-start | bytes 1966088 | tf_op jit(solution)/shard_map/ppermute | solution.py:232
  88.3 8.7 %collective-permute-done.13.u2_ref = bf16[128,2560]{1,0:T(8,128)(2,1)S(1)} collective-permute-done((bf16[128,2560]{1,0:T(8,128)(2,1)}, bf16[128,2560]{1,0:T(8,128)(2,1)S(1)}, u32[]{:S(2)}, u32[]{:S(2)}) %collective-permute-start.13) | collective-permute-done | bytes 655392 | tf_op jit(solution)/shard_map/ppermute | solution.py:232
  97.0 12.7 %collective-permute-done.12.u1_ref = bf16[128,2560]{1,0:T(8,128)(2,1)} collective-permute-done((bf16[128,2560]{1,0:T(8,128)(2,1)}, bf16[128,2560]{1,0:T(8,128)(2,1)}, u32[]{:S(2)}, u32[]{:S(2)}) %collective-permute-start.12) | collective-permute-done | bytes 655392 | tf_op jit(solution)/shard_map/ppermute | solution.py:232
  109.7 4.4 %final_norm.1 = bf16[128,5120]{1,0:T(8,128)(2,1)} custom-call(bf16[128,5120]{1,0:T(8,128)(2,1)S(1)} %copy-done, bf16[128,2560]{1,0:T(8,128)(2,1)S(1)} %copy-done.1, bf16[128,2560]{1,0:T(8,128)(2,1)S(1)} %copy-done.2, bf16[128,2560]{1,0:T(8,128)(2,1)} %collective-permute-done.12.u1_ref, bf16[128,2560]{1,0:T(8,128)(2,1)S(1)} %collective-permute-done.13.u2_ref, ...), custom_call_target="tpu_custom_call" | custom-call | tf_op jit(solution)/shard_map/final_norm/pallas_call | solution.py:217
  (63 shorter events, 3.2 us)
Async XLA Ops:
  5.6 14.4 %collective-permute-start.2 = (bf16[512,256]{1,0:T(8,128)(2,1)}, bf16[512,256]{1,0:T(8,128)(2,1)S(1)}, u32[]{:S(2)}, u32[]{:S(2)}) collective-permute-start(bf16[512,256]{1,0:T(8,128)(2,1)} %kv_project.1.rest_0_), channel_id=1, source_target_pairs={{0,16},{16,32},{32,48},{48,0},{1,17},{17,33},{33,49},{49,1},{2,18}... | collective-permute-start | bytes 786440 | tf_op jit(solution)/shard_map/ppermute | solution.py:232
  7.6 12.5 %collective-permute-start.1 = (bf16[512,256]{1,0:T(8,128)(2,1)}, bf16[512,256]{1,0:T(8,128)(2,1)S(1)}, u32[]{:S(2)}, u32[]{:S(2)}) collective-permute-start(bf16[512,256]{1,0:T(8,128)(2,1)} %kv_project.1.rest_0_), channel_id=1, source_target_pairs={{0,48},{16,0},{32,16},{48,32},{1,49},{17,1},{33,17},{49,33},{2,50}... | collective-permute-start | bytes 786440 | tf_op jit(solution)/shard_map/ppermute | solution.py:232
  9.8 10.3 %collective-permute-start = (bf16[512,256]{1,0:T(8,128)(2,1)}, bf16[512,256]{1,0:T(8,128)(2,1)S(1)}, u32[]{:S(2)}, u32[]{:S(2)}) collective-permute-start(bf16[512,256]{1,0:T(8,128)(2,1)} %kv_project.1.rest_0_), channel_id=1, source_target_pairs={{0,8},{8,0},{1,9},{9,1},{2,10},{10,2},{3,11},{11,3},{4,12},{12,4},... | collective-permute-start | bytes 786440 | tf_op jit(solution)/shard_map/ppermute | solution.py:232
  20.0 21.1 %copy-start.5 = (bf16[512,256]{1,0:T(8,128)(2,1)}, bf16[512,256]{1,0:T(8,128)(2,1)S(1)}, u32[]{:S(2)}) copy-start(bf16[512,256]{1,0:T(8,128)(2,1)S(1)} %collective-permute-done.2.rest_4_) | copy-start | bytes 786436
  20.0 21.1 %copy-start.6 = (bf16[512,256]{1,0:T(8,128)(2,1)}, bf16[512,256]{1,0:T(8,128)(2,1)S(1)}, u32[]{:S(2)}) copy-start(bf16[512,256]{1,0:T(8,128)(2,1)S(1)} %collective-permute-done.1.rest_3_) | copy-start | bytes 786436
  20.0 21.1 %copy-start.12 = (bf16[512,256]{1,0:T(8,128)(2,1)}, bf16[512,256]{1,0:T(8,128)(2,1)S(1)}, u32[]{:S(2)}) copy-start(bf16[512,256]{1,0:T(8,128)(2,1)S(1)} %collective-permute-done.rest_2_) | copy-start | bytes 786436
  20.1 13.4 %collective-permute-start.5 = (bf16[512,256]{1,0:T(8,128)(2,1)S(1)}, bf16[512,256]{1,0:T(8,128)(2,1)S(1)}, u32[]{:S(2)}, u32[]{:S(2)}) collective-permute-start(bf16[512,256]{1,0:T(8,128)(2,1)S(1)} %collective-permute-done.rest_2_), channel_id=1, source_target_pairs={{0,48},{16,0},{32,16},{48,32},{1,49},{17,1},{33,17},{49,33},{2,50}... | collective-permute-start | bytes 786440 | tf_op jit(solution)/shard_map/ppermute | solution.py:232
  22.1 15.2 %collective-permute-start.6 = (bf16[512,256]{1,0:T(8,128)(2,1)S(1)}, bf16[512,256]{1,0:T(8,128)(2,1)S(1)}, u32[]{:S(2)}, u32[]{:S(2)}) collective-permute-start(bf16[512,256]{1,0:T(8,128)(2,1)S(1)} %collective-permute-done.rest_2_), channel_id=1, source_target_pairs={{0,16},{16,32},{32,48},{48,0},{1,17},{17,33},{33,49},{49,1},{2,18}... | collective-permute-start | bytes 786440 | tf_op jit(solution)/shard_map/ppermute | solution.py:232
  22.2 17.2 %collective-permute-start.9 = (bf16[512,256]{1,0:T(8,128)(2,1)S(1)}, bf16[512,256]{1,0:T(8,128)(2,1)S(1)}, u32[]{:S(2)}, u32[]{:S(2)}) collective-permute-start(bf16[512,256]{1,0:T(8,128)(2,1)S(1)} %collective-permute-done.rest_2_), channel_id=1, source_target_pairs={{0,32},{16,48},{32,0},{48,16},{1,33},{17,49},{33,1},{49,17},{2,34}... | collective-permute-start | bytes 786440 | tf_op jit(solution)/shard_map/ppermute | solution.py:232
  24.0 14.7 %collective-permute-start.8 = (bf16[256,256]{1,0:T(8,128)(2,1)S(1)}, bf16[256,256]{1,0:T(8,128)(2,1)S(1)}, u32[]{:S(2)}, u32[]{:S(2)}) collective-permute-start(bf16[256,256]{1,0:T(8,128)(2,1)S(1)} %slice.14), channel_id=1, source_target_pairs={{0,16},{16,32},{32,48},{48,0},{1,17},{17,33},{33,49},{49,1},{2,18}... | collective-permute-start | bytes 393224 | tf_op jit(solution)/shard_map/ppermute | solution.py:232
  26.3 11.7 %collective-permute-start.7 = (bf16[256,256]{1,0:T(8,128)(2,1)S(1)}, bf16[256,256]{1,0:T(8,128)(2,1)S(1)}, u32[]{:S(2)}, u32[]{:S(2)}) collective-permute-start(bf16[256,256]{1,0:T(8,128)(2,1)S(1)} %slice.13), channel_id=1, source_target_pairs={{0,48},{16,0},{32,16},{48,32},{1,49},{17,1},{33,17},{49,33},{2,50}... | collective-permute-start | bytes 393224 | tf_op jit(solution)/shard_map/ppermute | solution.py:232
  33.5 7.6 %copy-start.9 = (bf16[512,256]{1,0:T(8,128)(2,1)}, bf16[512,256]{1,0:T(8,128)(2,1)S(1)}, u32[]{:S(2)}) copy-start(bf16[512,256]{1,0:T(8,128)(2,1)S(1)} %collective-permute-done.5.rest_6_) | copy-start | bytes 786436
  34.3 7.5 %copy-start.8 = (bf16[512,256]{1,0:T(8,128)(2,1)S(1)}, bf16[512,256]{1,0:T(8,128)(2,1)}, u32[]{:S(2)}) copy-start(bf16[512,256]{1,0:T(8,128)(2,1)} %kv_project.1.rest_0_) | copy-start | bytes 786436
  34.3 7.7 %copy-start.20 = (s32[4]{0:T(128)S(1)}, s32[4]{0:T(128)}, u32[]{:S(2)}) copy-start(s32[4]{0:T(128)} %constant.95.clone) | copy-start | bytes 52
  34.3 8.3 %copy-start.17 = (s32[4,16]{1,0:T(4,128)S(1)}, s32[4,16]{1,0:T(4,128)}, u32[]{:S(2)}) copy-start(s32[4,16]{1,0:T(4,128)} %param.17) | copy-start | bytes 772
  38.0 6.4 %copy-start.14 = (bf16[256,256]{1,0:T(8,128)(2,1)}, bf16[256,256]{1,0:T(8,128)(2,1)S(1)}, u32[]{:S(2)}) copy-start(bf16[256,256]{1,0:T(8,128)(2,1)S(1)} %collective-permute-done.7.rest_8_) | copy-start | bytes 393220
  38.7 5.7 %copy-start.13 = (bf16[256,256]{1,0:T(8,128)(2,1)}, bf16[256,256]{1,0:T(8,128)(2,1)S(1)}, u32[]{:S(2)}) copy-start(bf16[256,256]{1,0:T(8,128)(2,1)S(1)} %collective-permute-done.8.rest_9_) | copy-start | bytes 393220
  40.2 4.2 %collective-permute-start.10 = (bf16[2048,256]{1,0:T(8,128)(2,1)}, bf16[2048,256]{1,0:T(8,128)(2,1)S(1)}, u32[]{:S(2)}, u32[]{:S(2)}) collective-permute-start(bf16[2048,256]{1,0:T(8,128)(2,1)} %constant_dynamic-update-slice_fusion), channel_id=1, source_target_pairs={{0,4},{4,0},{1,5},{5,1},{2,6},{6,2},{3,7},{7,3},{8,12},{12,8},{9,1... | collective-permute-start | bytes 3145736 | tf_op jit(solution)/shard_map/ppermute | solution.py:232
  41.1 3.2 %collective-permute-start.4 = (bf16[1536,256]{1,0:T(8,128)(2,1)}, bf16[1536,256]{1,0:T(8,128)(2,1)S(1)}, u32[]{:S(2)}, u32[]{:S(2)}) collective-permute-start(bf16[1536,256]{1,0:T(8,128)(2,1)} %pad_maximum_fusion), channel_id=1, source_target_pairs={{0,4},{4,0},{1,5},{5,1},{2,6},{6,2},{3,7},{7,3},{8,12},{12,8},{9,1... | collective-permute-start | bytes 2359304 | tf_op jit(solution)/shard_map/ppermute | solution.py:232
  41.7 2.6 %collective-permute-start.3 = (bf16[512,256]{1,0:T(8,128)(2,1)S(1)}, bf16[512,256]{1,0:T(8,128)(2,1)S(1)}, u32[]{:S(2)}, u32[]{:S(2)}) collective-permute-start(bf16[512,256]{1,0:T(8,128)(2,1)S(1)} %copy-done.8), channel_id=1, source_target_pairs={{0,4},{4,0},{1,5},{5,1},{2,6},{6,2},{3,7},{7,3},{8,12},{12,8},{9,1... | collective-permute-start | bytes 786440 | tf_op jit(solution)/shard_map/ppermute | solution.py:232
  45.6 12.3 %copy-start.18 = (s32[4]{0:T(128)S(1)}, s32[4]{0:T(128)}, u32[]{:S(2)}) copy-start(s32[4]{0:T(128)} %and_select_fusion) | copy-start | bytes 52
  54.7 26.5 %collective-permute-start.11 = (bf16[128,2560]{1,0:T(8,128)(2,1)}, bf16[128,2560]{1,0:T(8,128)(2,1)S(1)}, u32[]{:S(2)}, u32[]{:S(2)}) collective-permute-start(bf16[128,2560]{1,0:T(8,128)(2,1)} %get-tuple-element.24), channel_id=1, source_target_pairs={{0,1},{1,2},{2,3},{3,0},{4,5},{5,6},{6,7},{7,4},{8,9},{9,10},{10,1... | collective-permute-start | bytes 1966088 | tf_op jit(solution)/shard_map/ppermute | solution.py:232
  56.2 27.2 %collective-permute-start.15 = (bf16[128,2560]{1,0:T(8,128)(2,1)}, bf16[128,2560]{1,0:T(8,128)(2,1)S(1)}, u32[]{:S(2)}, u32[]{:S(2)}) collective-permute-start(bf16[128,2560]{1,0:T(8,128)(2,1)} %get-tuple-element.28), channel_id=1, source_target_pairs={{0,3},{1,0},{2,1},{3,2},{4,7},{5,4},{6,5},{7,6},{8,11},{9,8},{10,9... | collective-permute-start | bytes 1966088 | tf_op jit(solution)/shard_map/ppermute | solution.py:232
  77.8 19.2 %collective-permute-start.13 = (bf16[128,2560]{1,0:T(8,128)(2,1)}, bf16[128,2560]{1,0:T(8,128)(2,1)S(1)}, u32[]{:S(2)}, u32[]{:S(2)}) collective-permute-start(bf16[128,2560]{1,0:T(8,128)(2,1)} %get-tuple-element.25), channel_id=1, source_target_pairs={{0,1},{1,2},{2,3},{3,0},{4,5},{5,6},{6,7},{7,4},{8,9},{9,10},{10,1... | collective-permute-start | bytes 1966088 | tf_op jit(solution)/shard_map/ppermute | solution.py:232
  78.2 18.8 %collective-permute-start.14 = (bf16[128,2560]{1,0:T(8,128)(2,1)}, bf16[128,2560]{1,0:T(8,128)(2,1)}, u32[]{:S(2)}, u32[]{:S(2)}) collective-permute-start(bf16[128,2560]{1,0:T(8,128)(2,1)} %get-tuple-element.26), channel_id=1, source_target_pairs={{0,3},{1,0},{2,1},{3,2},{4,7},{5,4},{6,5},{7,6},{8,11},{9,8},{10,9... | collective-permute-start | bytes 1966088 | tf_op jit(solution)/shard_map/ppermute | solution.py:232
  81.2 6.5 %copy-start.19 = (s32[4]{0:T(128)S(1)}, s32[4]{0:T(128)}, u32[]{:S(2)}) copy-start(s32[4]{0:T(128)} %param.18) | copy-start | bytes 52
  81.2 28.5 %copy-start = (bf16[128,5120]{1,0:T(8,128)(2,1)S(1)}, bf16[128,5120]{1,0:T(8,128)(2,1)}, u32[]{:S(2)}) copy-start(bf16[128,5120]{1,0:T(8,128)(2,1)} %res_ref.1) | copy-start | bytes 3932164
  81.2 28.5 %copy-start.1 = (bf16[128,2560]{1,0:T(8,128)(2,1)S(1)}, bf16[128,2560]{1,0:T(8,128)(2,1)}, u32[]{:S(2)}) copy-start(bf16[128,2560]{1,0:T(8,128)(2,1)} %get-tuple-element.21.o1_ref) | copy-start | bytes 1966084
  81.2 28.5 %copy-start.2 = (bf16[128,2560]{1,0:T(8,128)(2,1)S(1)}, bf16[128,2560]{1,0:T(8,128)(2,1)}, u32[]{:S(2)}) copy-start(bf16[128,2560]{1,0:T(8,128)(2,1)} %get-tuple-element.22.o2_ref) | copy-start | bytes 1966084
  81.2 28.5 %copy-start.3 = (f32[5120]{0:T(1024)S(1)}, f32[5120]{0:T(1024)}, u32[]{:S(2)}) copy-start(f32[5120]{0:T(1024)} %param.16) | copy-start | bytes 61444
  83.4 26.3 %collective-permute-start.12 = (bf16[128,2560]{1,0:T(8,128)(2,1)}, bf16[128,2560]{1,0:T(8,128)(2,1)}, u32[]{:S(2)}, u32[]{:S(2)}) collective-permute-start(bf16[128,2560]{1,0:T(8,128)(2,1)} %add.61), channel_id=1, source_target_pairs={{0,1},{1,2},{2,3},{3,0},{4,5},{5,6},{6,7},{7,4},{8,9},{9,10},{10,1... | collective-permute-start | bytes 1966088 | tf_op jit(solution)/shard_map/ppermute | solution.py:232
  84.4 25.3 %collective-permute-start.16 = (bf16[128,2560]{1,0:T(8,128)(2,1)}, bf16[128,2560]{1,0:T(8,128)(2,1)}, u32[]{:S(2)}, u32[]{:S(2)}) collective-permute-start(bf16[128,2560]{1,0:T(8,128)(2,1)} %add.62), channel_id=1, source_target_pairs={{0,3},{1,0},{2,1},{3,2},{4,7},{5,4},{6,5},{7,6},{8,11},{9,8},{10,9... | collective-permute-start | bytes 1966088 | tf_op jit(solution)/shard_map/ppermute | solution.py:232
  (6 other events, 17.4 us)

commit v4 on v3

--- a/solution.py
+++ b/solution.py
@@ -234,34 +234,21 @@
 
 def gather_blocks(own, queries_of):
     rows = own.shape[0]
-    half = rows // 2
-    own_c = shift(own, "core", 1)
-    y = shift(own, "y", 1)
-    up = shift(own, "z", 3)
-    down = shift(own, "z", 1)
-    queries, y, up, down = lax.optimization_barrier((queries_of(), y, up, down))
-    y_up = shift(y, "z", 3)
-    y_down = shift(y, "z", 1)
-    far_a = shift(up[:half], "z", 3)
-    far_b = shift(down[half:], "z", 1)
-    y_far = shift(y, "z", 2)
-    first = shift(jnp.concatenate([y, up, down], axis=0), "core", 1)
-    second = shift(jnp.concatenate([y_up, y_down, far_a, far_b, y_far], axis=0), "core", 1)
-    spot = lambda dz, dy, dc: (dz * 4 + dy * 2 + dc) * rows
-    return queries, [
-        (own, (spot(0, 0, 0),)),
-        (own_c, (spot(0, 0, 1),)),
-        (y, (spot(0, 1, 0),)),
-        (up, (spot(1, 0, 0),)),
-        (down, (spot(3, 0, 0),)),
-        (first, (spot(0, 1, 1), spot(1, 0, 1), spot(3, 0, 1))),
-        (y_up, (spot(1, 1, 0),)),
-        (y_down, (spot(3, 1, 0),)),
-        (far_a, (spot(2, 0, 0),)),
-        (far_b, (spot(2, 0, 0) + half,)),
-        (y_far, (spot(2, 1, 0),)),
-        (second, (spot(1, 1, 1), spot(3, 1, 1), spot(2, 0, 1), spot(2, 1, 1))),
-    ]
+
+    def fetch(dz, dy):
+        pairs = [(i, ((i // 2 - dz) % 4) * 2 + (i + dy) % 2) for i in range(8)]
+        return lax.ppermute(own, ("z", "y"), pairs)
+
+    places = ((2, 1), (2, 0), (1, 1), (3, 1), (0, 1), (1, 0), (3, 0))
+    early = [fetch(*p) for p in places[:5]]
+    queries = queries_of()
+    pieces = early + [fetch(*p) for p in places[5:]]
+    result = []
+    for (dz, dy), piece in zip(((0, 0),) + places, [own] + pieces):
+        other = shift(piece, "core", 1)
+        for dc, x in ((0, piece), (1, other)):
+            result.append((x, ((dz * 4 + dy * 2 + dc) * rows,)))
+    return queries, result
 
 
 def block_rows(ancestors):
@@ -290,9 +277,10 @@
     ((lo2, hi2),) = block_terms(order[:1], rows, queries, kv, w_out)
     a = send(lo2, 1)
     b = send(hi2, 3)
-    (lo1, hi1), (lo3, hi3), own = block_terms(order[1:], rows, queries, kv, w_out)
+    (lo1, hi1), (lo3, hi3) = block_terms(order[1:3], rows, queries, kv, w_out)
     u2 = send(hi1, 1)
     v1 = send(lo3, 3)
+    (own,) = block_terms(order[3:], rows, queries, kv, w_out)
     u1 = send(lo1 + a, 1)
     v2 = send(hi3 + b, 3)
     keep = lax.dynamic_slice_in_dim(kept, t, 1, 0)

time: 115 us -> 114 us (level)
  the two profiles are of different devices: /device:TPU:24 before, /device:TPU:86 now
where the time goes in v4:
time: 114 us; the launch traced here: 113 us
  Pallas kernels  40.8 us (36%)
  waiting for transfers between devices  27.7 us (24%)
  starting transfers between devices  26.2 us (23%)
  matrix products  9.51 us (8%)
  local copies, waits for them, and re-layouts  4.9 us (4%)
  other arithmetic  3.95 us (3%)
    pallas_call x3, Pallas kernels, block_terms(): pl.pallas_call(functools.partial(block_kernel, places), name='block_terms...  32.4 us
    ppermute x7, starting transfers between devices, fetch(): return lax.ppermute(own, ('z', 'y'), pairs)  15.3 us
    ppermute x7, waiting for transfers between devices, fetch(): return lax.ppermute(own, ('z', 'y'), pairs)  13.9 us
    ppermute x14, waiting for transfers between devices, shift(): lax.ppermute(x, axis, ring({'y': 2, 'core': 2, 'z': 4, 'tp': 4}[axis], s))  13.8 us
    ppermute x14, starting transfers between devices, shift(): lax.ppermute(x, axis, ring({'y': 2, 'core': 2, 'z': 4, 'tp': 4}[axis], s))  10.9 us
    dot_general x1, matrix products, on_device(): jnp.dot(activations, w_query, preferred_element_type=F32).astype(BF16)  9.51 us
    pallas_call x1, Pallas kernels, kv_project(): pl.pallas_call(kv_kernel, name='kv_project', out_shape=jax.ShapeDtypeStru...  5.59 us
    unnamed x44, local copies, waits for them, and re-layouts  3.02 us
  transfers between devices with their start and end apart: 21, of which 5 were waited for; matrix products, arithmetic and copies ran while one was open for 14% of the time, Pallas kernels for 21%

profile of v4, /device:TPU:86, one launch (start us, length us, event | category | flops | bytes accessed | tf_op | source)
XLA Modules:
  0.0 113.4 jit_solution(10179775759171939024)
XLA Ops:
  0.0 5.6 %kv_project.1.rest_0_ = bf16[512,256]{1,0:T(8,128)(2,1)} custom-call(bf16[512,5120]{1,0:T(8,128)(2,1)} %x_ref.1, bf16[5120,128]{1,0:T(8,128)(2,1)} %wk_ref.1, bf16[5120,128]{1,0:T(8,128)(2,1)} %wv_ref.1), custom_call_target="tpu_custom_call" | custom-call | flops 1342177280 | bytes 7864320 | tf_op jit(solution)/shard_map/kv_project/pallas_call | solution.py:50
  5.6 1.4 %collective-permute-start.9 = (bf16[512,256]{1,0:T(8,128)(2,1)}, bf16[512,256]{1,0:T(8,128)(2,1)S(1)}, u32[]{:S(2)}, u32[]{:S(2)}) collective-permute-start(bf16[512,256]{1,0:T(8,128)(2,1)} %kv_project.1.rest_0_), channel_id=1, source_target_pairs={{0,8},{8,0},{16,24},{24,16},{32,40},{40,32},{48,56},{56,48},{1,9},... | collective-permute-start | bytes 786440 | tf_op jit(solution)/shard_map/ppermute | solution.py:240
  7.1 1.9 %collective-permute-start.13 = (bf16[512,256]{1,0:T(8,128)(2,1)}, bf16[512,256]{1,0:T(8,128)(2,1)S(1)}, u32[]{:S(2)}, u32[]{:S(2)}) collective-permute-start(bf16[512,256]{1,0:T(8,128)(2,1)} %kv_project.1.rest_0_), channel_id=1, source_target_pairs={{0,16},{8,24},{16,32},{24,40},{32,48},{40,56},{48,0},{56,8},{1,17}... | collective-permute-start | bytes 786440 | tf_op jit(solution)/shard_map/ppermute | solution.py:240
  9.0 1.8 %collective-permute-start.1 = (bf16[512,256]{1,0:T(8,128)(2,1)}, bf16[512,256]{1,0:T(8,128)(2,1)S(1)}, u32[]{:S(2)}, u32[]{:S(2)}) collective-permute-start(bf16[512,256]{1,0:T(8,128)(2,1)} %kv_project.1.rest_0_), channel_id=1, source_target_pairs={{0,40},{8,32},{16,56},{24,48},{32,8},{40,0},{48,24},{56,16},{1,41}... | collective-permute-start | bytes 786440 | tf_op jit(solution)/shard_map/ppermute | solution.py:240
  10.9 1.9 %collective-permute-start.3 = (bf16[512,256]{1,0:T(8,128)(2,1)}, bf16[512,256]{1,0:T(8,128)(2,1)S(1)}, u32[]{:S(2)}, u32[]{:S(2)}) collective-permute-start(bf16[512,256]{1,0:T(8,128)(2,1)} %kv_project.1.rest_0_), channel_id=1, source_target_pairs={{0,32},{8,40},{16,48},{24,56},{32,0},{40,8},{48,16},{56,24},{1,33}... | collective-permute-start | bytes 786440 | tf_op jit(solution)/shard_map/ppermute | solution.py:240
  12.7 2.4 %collective-permute-done.9.rest_10_ = bf16[512,256]{1,0:T(8,128)(2,1)S(1)} collective-permute-done((bf16[512,256]{1,0:T(8,128)(2,1)}, bf16[512,256]{1,0:T(8,128)(2,1)S(1)}, u32[]{:S(2)}, u32[]{:S(2)}) %collective-permute-start.9) | collective-permute-done | bytes 262176 | tf_op jit(solution)/shard_map/ppermute | solution.py:240
  15.1 11.5 %collective-permute-done.11.rest_12_ = bf16[512,256]{1,0:T(8,128)(2,1)S(1)} collective-permute-done((bf16[512,256]{1,0:T(8,128)(2,1)}, bf16[512,256]{1,0:T(8,128)(2,1)S(1)}, u32[]{:S(2)}, u32[]{:S(2)}) %collective-permute-start.11) | collective-permute-done | bytes 262176 | tf_op jit(solution)/shard_map/ppermute | solution.py:240
  26.6 8.2 %collective-permute-start.7 = (bf16[512,256]{1,0:T(8,128)(2,1)}, bf16[512,256]{1,0:T(8,128)(2,1)S(1)}, u32[]{:S(2)}, u32[]{:S(2)}) collective-permute-start(bf16[512,256]{1,0:T(8,128)(2,1)} %kv_project.1.rest_0_), channel_id=1, source_target_pairs={{0,24},{8,16},{16,40},{24,32},{32,56},{40,48},{48,8},{56,0},{1,25}... | collective-permute-start | bytes 786440 | tf_op jit(solution)/shard_map/ppermute | solution.py:240
  34.9 0.5 collective-permute-start.10
  35.5 9.5 %convolution_convert_fusion.q_ref = bf16[512,640]{1,0:T(8,128)(2,1)} fusion(bf16[512,5120]{1,0:T(8,128)(2,1)} %x_ref.1, bf16[5120,640]{1,0:T(8,128)(2,1)} %param.12), kind=kOutput, calls=%fused_computation | convolution fusion | flops 3355770880 | bytes 12451840 | tf_op jit(solution)/shard_map/dot_general | solution.py:268
  45.0 0.5 collective-permute-start.14
  45.7 0.5 collective-permute-start.4
  46.3 0.4 collective-permute-start.8
  46.7 0.6 fusion.17
  47.3 0.6 fusion.9.rows_ref
  48.3 0.4 copy-done.14
  49.1 8.8 %block_terms.5 = (bf16[128,2560]{1,0:T(8,128)(2,1)}, bf16[128,2560]{1,0:T(8,128)(2,1)}) custom-call(s32[1]{0:T(128)} %get-tuple-element.21.order_ref, s32[4,16]{1,0:T(4,128)} %fusion.9.rows_ref, bf16[512,640]{1,0:T(8,128)(2,1)} %convolution_convert_fusion.q_ref, bf16[640,5120]{1,0:T(8,128)(2,1)} %w_ref.5, bf16[512,256]{1,0:T(8,128)(2,1)} %kv_project.1.rest_0_, ...), custom_call_target="tpu_custom_call" | custom-call | flops 1048576 | bytes 1048576 | tf_op jit(solution)/shard_map/block_terms/pallas_call | solution.py:171
  57.9 0.9 collective-permute-start.19
  58.8 2.4 %collective-permute-start.15 = (bf16[128,2560]{1,0:T(8,128)(2,1)}, bf16[128,2560]{1,0:T(8,128)(2,1)S(1)}, u32[]{:S(2)}, u32[]{:S(2)}) collective-permute-start(bf16[128,2560]{1,0:T(8,128)(2,1)} %get-tuple-element.16), channel_id=1, source_target_pairs={{0,1},{1,2},{2,3},{3,0},{4,5},{5,6},{6,7},{7,4},{8,9},{9,10},{10,1... | collective-permute-start | bytes 1966088 | tf_op jit(solution)/shard_map/ppermute | solution.py:232
  61.2 0.6 slice.10.order_ref
  61.9 14.5 %block_terms.4 = (bf16[128,2560]{1,0:T(8,128)(2,1)}, bf16[128,2560]{1,0:T(8,128)(2,1)}, bf16[128,2560]{1,0:T(8,128)(2,1)}, bf16[128,2560]{1,0:T(8,128)(2,1)}) custom-call(s32[2]{0:T(128)} %slice.10.order_ref, s32[4,16]{1,0:T(4,128)} %fusion.9.rows_ref, bf16[512,640]{1,0:T(8,128)(2,1)} %convolution_convert_fusion.q_ref, bf16[640,5120]{1,0:T(8,128)(2,1)} %w_ref.5, ...), custom_call_target="tpu_custom_call" | custom-call | flops 1048576 | bytes 1048576 | tf_op jit(solution)/shard_map/block_terms/pallas_call | solution.py:171
  76.4 2.0 %collective-permute-start.18 = (bf16[128,2560]{1,0:T(8,128)(2,1)}, bf16[128,2560]{1,0:T(8,128)(2,1)S(1)}, u32[]{:S(2)}, u32[]{:S(2)}) collective-permute-start(bf16[128,2560]{1,0:T(8,128)(2,1)} %get-tuple-element.18), channel_id=1, source_target_pairs={{0,3},{1,0},{2,1},{3,2},{4,7},{5,4},{6,5},{7,6},{8,11},{9,8},{10,9... | collective-permute-start | bytes 1966088 | tf_op jit(solution)/shard_map/ppermute | solution.py:232
  78.5 1.2 %add.62 = bf16[128,2560]{1,0:T(8,128)(2,1)S(1)} add(bf16[128,2560]{1,0:T(8,128)(2,1)} %get-tuple-element.19, bf16[128,2560]{1,0:T(8,128)(2,1)S(1)} %collective-permute-done.19) | non-fusion elementwise | flops 327680 | bytes 1966080 | tf_op jit(solution)/shard_map/add | solution.py:285
  79.8 2.1 %add.61 = bf16[128,2560]{1,0:T(8,128)(2,1)} add(bf16[128,2560]{1,0:T(8,128)(2,1)} %get-tuple-element.15, bf16[128,2560]{1,0:T(8,128)(2,1)S(1)} %collective-permute-done.15) | non-fusion elementwise | flops 327680 | bytes 1966080 | tf_op jit(solution)/shard_map/add | solution.py:284
  81.9 3.2 %collective-permute-start.16 = (bf16[128,2560]{1,0:T(8,128)(2,1)}, bf16[128,2560]{1,0:T(8,128)(2,1)S(1)}, u32[]{:S(2)}, u32[]{:S(2)}) collective-permute-start(bf16[128,2560]{1,0:T(8,128)(2,1)} %add.61), channel_id=1, source_target_pairs={{0,1},{1,2},{2,3},{3,0},{4,5},{5,6},{6,7},{7,4},{8,9},{9,10},{10,1... | collective-permute-start | bytes 1966088 | tf_op jit(solution)/shard_map/ppermute | solution.py:232
  85.1 0.6 dynamic_slice.3.keep_ref
  85.7 9.0 %block_terms.3 = (bf16[128,2560]{1,0:T(8,128)(2,1)}, bf16[128,2560]{1,0:T(8,128)(2,1)}) custom-call(s32[1]{0:T(128)} %get-tuple-element.22.order_ref, s32[4,16]{1,0:T(4,128)} %fusion.9.rows_ref, bf16[512,640]{1,0:T(8,128)(2,1)} %convolution_convert_fusion.q_ref, bf16[640,5120]{1,0:T(8,128)(2,1)} %w_ref.5, bf16[512,256]{1,0:T(8,128)(2,1)} %kv_project.1.rest_0_, ...), custom_call_target="tpu_custom_call" | custom-call | flops 1048576 | bytes 1048576 | tf_op jit(solution)/shard_map/block_terms/pallas_call | solution.py:171
  94.8 0.8 collective-permute-done.18.v1_ref
  95.6 12.8 %collective-permute-done.20.v2_ref = bf16[128,2560]{1,0:T(8,128)(2,1)S(1)} collective-permute-done((bf16[128,2560]{1,0:T(8,128)(2,1)S(1)}, bf16[128,2560]{1,0:T(8,128)(2,1)S(1)}, u32[]{:S(2)}, u32[]{:S(2)}) %collective-permute-start.20) | collective-permute-done | bytes 655392 | tf_op jit(solution)/shard_map/ppermute | solution.py:232
  108.3 1.1 copy-done.1
  109.4 1.1 copy-done.2
  110.5 2.9 %final_norm.1 = bf16[128,5120]{1,0:T(8,128)(2,1)} custom-call(bf16[128,5120]{1,0:T(8,128)(2,1)S(1)} %copy-done, bf16[128,2560]{1,0:T(8,128)(2,1)S(1)} %copy-done.1, bf16[128,2560]{1,0:T(8,128)(2,1)S(1)} %copy-done.2, bf16[128,2560]{1,0:T(8,128)(2,1)S(1)} %collective-permute-done.16.u1_ref, bf16[128,2560]{1,0:T(8,128)(2,1)S(1)} %collective-permute-done.17.u2_ref, ...), custom_call_target="tpu_custom_call" | custom-call | tf_op jit(solution)/shard_map/final_norm/pallas_call | solution.py:217
  (67 shorter events, 1.4 us)
Async XLA Ops:
  5.6 39.4 %copy-start.21 = (s32[4]{0:T(128)S(1)}, s32[4]{0:T(128)}, u32[]{:S(2)}) copy-start(s32[4]{0:T(128)} %constant.95.clone) | copy-start | bytes 52
  5.6 41.7 %copy-start.19 = (s32[4,16]{1,0:T(4,128)S(1)}, s32[4,16]{1,0:T(4,128)}, u32[]{:S(2)}) copy-start(s32[4,16]{1,0:T(4,128)} %param.17) | copy-start | bytes 772
  5.6 9.5 %collective-permute-start.9 = (bf16[512,256]{1,0:T(8,128)(2,1)}, bf16[512,256]{1,0:T(8,128)(2,1)S(1)}, u32[]{:S(2)}, u32[]{:S(2)}) collective-permute-start(bf16[512,256]{1,0:T(8,128)(2,1)} %kv_project.1.rest_0_), channel_id=1, source_target_pairs={{0,8},{8,0},{16,24},{24,16},{32,40},{40,32},{48,56},{56,48},{1,9},... | collective-permute-start | bytes 786440 | tf_op jit(solution)/shard_map/ppermute | solution.py:240
  7.0 19.7 %collective-permute-start.11 = (bf16[512,256]{1,0:T(8,128)(2,1)}, bf16[512,256]{1,0:T(8,128)(2,1)S(1)}, u32[]{:S(2)}, u32[]{:S(2)}) collective-permute-start(bf16[512,256]{1,0:T(8,128)(2,1)} %kv_project.1.rest_0_), channel_id=1, source_target_pairs={{0,48},{8,56},{16,0},{24,8},{32,16},{40,24},{48,32},{56,40},{1,49}... | collective-permute-start | bytes 786440 | tf_op jit(solution)/shard_map/ppermute | solution.py:240
  7.1 27.7 %collective-permute-start.13 = (bf16[512,256]{1,0:T(8,128)(2,1)}, bf16[512,256]{1,0:T(8,128)(2,1)S(1)}, u32[]{:S(2)}, u32[]{:S(2)}) collective-permute-start(bf16[512,256]{1,0:T(8,128)(2,1)} %kv_project.1.rest_0_), channel_id=1, source_target_pairs={{0,16},{8,24},{16,32},{24,40},{32,48},{40,56},{48,0},{56,8},{1,17}... | collective-permute-start | bytes 786440 | tf_op jit(solution)/shard_map/ppermute | solution.py:240
  9.0 25.8 %collective-permute-start.1 = (bf16[512,256]{1,0:T(8,128)(2,1)}, bf16[512,256]{1,0:T(8,128)(2,1)S(1)}, u32[]{:S(2)}, u32[]{:S(2)}) collective-permute-start(bf16[512,256]{1,0:T(8,128)(2,1)} %kv_project.1.rest_0_), channel_id=1, source_target_pairs={{0,40},{8,32},{16,56},{24,48},{32,8},{40,0},{48,24},{56,16},{1,41}... | collective-permute-start | bytes 786440 | tf_op jit(solution)/shard_map/ppermute | solution.py:240
  10.9 24.5 %collective-permute-start.3 = (bf16[512,256]{1,0:T(8,128)(2,1)}, bf16[512,256]{1,0:T(8,128)(2,1)S(1)}, u32[]{:S(2)}, u32[]{:S(2)}) collective-permute-start(bf16[512,256]{1,0:T(8,128)(2,1)} %kv_project.1.rest_0_), channel_id=1, source_target_pairs={{0,32},{8,40},{16,48},{24,56},{32,0},{40,8},{48,16},{56,24},{1,33}... | collective-permute-start | bytes 786440 | tf_op jit(solution)/shard_map/ppermute | solution.py:240
  15.1 29.9 %copy-start.4 = (bf16[512,256]{1,0:T(8,128)(2,1)}, bf16[512,256]{1,0:T(8,128)(2,1)S(1)}, u32[]{:S(2)}) copy-start(bf16[512,256]{1,0:T(8,128)(2,1)S(1)} %collective-permute-done.9.rest_10_) | copy-start | bytes 786436
  15.1 29.9 %collective-permute-start.5 = (bf16[512,256]{1,0:T(8,128)(2,1)}, bf16[512,256]{1,0:T(8,128)(2,1)S(1)}, u32[]{:S(2)}, u32[]{:S(2)}) collective-permute-start(bf16[512,256]{1,0:T(8,128)(2,1)} %kv_project.1.rest_0_), channel_id=1, source_target_pairs={{0,56},{8,48},{16,8},{24,0},{32,24},{40,16},{48,40},{56,32},{1,57}... | collective-permute-start | bytes 786440 | tf_op jit(solution)/shard_map/ppermute | solution.py:240
  26.6 18.3 %copy-start.5 = (bf16[512,256]{1,0:T(8,128)(2,1)}, bf16[512,256]{1,0:T(8,128)(2,1)S(1)}, u32[]{:S(2)}) copy-start(bf16[512,256]{1,0:T(8,128)(2,1)S(1)} %collective-permute-done.11.rest_12_) | copy-start | bytes 786436
  26.6 18.9 %collective-permute-start.7 = (bf16[512,256]{1,0:T(8,128)(2,1)}, bf16[512,256]{1,0:T(8,128)(2,1)S(1)}, u32[]{:S(2)}, u32[]{:S(2)}) collective-permute-start(bf16[512,256]{1,0:T(8,128)(2,1)} %kv_project.1.rest_0_), channel_id=1, source_target_pairs={{0,24},{8,16},{16,40},{24,32},{32,56},{40,48},{48,8},{56,0},{1,25}... | collective-permute-start | bytes 786440 | tf_op jit(solution)/shard_map/ppermute | solution.py:240
  34.8 10.2 %copy-start.6 = (bf16[512,256]{1,0:T(8,128)(2,1)}, bf16[512,256]{1,0:T(8,128)(2,1)S(1)}, u32[]{:S(2)}) copy-start(bf16[512,256]{1,0:T(8,128)(2,1)S(1)} %collective-permute-done.13.rest_14_) | copy-start | bytes 786436
  34.8 10.9 %collective-permute-start = (bf16[512,256]{1,0:T(8,128)(2,1)}, bf16[512,256]{1,0:T(8,128)(2,1)S(1)}, u32[]{:S(2)}, u32[]{:S(2)}) collective-permute-start(bf16[512,256]{1,0:T(8,128)(2,1)} %kv_project.1.rest_0_), channel_id=1, source_target_pairs={{0,4},{4,0},{1,5},{5,1},{2,6},{6,2},{3,7},{7,3},{8,12},{12,8},{9,1... | collective-permute-start | bytes 786440 | tf_op jit(solution)/shard_map/ppermute | solution.py:232
  34.9 10.7 %copy-start.7 = (bf16[512,256]{1,0:T(8,128)(2,1)}, bf16[512,256]{1,0:T(8,128)(2,1)S(1)}, u32[]{:S(2)}) copy-start(bf16[512,256]{1,0:T(8,128)(2,1)S(1)} %collective-permute-done.1.rest_2_) | copy-start | bytes 786436
  34.9 11.3 %collective-permute-start.10 = (bf16[512,256]{1,0:T(8,128)(2,1)S(1)}, bf16[512,256]{1,0:T(8,128)(2,1)S(1)}, u32[]{:S(2)}, u32[]{:S(2)}) collective-permute-start(bf16[512,256]{1,0:T(8,128)(2,1)S(1)} %collective-permute-done.9.rest_10_), channel_id=1, source_target_pairs={{0,4},{4,0},{1,5},{5,1},{2,6},{6,2},{3,7},{7,3},{8,12},{12,8},{9,1... | collective-permute-start | bytes 786440 | tf_op jit(solution)/shard_map/ppermute | solution.py:232
  35.4 10.3 %copy-start.8 = (bf16[512,256]{1,0:T(8,128)(2,1)}, bf16[512,256]{1,0:T(8,128)(2,1)S(1)}, u32[]{:S(2)}) copy-start(bf16[512,256]{1,0:T(8,128)(2,1)S(1)} %collective-permute-done.3.rest_4_) | copy-start | bytes 786436
  35.4 10.9 %collective-permute-start.12 = (bf16[512,256]{1,0:T(8,128)(2,1)S(1)}, bf16[512,256]{1,0:T(8,128)(2,1)S(1)}, u32[]{:S(2)}, u32[]{:S(2)}) collective-permute-start(bf16[512,256]{1,0:T(8,128)(2,1)S(1)} %collective-permute-done.11.rest_12_), channel_id=1, source_target_pairs={{0,4},{4,0},{1,5},{5,1},{2,6},{6,2},{3,7},{7,3},{8,12},{12,8},{9,1... | collective-permute-start | bytes 786440 | tf_op jit(solution)/shard_map/ppermute | solution.py:232
  45.0 3.2 %copy-start.9 = (bf16[512,256]{1,0:T(8,128)(2,1)}, bf16[512,256]{1,0:T(8,128)(2,1)S(1)}, u32[]{:S(2)}) copy-start(bf16[512,256]{1,0:T(8,128)(2,1)S(1)} %collective-permute-done.5.rest_6_) | copy-start | bytes 786436
  45.0 2.9 %collective-permute-start.14 = (bf16[512,256]{1,0:T(8,128)(2,1)S(1)}, bf16[512,256]{1,0:T(8,128)(2,1)S(1)}, u32[]{:S(2)}, u32[]{:S(2)}) collective-permute-start(bf16[512,256]{1,0:T(8,128)(2,1)S(1)} %collective-permute-done.13.rest_14_), channel_id=1, source_target_pairs={{0,4},{4,0},{1,5},{5,1},{2,6},{6,2},{3,7},{7,3},{8,12},{12,8},{9,1... | collective-permute-start | bytes 786440 | tf_op jit(solution)/shard_map/ppermute | solution.py:232
  45.5 2.4 %collective-permute-start.2 = (bf16[512,256]{1,0:T(8,128)(2,1)S(1)}, bf16[512,256]{1,0:T(8,128)(2,1)S(1)}, u32[]{:S(2)}, u32[]{:S(2)}) collective-permute-start(bf16[512,256]{1,0:T(8,128)(2,1)S(1)} %collective-permute-done.1.rest_2_), channel_id=1, source_target_pairs={{0,4},{4,0},{1,5},{5,1},{2,6},{6,2},{3,7},{7,3},{8,12},{12,8},{9,1... | collective-permute-start | bytes 786440 | tf_op jit(solution)/shard_map/ppermute | solution.py:232
  45.7 2.3 %collective-permute-start.4 = (bf16[512,256]{1,0:T(8,128)(2,1)S(1)}, bf16[512,256]{1,0:T(8,128)(2,1)S(1)}, u32[]{:S(2)}, u32[]{:S(2)}) collective-permute-start(bf16[512,256]{1,0:T(8,128)(2,1)S(1)} %collective-permute-done.3.rest_4_), channel_id=1, source_target_pairs={{0,4},{4,0},{1,5},{5,1},{2,6},{6,2},{3,7},{7,3},{8,12},{12,8},{9,1... | collective-permute-start | bytes 786440 | tf_op jit(solution)/shard_map/ppermute | solution.py:232
  46.2 1.8 %collective-permute-start.6 = (bf16[512,256]{1,0:T(8,128)(2,1)S(1)}, bf16[512,256]{1,0:T(8,128)(2,1)S(1)}, u32[]{:S(2)}, u32[]{:S(2)}) collective-permute-start(bf16[512,256]{1,0:T(8,128)(2,1)S(1)} %collective-permute-done.5.rest_6_), channel_id=1, source_target_pairs={{0,4},{4,0},{1,5},{5,1},{2,6},{6,2},{3,7},{7,3},{8,12},{12,8},{9,1... | collective-permute-start | bytes 786440 | tf_op jit(solution)/shard_map/ppermute | solution.py:232
  46.3 1.9 %collective-permute-start.8 = (bf16[512,256]{1,0:T(8,128)(2,1)S(1)}, bf16[512,256]{1,0:T(8,128)(2,1)S(1)}, u32[]{:S(2)}, u32[]{:S(2)}) collective-permute-start(bf16[512,256]{1,0:T(8,128)(2,1)S(1)} %collective-permute-done.7.rest_8_), channel_id=1, source_target_pairs={{0,4},{4,0},{1,5},{5,1},{2,6},{6,2},{3,7},{7,3},{8,12},{12,8},{9,1... | collective-permute-start | bytes 786440 | tf_op jit(solution)/shard_map/ppermute | solution.py:232
  57.9 20.5 %collective-permute-start.19 = (bf16[128,2560]{1,0:T(8,128)(2,1)}, bf16[128,2560]{1,0:T(8,128)(2,1)S(1)}, u32[]{:S(2)}, u32[]{:S(2)}) collective-permute-start(bf16[128,2560]{1,0:T(8,128)(2,1)} %get-tuple-element.20), channel_id=1, source_target_pairs={{0,3},{1,0},{2,1},{3,2},{4,7},{5,4},{6,5},{7,6},{8,11},{9,8},{10,9... | collective-permute-start | bytes 1966088 | tf_op jit(solution)/shard_map/ppermute | solution.py:232
  58.8 20.9 %collective-permute-start.15 = (bf16[128,2560]{1,0:T(8,128)(2,1)}, bf16[128,2560]{1,0:T(8,128)(2,1)S(1)}, u32[]{:S(2)}, u32[]{:S(2)}) collective-permute-start(bf16[128,2560]{1,0:T(8,128)(2,1)} %get-tuple-element.16), channel_id=1, source_target_pairs={{0,1},{1,2},{2,3},{3,0},{4,5},{5,6},{6,7},{7,4},{8,9},{9,10},{10,1... | collective-permute-start | bytes 1966088 | tf_op jit(solution)/shard_map/ppermute | solution.py:232
  61.9 23.2 %copy-start.20 = (s32[4]{0:T(128)S(1)}, s32[4]{0:T(128)}, u32[]{:S(2)}) copy-start(s32[4]{0:T(128)} %param.18) | copy-start | bytes 52
  76.4 18.4 %collective-permute-start.17 = (bf16[128,2560]{1,0:T(8,128)(2,1)}, bf16[128,2560]{1,0:T(8,128)(2,1)S(1)}, u32[]{:S(2)}, u32[]{:S(2)}) collective-permute-start(bf16[128,2560]{1,0:T(8,128)(2,1)} %get-tuple-element.17), channel_id=1, source_target_pairs={{0,1},{1,2},{2,3},{3,0},{4,5},{5,6},{6,7},{7,4},{8,9},{9,10},{10,1... | collective-permute-start | bytes 1966088 | tf_op jit(solution)/shard_map/ppermute | solution.py:232
  76.4 19.1 %collective-permute-start.18 = (bf16[128,2560]{1,0:T(8,128)(2,1)}, bf16[128,2560]{1,0:T(8,128)(2,1)S(1)}, u32[]{:S(2)}, u32[]{:S(2)}) collective-permute-start(bf16[128,2560]{1,0:T(8,128)(2,1)} %get-tuple-element.18), channel_id=1, source_target_pairs={{0,3},{1,0},{2,1},{3,2},{4,7},{5,4},{6,5},{7,6},{8,11},{9,8},{10,9... | collective-permute-start | bytes 1966088 | tf_op jit(solution)/shard_map/ppermute | solution.py:232
  79.7 28.6 %collective-permute-start.20 = (bf16[128,2560]{1,0:T(8,128)(2,1)S(1)}, bf16[128,2560]{1,0:T(8,128)(2,1)S(1)}, u32[]{:S(2)}, u32[]{:S(2)}) collective-permute-start(bf16[128,2560]{1,0:T(8,128)(2,1)S(1)} %add.62), channel_id=1, source_target_pairs={{0,3},{1,0},{2,1},{3,2},{4,7},{5,4},{6,5},{7,6},{8,11},{9,8},{10,9... | collective-permute-start | bytes 1966088 | tf_op jit(solution)/shard_map/ppermute | solution.py:232
  81.9 26.5 %collective-permute-start.16 = (bf16[128,2560]{1,0:T(8,128)(2,1)}, bf16[128,2560]{1,0:T(8,128)(2,1)S(1)}, u32[]{:S(2)}, u32[]{:S(2)}) collective-permute-start(bf16[128,2560]{1,0:T(8,128)(2,1)} %add.61), channel_id=1, source_target_pairs={{0,1},{1,2},{2,3},{3,0},{4,5},{5,6},{6,7},{7,4},{8,9},{9,10},{10,1... | collective-permute-start | bytes 1966088 | tf_op jit(solution)/shard_map/ppermute | solution.py:232
  85.7 22.6 %copy-start = (bf16[128,5120]{1,0:T(8,128)(2,1)S(1)}, bf16[128,5120]{1,0:T(8,128)(2,1)}, u32[]{:S(2)}) copy-start(bf16[128,5120]{1,0:T(8,128)(2,1)} %res_ref.1) | copy-start | bytes 3932164
  85.7 22.6 %copy-start.3 = (f32[5120]{0:T(1024)S(1)}, f32[5120]{0:T(1024)}, u32[]{:S(2)}) copy-start(f32[5120]{0:T(1024)} %param.16) | copy-start | bytes 61444
  (11 other events, 15.7 us)

commit v5 on v4

v5 whole, which is shorter than its diff:
```python
import functools
import math

import jax
import jax.numpy as jnp
from jax import lax
from jax.experimental import pallas as pl
from jax.experimental.pallas import tpu as pltpu
from jax.sharding import Mesh, PartitionSpec as P

HD = 128
BLK = 128
CHUNK = 4
CTX = ("z", "y", "core")
F32 = jnp.float32
BF16 = jnp.bfloat16
SCALE2 = math.log2(math.e) / math.sqrt(HD)
SPLIT = ((0, 3), (3, 5))
KERNEL_VMEM = 36 << 20
SMALL_COST = pl.CostEstimate(flops=1 << 20, bytes_accessed=1 << 20, transcendentals=0)
NT = (((1,), (1,)), ((), ()))


def kv_kernel(x_ref, wk_ref, wv_ref, o_ref, xbuf, wbuf, sems):
    parts, tile, _ = wbuf.shape
    copies = []
    for k in range(parts):
        cut = pl.ds(k * tile, tile)
        group = [
            pltpu.make_async_copy(x_ref.at[:, cut], xbuf.at[:, cut], sems.at[0, k]),
            pltpu.make_async_copy(wk_ref.at[cut], wbuf.at[k, :, pl.ds(0, HD)], sems.at[1, k]),
            pltpu.make_async_copy(wv_ref.at[cut], wbuf.at[k, :, pl.ds(HD, HD)], sems.at[2, k]),
        ]
        for copy in group:
            copy.start()
        copies.append(group)
    total = None
    for k in range(parts):
        for copy in copies[k]:
            copy.wait()
        part = jnp.dot(
            xbuf[:, k * tile:(k + 1) * tile], wbuf[k], preferred_element_type=F32
        )
        total = part if total is None else total + part
    o_ref[...] = total.astype(BF16)


def kv_project(x, wk, wv):
    rows, depth = x.shape
    parts = 10
    hbm = pl.BlockSpec(memory_space=pltpu.HBM)
    vmem = pl.BlockSpec(memory_space=pltpu.VMEM)
    return pl.pallas_call(
        kv_kernel,
        name="kv_project",
        out_shape=[
            jax.ShapeDtypeStruct((rows, 2 * HD), BF16),
            jax.ShapeDtypeStruct((rows, depth), BF16),
        ],
        in_specs=[hbm] * 3,
        out_specs=[vmem] * 2,
        scratch_shapes=[
            pltpu.VMEM((parts, depth // parts, 2 * HD), BF16),
            pltpu.SemaphoreType.DMA((3, parts)),
        ],
        compiler_params=pltpu.CompilerParams(vmem_limit_bytes=52 << 20),
        cost_estimate=SMALL_COST,
    )(x, wk, wv)


def q_kernel(x_ref, w_ref, o_ref, wbuf, sems):
    parts, tile, _ = wbuf.shape
    copies = [
        pltpu.make_async_copy(w_ref.at[pl.ds(k * tile, tile)], wbuf.at[k], sems.at[k])
        for k in range(parts)
    ]
    for copy in copies:
        copy.start()
    total = None
    for k in range(parts):
        copies[k].wait()
        part = jnp.dot(x_ref[:, k * tile:(k + 1) * tile], wbuf[k], preferred_element_type=F32)
        total = part if total is None else total + part
    o_ref[...] = total.astype(BF16)


def q_project(x, w):
    parts = 5
    vmem = pl.BlockSpec(memory_space=pltpu.VMEM)
    return pl.pallas_call(
        q_kernel,
        name="q_project",
        out_shape=jax.ShapeDtypeStruct((x.shape[0], w.shape[1]), BF16),
        in_specs=[vmem, pl.BlockSpec(memory_space=pltpu.HBM)],
        out_specs=vmem,
        scratch_shapes=[
            pltpu.VMEM((parts, w.shape[0] // parts, w.shape[1]), BF16),
            pltpu.SemaphoreType.DMA((parts,)),
        ],
        compiler_params=pltpu.CompilerParams(vmem_limit_bytes=40 << 20),
        cost_estimate=SMALL_COST,
    )(x, w)


def collect_kernel(places, based, *refs):
    pieces, out, sems = refs[based:-2], refs[-2], refs[-1]
    copies = [
        pltpu.make_async_copy(piece, out.at[pl.ds(spot, piece.shape[0])], sems.at[k])
        for k, (piece, spot) in enumerate(zip(pieces, places))
    ]
    for copy in copies:
        copy.start()
    for copy in copies:
        copy.wait()


def collect(parts, shape, base=None):
    pieces, places = zip(*parts)
    based = 0 if base is None else 1
    return pl.pallas_call(
        functools.partial(collect_kernel, places, based),
        name="collect",
        out_shape=jax.ShapeDtypeStruct(shape, BF16),
        in_specs=[pl.BlockSpec(memory_space=pl.ANY)] * (based + len(pieces)),
        out_specs=pl.BlockSpec(memory_space=pl.ANY),
        scratch_shapes=[pltpu.SemaphoreType.DMA((len(pieces),))],
        input_output_aliases={0: 0} if based else {},
        compiler_params=pltpu.CompilerParams(vmem_limit_bytes=8 << 20),
        cost_estimate=SMALL_COST,
    )(*([base] if based else []), *pieces)


def attend(q, kv_ref, own_row, rows, count):
    slots = len(rows)
    take = [kv_ref[pl.ds(pl.multiple_of(r, BLK), BLK), :] for r in rows]
    own = kv_ref[pl.ds(pl.multiple_of(own_row, BLK), BLK), :]
    groups = [take[c:c + CHUNK] for c in range(0, slots, CHUNK)]
    keys = [jnp.concatenate([x[:, :HD] for x in g], axis=0) for g in groups]
    values = [jnp.concatenate([x[:, HD:] for x in g], axis=0) for g in groups]
    results = []
    for lo, hi in SPLIT:
        part = q[lo * BLK:hi * BLK]
        s = lax.dot_general(part, own[:, :HD], NT, preferred_element_type=F32)
        row = lax.broadcasted_iota(jnp.int32, s.shape, 0) % BLK
        col = lax.broadcasted_iota(jnp.int32, s.shape, 1)
        pieces = [jnp.where(col <= row, s, -jnp.inf)]
        for c, key in enumerate(keys):
            s = lax.dot_general(part, key, NT, preferred_element_type=F32)
            for j in range(CHUNK):
                pieces.append(
                    jnp.where(c * CHUNK + j < count, s[:, j * BLK:(j + 1) * BLK], -jnp.inf)
                )
        top = pieces[0]
        for piece in pieces[1:]:
            top = jnp.maximum(top, piece)
        top = jnp.max(top, axis=1, keepdims=True)
        weights = [jnp.exp2((piece - top) * SCALE2) for piece in pieces]
        total = weights[0]
        for w in weights[1:]:
            total = total + w
        out = jnp.dot(weights[0].astype(BF16), own[:, HD:], preferred_element_type=F32)
        for c, value in enumerate(values):
            w = jnp.concatenate(
                [x.astype(BF16) for x in weights[1 + c * CHUNK:1 + (c + 1) * CHUNK]], axis=1
            )
            out = out + jnp.dot(w, value, preferred_element_type=F32)
        out = (out / jnp.sum(total, axis=1, keepdims=True)).astype(BF16)
        results += [out[h * BLK:(h + 1) * BLK] for h in range(hi - lo)]
    return jnp.concatenate(results, axis=1)


def block_kernel(order_ref, rows_ref, q_ref, kv_ref, w_ref, *rest):
    res_ref, outs = (rest[0], rest[1:]) if len(rest) % 2 else (None, rest)
    step = pl.program_id(0)
    local = order_ref[step]
    slots = rows_ref.shape[1]
    rows, count = [], jnp.int32(0)
    for l in range(slots):
        entry = rows_ref[local, l]
        count += jnp.where(entry >= 0, 1, 0).astype(jnp.int32)
        rows.append(jnp.maximum(entry, 0))
    q_all = q_ref[...]
    heads = q_all.shape[1] // HD
    q = jnp.concatenate([q_all[:, h * HD:(h + 1) * HD] for h in range(heads)], axis=0)
    head_out = attend(q, kv_ref, local * BLK, rows, count)
    half = outs[0].shape[1]
    tile = half // 2
    for side in range(2):
        for c in range(0, half, tile):
            cut = slice(side * half + c, side * half + c + tile)
            part = jnp.dot(head_out, w_ref[:, cut], preferred_element_type=F32).astype(BF16)
            if res_ref is not None:
                part = part.astype(F32) + res_ref[:, cut].astype(F32)
            for k in range(len(outs) // 2):
                @pl.when(step == k)
                def _():
                    outs[2 * k + side][:, c:c + tile] = part


def block_terms(order, rows, q, kv, w_out, residual=None):
    count = order.shape[0]
    width = q.shape[1]
    cols = w_out.shape[1]
    vmem = pl.BlockSpec(memory_space=pltpu.VMEM)
    extra = [] if residual is None else [residual]
    kind = BF16 if residual is None else F32
    outs = pl.pallas_call(
        block_kernel,
        name="block_terms",
        out_shape=[jax.ShapeDtypeStruct((BLK, cols // 2), kind)] * (2 * count),
        grid_spec=pltpu.PrefetchScalarGridSpec(
            num_scalar_prefetch=2,
            grid=(count,),
            in_specs=[pl.BlockSpec((BLK, width), lambda i, order, rows: (order[i], 0)), vmem, vmem]
            + [vmem] * len(extra),
            out_specs=[vmem] * (2 * count),
        ),
        compiler_params=pltpu.CompilerParams(vmem_limit_bytes=KERNEL_VMEM),
        cost_estimate=SMALL_COST,
    )(order, rows, q, kv, w_out, *extra)
    return [(outs[2 * k], outs[2 * k + 1]) for k in range(count)]


def norm_kernel(b1_ref, b2_ref, u1_ref, u2_ref, v1_ref, v2_ref, gain_ref, keep_ref, o_ref):
    half = u1_ref.shape[1]
    total = [
        b[...] + u[...].astype(F32) + v[...].astype(F32)
        for b, u, v in ((b1_ref, u1_ref, v1_ref), (b2_ref, u2_ref, v2_ref))
    ]
    square = sum(jnp.sum(x * x, axis=1, keepdims=True) for x in total)
    factor = lax.rsqrt(square * (1.0 / (2 * half)) + 1e-06) * keep_ref[0].astype(F32)
    for lo, x in zip((0, half), total):
        o_ref[:, lo:lo + half] = (x * factor * gain_ref[:, lo:lo + half]).astype(BF16)


def final_norm(base, u, v, gain, keep):
    rows, half = base[0].shape
    vm = pl.BlockSpec(memory_space=pltpu.VMEM)
    return pl.pallas_call(
        norm_kernel,
        name="final_norm",
        out_shape=jax.ShapeDtypeStruct((rows, 2 * half), BF16),
        in_specs=[vm] * 7 + [pl.BlockSpec(memory_space=pltpu.SMEM)],
        out_specs=vm,
        compiler_params=pltpu.CompilerParams(vmem_limit_bytes=30 << 20),
    )(*base, *u, *v, gain[None, :], keep)


def ring(n, s):
    return [(i, (i + s) % n) for i in range(n)]


def shift(x, axis, s):
    return lax.ppermute(x, axis, ring({"y": 2, "core": 2, "z": 4, "tp": 4}[axis], s))


def gather_blocks(own, beside):
    rows = own.shape[0]
    shape = (16 * rows, own.shape[1])

    def fetch(x, dz, dy):
        pairs = [(i, ((i // 2 - dz) % 4) * 2 + (i + dy) % 2) for i in range(8)]
        return lax.ppermute(x, ("z", "y"), pairs)

    def both(dz, dy, piece):
        spot = (dz * 4 + dy * 2) * rows
        return [(piece, spot), (shift(piece, "core", 1), spot + rows)]

    places = ((2, 1), (2, 0), (1, 1), (3, 1), (0, 1), (1, 0), (3, 0))
    pieces = [fetch(own, *p) for p in places[:5]]
    extra = beside()
    pieces, own, extra = lax.optimization_barrier((pieces, own, extra))
    late = [fetch(own, *p) for p in places[5:]]
    early = both(0, 0, own)
    for p, piece in zip(places[:5], pieces):
        early += both(*p, piece)
    base = collect(early, shape)
    last = []
    for p, piece in zip(places[5:], late):
        last += both(*p, piece)
    return collect(last, shape, base), extra


def block_rows(ancestors):
    per = ancestors.shape[0]
    owner = ancestors // per
    dz = (owner // 4 - lax.axis_index("z")) % 4
    dy = (owner // 2 - lax.axis_index("y")) % 2
    dc = (owner - lax.axis_index("core")) % 2
    row = ((dz * 4 + dy * 2 + dc) * per + ancestors % per) * BLK
    return jnp.where(ancestors >= 0, row, -1).astype(jnp.int32)


def on_device(activations, residual, w_query, w_key, w_value, w_out, gain, ancestors, kept):
    kv_own, held = kv_project(activations, w_key, w_value)
    kv, (queries, w_held) = gather_blocks(
        kv_own, lambda: (q_project(held, w_query), collect([(w_out, 0)], w_out.shape))
    )
    rows = block_rows(ancestors)
    t = lax.axis_index("tp").astype(jnp.int32)
    order = (t + jnp.array([2, 1, 3, 0], jnp.int32)) % 4

    def send(x, s):
        return shift(x, "tp", s % 4)

    ((lo2, hi2),) = block_terms(order[:1], rows, queries, kv, w_held)
    a = send(lo2, 1)
    b = send(hi2, 3)
    (lo1, hi1), (lo3, hi3) = block_terms(order[1:3], rows, queries, kv, w_held)
    u2 = send(hi1, 1)
    v1 = send(lo3, 3)
    (base,) = block_terms(order[3:], rows, queries, kv, w_held, residual)
    u1 = send(lo1 + a, 1)
    v2 = send(hi3 + b, 3)
    keep = lax.dynamic_slice_in_dim(kept, t, 1, 0)
    return final_norm(base, (u1, u2), (v1, v2), gain, keep)


def solution(mesh):
    fine = Mesh(mesh.devices.reshape(2, 4, 2, 2, 4), ("dp", "z", "y", "core", "tp"))
    ctx = ("dp",) + CTX
    in_specs = (
        P(ctx, None),
        P(ctx + ("tp",), None),
        P(None, "tp"),
        P(None, "tp"),
        P(None, "tp"),
        P("tp", None),
        P(),
        P(ctx, None),
        P(ctx),
    )
    out_specs = P(ctx + ("tp",), None)
    return jax.shard_map(
        on_device, mesh=fine, in_specs=in_specs, out_specs=out_specs, check_vma=False
    )
```

time: 114 us -> 110 us (0.965)
  the two profiles are of different devices: /device:TPU:86 before, /device:TPU:24 now
where the time goes in v5:
time: 110 us
  Pallas kernels  40.4 us (37%)
  waiting for transfers between devices  33.8 us (31%)
  starting transfers between devices  22.3 us (20%)
  local copies, waits for them, and re-layouts  11.4 us (10%)
  other arithmetic  2.06 us (2%)
    pallas_call x3, Pallas kernels, block_terms(): pl.pallas_call(block_kernel, name='block_terms', out_shape=[jax.ShapeDtyp...  19.8 us
    ppermute x7, waiting for transfers between devices, fetch(): return lax.ppermute(x, ('z', 'y'), pairs)  17.2 us
    ppermute x14, waiting for transfers between devices, shift(): lax.ppermute(x, axis, ring({'y': 2, 'core': 2, 'z': 4, 'tp': 4}[axis], s))  16.5 us
    ppermute x7, starting transfers between devices, fetch(): return lax.ppermute(x, ('z', 'y'), pairs)  11.3 us
    ppermute x14, starting transfers between devices, shift(): lax.ppermute(x, axis, ring({'y': 2, 'core': 2, 'z': 4, 'tp': 4}[axis], s))  11 us
    unnamed x32, local copies, waits for them, and re-layouts  10.1 us
    pallas_call x1, Pallas kernels, kv_project(): pl.pallas_call(kv_kernel, name='kv_project', out_shape=[jax.ShapeDtypeStr...  6.92 us
    pallas_call x1, Pallas kernels, q_project(): pl.pallas_call(q_kernel, name='q_project', out_shape=jax.ShapeDtypeStruct...  6.6 us
  transfers between devices with their start and end apart: 21, of which 8 were waited for; matrix products, arithmetic and copies ran while one was open for 3% of the time, Pallas kernels for 21%

profile of v5, /device:TPU:24, one launch (start us, length us, event | category | flops | bytes accessed | tf_op | source)
XLA Modules:
  0.0 110.2 jit_solution(14037178361313218299)
XLA Ops:
  0.0 1.5 %copy-done.6 = bf16[5120,128]{1,0:T(8,128)(2,1)S(1)} copy-done((bf16[5120,128]{1,0:T(8,128)(2,1)S(1)}, bf16[5120,128]{1,0:T(8,128)(2,1)}, u32[]{:S(2)}) %copy-start.6) | copy-done | bytes 1310744
  1.5 6.9 %kv_project.1 = (bf16[512,256]{1,0:T(8,128)(2,1)S(1)}, bf16[512,5120]{1,0:T(8,128)(2,1)}) custom-call(bf16[512,5120]{1,0:T(8,128)(2,1)} %x_ref.1, bf16[5120,128]{1,0:T(8,128)(2,1)S(1)} %copy-done.6, bf16[5120,128]{1,0:T(8,128)(2,1)} %wv_ref.1), custom_call_target="tpu_custom_call" | custom-call | flops 1048576 | bytes 1048576 | tf_op jit(solution)/shard_map/kv_project/pallas_call | solution.py:53
  8.4 4.1 %collective-permute-start = (bf16[512,256]{1,0:T(8,128)(2,1)S(1)}, bf16[512,256]{1,0:T(8,128)(2,1)S(1)}, u32[]{:S(2)}, u32[]{:S(2)}) collective-permute-start(bf16[512,256]{1,0:T(8,128)(2,1)S(1)} %get-tuple-element.26.refs_0_), channel_id=1, source_target_pairs={{0,40},{8,32},{16,56},{24,48},{32,8},{40,0},{48,24},{56,16},{1,41}... | collective-permute-start | bytes 786440 | tf_op jit(solution)/shard_map/ppermute | solution.py:263
  12.6 4.4 %collective-permute-start.2 = (bf16[512,256]{1,0:T(8,128)(2,1)S(1)}, bf16[512,256]{1,0:T(8,128)(2,1)S(1)}, u32[]{:S(2)}, u32[]{:S(2)}) collective-permute-start(bf16[512,256]{1,0:T(8,128)(2,1)S(1)} %get-tuple-element.26.refs_0_), channel_id=1, source_target_pairs={{0,56},{8,48},{16,8},{24,0},{32,24},{40,16},{48,40},{56,32},{1,57}... | collective-permute-start | bytes 786440 | tf_op jit(solution)/shard_map/ppermute | solution.py:263
  17.0 0.7 collective-permute-start.4
  18.2 2.7 %copy-done = bf16[640,5120]{1,0:T(8,128)(2,1)} copy-done((bf16[640,5120]{1,0:T(8,128)(2,1)}, bf16[640,5120]{1,0:T(8,128)(2,1)S(1)}, u32[]{:S(2)}) %copy-start) | copy-done | bytes 6553624
  21.0 6.6 %q_project.1.q_ref = bf16[512,640]{1,0:T(8,128)(2,1)S(1)} custom-call(bf16[512,5120]{1,0:T(8,128)(2,1)S(1)} %copy-done.5, bf16[5120,640]{1,0:T(8,128)(2,1)S(1)} %bitcast.4), custom_call_target="tpu_custom_call" | custom-call | flops 1048576 | bytes 1048576 | tf_op jit(solution)/shard_map/q_project/pallas_call | solution.py:90
  27.6 5.3 %collective-permute-done.3.refs_8_ = bf16[512,256]{1,0:T(8,128)(2,1)S(1)} collective-permute-done((bf16[512,256]{1,0:T(8,128)(2,1)S(1)}, bf16[512,256]{1,0:T(8,128)(2,1)S(1)}, u32[]{:S(2)}, u32[]{:S(2)}) %collective-permute-start.3) | collective-permute-done | bytes 262176 | tf_op jit(solution)/shard_map/ppermute | solution.py:263
  32.9 4.3 %collective-permute-done.4.refs_10_ = bf16[512,256]{1,0:T(8,128)(2,1)S(1)} collective-permute-done((bf16[512,256]{1,0:T(8,128)(2,1)S(1)}, bf16[512,256]{1,0:T(8,128)(2,1)S(1)}, u32[]{:S(2)}, u32[]{:S(2)}) %collective-permute-start.4) | collective-permute-done | bytes 262176 | tf_op jit(solution)/shard_map/ppermute | solution.py:263
  37.7 0.7 collective-permute-start.11
  38.5 1.3 %collective-permute-start.13 = (bf16[512,256]{1,0:T(8,128)(2,1)S(1)}, bf16[512,256]{1,0:T(8,128)(2,1)S(1)}, u32[]{:S(2)}, u32[]{:S(2)}) collective-permute-start(bf16[512,256]{1,0:T(8,128)(2,1)S(1)} %get-tuple-element.26.refs_0_), channel_id=1, source_target_pairs={{0,16},{8,24},{16,32},{24,40},{32,48},{40,56},{48,0},{56,8},{1,17}... | collective-permute-start | bytes 786440 | tf_op jit(solution)/shard_map/ppermute | solution.py:263
  40.5 6.0 %collective-permute-done.11.refs_1_ = bf16[512,256]{1,0:T(8,128)(2,1)S(1)} collective-permute-done((bf16[512,256]{1,0:T(8,128)(2,1)S(1)}, bf16[512,256]{1,0:T(8,128)(2,1)S(1)}, u32[]{:S(2)}, u32[]{:S(2)}) %collective-permute-start.11) | collective-permute-done | bytes 262176 | tf_op jit(solution)/shard_map/ppermute | solution.py:263
  46.5 1.6 %collective-permute-done.13.refs_3_ = bf16[512,256]{1,0:T(8,128)(2,1)S(1)} collective-permute-done((bf16[512,256]{1,0:T(8,128)(2,1)S(1)}, bf16[512,256]{1,0:T(8,128)(2,1)S(1)}, u32[]{:S(2)}, u32[]{:S(2)}) %collective-permute-start.13) | collective-permute-done | bytes 262176 | tf_op jit(solution)/shard_map/ppermute | solution.py:263
  48.8 1.5 %collect.4.refs_0_ = bf16[8192,256]{1,0:T(8,128)(2,1)S(1)} custom-call(bf16[512,256]{1,0:T(8,128)(2,1)S(1)} %get-tuple-element.26.refs_0_, bf16[512,256]{1,0:T(8,128)(2,1)S(1)} %collective-permute-done.5.refs_1_, bf16[512,256]{1,0:T(8,128)(2,1)S(1)} %collective-permute-done.refs_2_, bf16[512,256]{1,0:T(8,128)(2,1)S(1)} %collective-permute-done.6.refs_3_, ...), custom_call_target="tpu_custom_call" | custom-call | flops 1048576 | bytes 1048576 | tf_op jit(solution)/shard_map/collect/pallas_call | solution.py:120
  50.3 1.2 %collect.5.kv_ref = bf16[8192,256]{1,0:T(8,128)(2,1)S(1)} custom-call(bf16[8192,256]{1,0:T(8,128)(2,1)S(1)} %collect.4.refs_0_, bf16[512,256]{1,0:T(8,128)(2,1)S(1)} %collective-permute-done.11.refs_1_, bf16[512,256]{1,0:T(8,128)(2,1)} %collective-permute-done.12.refs_2_, ...), custom_call_target="tpu_custom_call", output_to_operand_aliasing={{}: (0, {})} | custom-call | flops 1048576 | bytes 1048576 | tf_op jit(solution)/shard_map/collect/pallas_call | solution.py:120
  51.6 0.8 slice-done.1
  52.4 4.7 %block_terms.5 = (bf16[128,2560]{1,0:T(8,128)(2,1)S(1)}, bf16[128,2560]{1,0:T(8,128)(2,1)S(1)}) custom-call(s32[1]{0:T(128)} %get-tuple-element.41.order_ref, s32[4,16]{1,0:T(4,128)S(1)} %fusion.9.rows_ref, bf16[512,640]{1,0:T(8,128)(2,1)S(1)} %q_project.1.q_ref, bf16[8192,256]{1,0:T(8,128)(2,1)S(1)} %collect.5.kv_ref, bf16[640,5120]{1,0:T(8,128)(2,1)S(1)} %bitcast.2), custom_call_target="tpu_custom_call" | custom-call | flops 1048576 | bytes 1048576 | tf_op jit(solution)/shard_map/block_terms/pallas_call | solution.py:207
  57.1 2.8 %collective-permute-start.19 = (bf16[128,2560]{1,0:T(8,128)(2,1)S(1)}, bf16[128,2560]{1,0:T(8,128)(2,1)S(1)}, u32[]{:S(2)}, u32[]{:S(2)}) collective-permute-start(bf16[128,2560]{1,0:T(8,128)(2,1)S(1)} %get-tuple-element.40), channel_id=1, source_target_pairs={{0,3},{1,0},{2,1},{3,2},{4,7},{5,4},{6,5},{7,6},{8,11},{9,8},{10,9... | collective-permute-start | bytes 1966088 | tf_op jit(solution)/shard_map/ppermute | solution.py:254
  60.0 10.3 %block_terms.4 = (bf16[128,2560]{1,0:T(8,128)(2,1)S(1)}, bf16[128,2560]{1,0:T(8,128)(2,1)}, bf16[128,2560]{1,0:T(8,128)(2,1)}, bf16[128,2560]{1,0:T(8,128)(2,1)S(1)}) custom-call(s32[2]{0:T(128)S(1)} %slice.10.order_ref, s32[4,16]{1,0:T(4,128)S(1)} %fusion.9.rows_ref, bf16[512,640]{1,0:T(8,128)(2,1)S(1)} %q_project.1.q_ref, ...), custom_call_target="tpu_custom_call" | custom-call | flops 1048576 | bytes 1048576 | tf_op jit(solution)/shard_map/block_terms/pallas_call | solution.py:207
  70.3 0.8 collective-permute-start.17
  71.1 2.5 %collective-permute-start.18 = (bf16[128,2560]{1,0:T(8,128)(2,1)}, bf16[128,2560]{1,0:T(8,128)(2,1)S(1)}, u32[]{:S(2)}, u32[]{:S(2)}) collective-permute-start(bf16[128,2560]{1,0:T(8,128)(2,1)} %get-tuple-element.38), channel_id=1, source_target_pairs={{0,3},{1,0},{2,1},{3,2},{4,7},{5,4},{6,5},{7,6},{8,11},{9,8},{10,9... | collective-permute-start | bytes 1966088 | tf_op jit(solution)/shard_map/ppermute | solution.py:254
  73.6 1.4 %collective-permute-done.19 = bf16[128,2560]{1,0:T(8,128)(2,1)S(1)} collective-permute-done((bf16[128,2560]{1,0:T(8,128)(2,1)S(1)}, bf16[128,2560]{1,0:T(8,128)(2,1)S(1)}, u32[]{:S(2)}, u32[]{:S(2)}) %collective-permute-start.19) | collective-permute-done | bytes 655392 | tf_op jit(solution)/shard_map/ppermute | solution.py:254
  75.0 1.0 add.62
  76.0 3.7 %collective-permute-start.20 = (bf16[128,2560]{1,0:T(8,128)(2,1)}, bf16[128,2560]{1,0:T(8,128)(2,1)}, u32[]{:S(2)}, u32[]{:S(2)}) collective-permute-start(bf16[128,2560]{1,0:T(8,128)(2,1)} %add.62), channel_id=1, source_target_pairs={{0,3},{1,0},{2,1},{3,2},{4,7},{5,4},{6,5},{7,6},{8,11},{9,8},{10,9... | collective-permute-start | bytes 1966088 | tf_op jit(solution)/shard_map/ppermute | solution.py:254
  79.7 1.0 add.61
  81.3 2.9 %copy-done.1 = bf16[640,5120]{1,0:T(8,128)(2,1)S(1)} copy-done((bf16[640,5120]{1,0:T(8,128)(2,1)S(1)}, bf16[640,5120]{1,0:T(8,128)(2,1)}, u32[]{:S(2)}) %copy-start.1) | copy-done | bytes 6553624
  84.2 2.2 %copy-done.3 = bf16[8192,256]{1,0:T(8,128)(2,1)S(1)} copy-done((bf16[8192,256]{1,0:T(8,128)(2,1)S(1)}, bf16[8192,256]{1,0:T(8,128)(2,1)}, u32[]{:S(2)}) %copy-start.3) | copy-done | bytes 4194328
  86.4 4.7 %block_terms.3 = (f32[128,2560]{1,0:T(8,128)S(1)}, f32[128,2560]{1,0:T(8,128)S(1)}) custom-call(s32[1]{0:T(128)} %get-tuple-element.42.order_ref, s32[4,16]{1,0:T(4,128)S(1)} %fusion.9.rows_ref, bf16[512,640]{1,0:T(8,128)(2,1)S(1)} %q_project.1.q_ref, bf16[8192,256]{1,0:T(8,128)(2,1)S(1)} %copy-done.3, bf16[640,5120]{1,0:T(8,128)(2,1)S(1)} %copy-done.1, ...), custom_call_target="tpu_custom_call" | custom-call | flops 1048576 | bytes 1048576 | tf_op jit(solution)/shard_map/block_terms/pallas_call | solution.py:207
  91.2 1.6 %collective-permute-done.17.u2_ref = bf16[128,2560]{1,0:T(8,128)(2,1)S(1)} collective-permute-done((bf16[128,2560]{1,0:T(8,128)(2,1)}, bf16[128,2560]{1,0:T(8,128)(2,1)S(1)}, u32[]{:S(2)}, u32[]{:S(2)}) %collective-permute-start.17) | collective-permute-done | bytes 655392 | tf_op jit(solution)/shard_map/ppermute | solution.py:254
  92.8 10.0 %collective-permute-done.20.v2_ref = bf16[128,2560]{1,0:T(8,128)(2,1)} collective-permute-done((bf16[128,2560]{1,0:T(8,128)(2,1)}, bf16[128,2560]{1,0:T(8,128)(2,1)}, u32[]{:S(2)}, u32[]{:S(2)}) %collective-permute-start.20) | collective-permute-done | bytes 655392 | tf_op jit(solution)/shard_map/ppermute | solution.py:254
  102.8 3.4 %collective-permute-done.16.u1_ref = bf16[128,2560]{1,0:T(8,128)(2,1)} collective-permute-done((bf16[128,2560]{1,0:T(8,128)(2,1)}, bf16[128,2560]{1,0:T(8,128)(2,1)}, u32[]{:S(2)}, u32[]{:S(2)}) %collective-permute-start.16) | collective-permute-done | bytes 655392 | tf_op jit(solution)/shard_map/ppermute | solution.py:254
  106.2 4.0 %final_norm.1 = bf16[128,5120]{1,0:T(8,128)(2,1)} custom-call(f32[128,2560]{1,0:T(8,128)S(1)} %get-tuple-element.33.b1_ref, f32[128,2560]{1,0:T(8,128)S(1)} %get-tuple-element.34.b2_ref, bf16[128,2560]{1,0:T(8,128)(2,1)} %collective-permute-done.16.u1_ref, bf16[128,2560]{1,0:T(8,128)(2,1)S(1)} %collective-permute-done.17.u2_ref, ...), custom_call_target="tpu_custom_call" | custom-call | tf_op jit(solution)/shard_map/final_norm/pallas_call | solution.py:239
  (60 shorter events, 3.2 us)
Async XLA Ops:
  0.0 17.7 %copy-start.4 = (bf16[640,5120]{1,0:T(8,128)(2,1)S(1)}, bf16[640,5120]{1,0:T(8,128)(2,1)}, u32[]{:S(2)}) copy-start(bf16[640,5120]{1,0:T(8,128)(2,1)} %refs_0_.1) | copy-start | bytes 19660804
  8.4 12.5 %slice-start.2 = ((s8[6553600]{0:T(1024)(128)(4,1)}), s8[4194304]{0:T(1024)(128)(4,1)S(1)}, s32[]{:S(2)}) async-start(s8[6553600]{0:T(1024)(128)(4,1)} %bitcast.3), calls=%async_computation.2 | async-start | bytes 8388608
  8.4 12.5 %slice-start.3 = ((s8[6553600]{0:T(1024)(128)(4,1)}), s8[2359296]{0:T(1024)(128)(4,1)S(1)}, s32[]{:S(2)}) async-start(s8[6553600]{0:T(1024)(128)(4,1)} %bitcast.3), calls=%async_computation.3 | async-start | bytes 4718592
  8.4 12.5 %copy-start.5 = (bf16[512,5120]{1,0:T(8,128)(2,1)S(1)}, bf16[512,5120]{1,0:T(8,128)(2,1)}, u32[]{:S(2)}) copy-start(bf16[512,5120]{1,0:T(8,128)(2,1)} %get-tuple-element.24.x_ref) | copy-start | bytes 15728644
  8.4 19.1 %collective-permute-start = (bf16[512,256]{1,0:T(8,128)(2,1)S(1)}, bf16[512,256]{1,0:T(8,128)(2,1)S(1)}, u32[]{:S(2)}, u32[]{:S(2)}) collective-permute-start(bf16[512,256]{1,0:T(8,128)(2,1)S(1)} %get-tuple-element.26.refs_0_), channel_id=1, source_target_pairs={{0,40},{8,32},{16,56},{24,48},{32,8},{40,0},{48,24},{56,16},{1,41}... | collective-permute-start | bytes 786440 | tf_op jit(solution)/shard_map/ppermute | solution.py:263
  12.6 15.0 %collective-permute-start.1 = (bf16[512,256]{1,0:T(8,128)(2,1)S(1)}, bf16[512,256]{1,0:T(8,128)(2,1)S(1)}, u32[]{:S(2)}, u32[]{:S(2)}) collective-permute-start(bf16[512,256]{1,0:T(8,128)(2,1)S(1)} %get-tuple-element.26.refs_0_), channel_id=1, source_target_pairs={{0,32},{8,40},{16,48},{24,56},{32,0},{40,8},{48,16},{56,24},{1,33}... | collective-permute-start | bytes 786440 | tf_op jit(solution)/shard_map/ppermute | solution.py:263
  12.6 15.0 %collective-permute-start.2 = (bf16[512,256]{1,0:T(8,128)(2,1)S(1)}, bf16[512,256]{1,0:T(8,128)(2,1)S(1)}, u32[]{:S(2)}, u32[]{:S(2)}) collective-permute-start(bf16[512,256]{1,0:T(8,128)(2,1)S(1)} %get-tuple-element.26.refs_0_), channel_id=1, source_target_pairs={{0,56},{8,48},{16,8},{24,0},{32,24},{40,16},{48,40},{56,32},{1,57}... | collective-permute-start | bytes 786440 | tf_op jit(solution)/shard_map/ppermute | solution.py:263
  17.0 15.9 %collective-permute-start.3 = (bf16[512,256]{1,0:T(8,128)(2,1)S(1)}, bf16[512,256]{1,0:T(8,128)(2,1)S(1)}, u32[]{:S(2)}, u32[]{:S(2)}) collective-permute-start(bf16[512,256]{1,0:T(8,128)(2,1)S(1)} %get-tuple-element.26.refs_0_), channel_id=1, source_target_pairs={{0,24},{8,16},{16,40},{24,32},{32,56},{40,48},{48,8},{56,0},{1,25}... | collective-permute-start | bytes 786440 | tf_op jit(solution)/shard_map/ppermute | solution.py:263
  17.0 20.2 %collective-permute-start.4 = (bf16[512,256]{1,0:T(8,128)(2,1)S(1)}, bf16[512,256]{1,0:T(8,128)(2,1)S(1)}, u32[]{:S(2)}, u32[]{:S(2)}) collective-permute-start(bf16[512,256]{1,0:T(8,128)(2,1)S(1)} %get-tuple-element.26.refs_0_), channel_id=1, source_target_pairs={{0,8},{8,0},{16,24},{24,16},{32,40},{40,32},{48,56},{56,48},{1,9},... | collective-permute-start | bytes 786440 | tf_op jit(solution)/shard_map/ppermute | solution.py:263
  20.9 18.8 %copy-start.11 = (s32[4]{0:T(128)S(1)}, s32[4]{0:T(128)}, u32[]{:S(2)}) copy-start(s32[4]{0:T(128)} %constant.95.clone) | copy-start | bytes 52
  21.0 27.8 %copy-start.9 = (s32[4,16]{1,0:T(4,128)S(1)}, s32[4,16]{1,0:T(4,128)}, u32[]{:S(2)}) copy-start(s32[4,16]{1,0:T(4,128)} %param.17) | copy-start | bytes 772
  37.2 2.6 %collective-permute-start.5 = (bf16[512,256]{1,0:T(8,128)(2,1)S(1)}, bf16[512,256]{1,0:T(8,128)(2,1)S(1)}, u32[]{:S(2)}, u32[]{:S(2)}) collective-permute-start(bf16[512,256]{1,0:T(8,128)(2,1)S(1)} %get-tuple-element.26.refs_0_), channel_id=1, source_target_pairs={{0,4},{4,0},{1,5},{5,1},{2,6},{6,2},{3,7},{7,3},{8,12},{12,8},{9,1... | collective-permute-start | bytes 786440 | tf_op jit(solution)/shard_map/ppermute | solution.py:254
  37.2 2.7 %collective-permute-start.10 = (bf16[512,256]{1,0:T(8,128)(2,1)S(1)}, bf16[512,256]{1,0:T(8,128)(2,1)S(1)}, u32[]{:S(2)}, u32[]{:S(2)}) collective-permute-start(bf16[512,256]{1,0:T(8,128)(2,1)S(1)} %collective-permute-done.4.refs_10_), channel_id=1, source_target_pairs={{0,4},{4,0},{1,5},{5,1},{2,6},{6,2},{3,7},{7,3},{8,12},{12,8},{9,1... | collective-permute-start | bytes 786440 | tf_op jit(solution)/shard_map/ppermute | solution.py:254
  37.7 2.6 %collective-permute-start.6 = (bf16[512,256]{1,0:T(8,128)(2,1)S(1)}, bf16[512,256]{1,0:T(8,128)(2,1)S(1)}, u32[]{:S(2)}, u32[]{:S(2)}) collective-permute-start(bf16[512,256]{1,0:T(8,128)(2,1)S(1)} %collective-permute-done.refs_2_), channel_id=1, source_target_pairs={{0,4},{4,0},{1,5},{5,1},{2,6},{6,2},{3,7},{7,3},{8,12},{12,8},{9,1... | collective-permute-start | bytes 786440 | tf_op jit(solution)/shard_map/ppermute | solution.py:254
  37.7 8.7 %collective-permute-start.11 = (bf16[512,256]{1,0:T(8,128)(2,1)S(1)}, bf16[512,256]{1,0:T(8,128)(2,1)S(1)}, u32[]{:S(2)}, u32[]{:S(2)}) collective-permute-start(bf16[512,256]{1,0:T(8,128)(2,1)S(1)} %get-tuple-element.26.refs_0_), channel_id=1, source_target_pairs={{0,48},{8,56},{16,0},{24,8},{32,16},{40,24},{48,32},{56,40},{1,49}... | collective-permute-start | bytes 786440 | tf_op jit(solution)/shard_map/ppermute | solution.py:263
  38.5 9.6 %collective-permute-start.13 = (bf16[512,256]{1,0:T(8,128)(2,1)S(1)}, bf16[512,256]{1,0:T(8,128)(2,1)S(1)}, u32[]{:S(2)}, u32[]{:S(2)}) collective-permute-start(bf16[512,256]{1,0:T(8,128)(2,1)S(1)} %get-tuple-element.26.refs_0_), channel_id=1, source_target_pairs={{0,16},{8,24},{16,32},{24,40},{32,48},{40,56},{48,0},{56,8},{1,17}... | collective-permute-start | bytes 786440 | tf_op jit(solution)/shard_map/ppermute | solution.py:263
  39.8 9.0 %collective-permute-start.7 = (bf16[512,256]{1,0:T(8,128)(2,1)S(1)}, bf16[512,256]{1,0:T(8,128)(2,1)}, u32[]{:S(2)}, u32[]{:S(2)}) collective-permute-start(bf16[512,256]{1,0:T(8,128)(2,1)S(1)} %collective-permute-done.1.refs_4_), channel_id=1, source_target_pairs={{0,4},{4,0},{1,5},{5,1},{2,6},{6,2},{3,7},{7,3},{8,12},{12,8},{9,1... | collective-permute-start | bytes 786440 | tf_op jit(solution)/shard_map/ppermute | solution.py:254
  39.9 8.9 %collective-permute-start.8 = (bf16[512,256]{1,0:T(8,128)(2,1)S(1)}, bf16[512,256]{1,0:T(8,128)(2,1)}, u32[]{:S(2)}, u32[]{:S(2)}) collective-permute-start(bf16[512,256]{1,0:T(8,128)(2,1)S(1)} %collective-permute-done.2.refs_6_), channel_id=1, source_target_pairs={{0,4},{4,0},{1,5},{5,1},{2,6},{6,2},{3,7},{7,3},{8,12},{12,8},{9,1... | collective-permute-start | bytes 786440 | tf_op jit(solution)/shard_map/ppermute | solution.py:254
  40.4 8.4 %collective-permute-start.9 = (bf16[512,256]{1,0:T(8,128)(2,1)S(1)}, bf16[512,256]{1,0:T(8,128)(2,1)}, u32[]{:S(2)}, u32[]{:S(2)}) collective-permute-start(bf16[512,256]{1,0:T(8,128)(2,1)S(1)} %collective-permute-done.3.refs_8_), channel_id=1, source_target_pairs={{0,4},{4,0},{1,5},{5,1},{2,6},{6,2},{3,7},{7,3},{8,12},{12,8},{9,1... | collective-permute-start | bytes 786440 | tf_op jit(solution)/shard_map/ppermute | solution.py:254
  46.5 3.9 %collective-permute-start.12 = (bf16[512,256]{1,0:T(8,128)(2,1)S(1)}, bf16[512,256]{1,0:T(8,128)(2,1)}, u32[]{:S(2)}, u32[]{:S(2)}) collective-permute-start(bf16[512,256]{1,0:T(8,128)(2,1)S(1)} %collective-permute-done.11.refs_1_), channel_id=1, source_target_pairs={{0,4},{4,0},{1,5},{5,1},{2,6},{6,2},{3,7},{7,3},{8,12},{12,8},{9,1... | collective-permute-start | bytes 786440 | tf_op jit(solution)/shard_map/ppermute | solution.py:254
  48.1 2.2 %collective-permute-start.14 = (bf16[512,256]{1,0:T(8,128)(2,1)S(1)}, bf16[512,256]{1,0:T(8,128)(2,1)}, u32[]{:S(2)}, u32[]{:S(2)}) collective-permute-start(bf16[512,256]{1,0:T(8,128)(2,1)S(1)} %collective-permute-done.13.refs_3_), channel_id=1, source_target_pairs={{0,4},{4,0},{1,5},{5,1},{2,6},{6,2},{3,7},{7,3},{8,12},{12,8},{9,1... | collective-permute-start | bytes 786440 | tf_op jit(solution)/shard_map/ppermute | solution.py:254
  51.6 8.4 %copy-start.2 = (bf16[8192,256]{1,0:T(8,128)(2,1)}, bf16[8192,256]{1,0:T(8,128)(2,1)S(1)}, u32[]{:S(2)}) copy-start(bf16[8192,256]{1,0:T(8,128)(2,1)S(1)} %collect.5.kv_ref) | copy-start | bytes 12582916
  57.1 17.9 %collective-permute-start.19 = (bf16[128,2560]{1,0:T(8,128)(2,1)S(1)}, bf16[128,2560]{1,0:T(8,128)(2,1)S(1)}, u32[]{:S(2)}, u32[]{:S(2)}) collective-permute-start(bf16[128,2560]{1,0:T(8,128)(2,1)S(1)} %get-tuple-element.40), channel_id=1, source_target_pairs={{0,3},{1,0},{2,1},{3,2},{4,7},{5,4},{6,5},{7,6},{8,11},{9,8},{10,9... | collective-permute-start | bytes 1966088 | tf_op jit(solution)/shard_map/ppermute | solution.py:254
  59.9 19.8 %collective-permute-start.15 = (bf16[128,2560]{1,0:T(8,128)(2,1)S(1)}, bf16[128,2560]{1,0:T(8,128)(2,1)S(1)}, u32[]{:S(2)}, u32[]{:S(2)}) collective-permute-start(bf16[128,2560]{1,0:T(8,128)(2,1)S(1)} %get-tuple-element.36), channel_id=1, source_target_pairs={{0,1},{1,2},{2,3},{3,0},{4,5},{5,6},{6,7},{7,4},{8,9},{9,10},{10,1... | collective-permute-start | bytes 1966088 | tf_op jit(solution)/shard_map/ppermute | solution.py:254
  60.0 20.7 %copy-start.10 = (s32[4]{0:T(128)S(1)}, s32[4]{0:T(128)}, u32[]{:S(2)}) copy-start(s32[4]{0:T(128)} %param.18) | copy-start | bytes 52
  70.3 11.0 %copy-start.7 = (bf16[128,5120]{1,0:T(8,128)(2,1)S(1)}, bf16[128,5120]{1,0:T(8,128)(2,1)}, u32[]{:S(2)}) copy-start(bf16[128,5120]{1,0:T(8,128)(2,1)} %rest_0_.1) | copy-start | bytes 3932164
  70.3 22.4 %collective-permute-start.17 = (bf16[128,2560]{1,0:T(8,128)(2,1)}, bf16[128,2560]{1,0:T(8,128)(2,1)S(1)}, u32[]{:S(2)}, u32[]{:S(2)}) collective-permute-start(bf16[128,2560]{1,0:T(8,128)(2,1)} %get-tuple-element.37), channel_id=1, source_target_pairs={{0,1},{1,2},{2,3},{3,0},{4,5},{5,6},{6,7},{7,4},{8,9},{9,10},{10,1... | collective-permute-start | bytes 1966088 | tf_op jit(solution)/shard_map/ppermute | solution.py:254
  71.1 21.7 %collective-permute-start.18 = (bf16[128,2560]{1,0:T(8,128)(2,1)}, bf16[128,2560]{1,0:T(8,128)(2,1)S(1)}, u32[]{:S(2)}, u32[]{:S(2)}) collective-permute-start(bf16[128,2560]{1,0:T(8,128)(2,1)} %get-tuple-element.38), channel_id=1, source_target_pairs={{0,3},{1,0},{2,1},{3,2},{4,7},{5,4},{6,5},{7,6},{8,11},{9,8},{10,9... | collective-permute-start | bytes 1966088 | tf_op jit(solution)/shard_map/ppermute | solution.py:254
  76.0 26.8 %collective-permute-start.20 = (bf16[128,2560]{1,0:T(8,128)(2,1)}, bf16[128,2560]{1,0:T(8,128)(2,1)}, u32[]{:S(2)}, u32[]{:S(2)}) collective-permute-start(bf16[128,2560]{1,0:T(8,128)(2,1)} %add.62), channel_id=1, source_target_pairs={{0,3},{1,0},{2,1},{3,2},{4,7},{5,4},{6,5},{7,6},{8,11},{9,8},{10,9... | collective-permute-start | bytes 1966088 | tf_op jit(solution)/shard_map/ppermute | solution.py:254
  80.7 25.5 %collective-permute-start.16 = (bf16[128,2560]{1,0:T(8,128)(2,1)}, bf16[128,2560]{1,0:T(8,128)(2,1)}, u32[]{:S(2)}, u32[]{:S(2)}) collective-permute-start(bf16[128,2560]{1,0:T(8,128)(2,1)} %add.61), channel_id=1, source_target_pairs={{0,1},{1,2},{2,3},{3,0},{4,5},{5,6},{6,7},{7,4},{8,9},{9,10},{10,1... | collective-permute-start | bytes 1966088 | tf_op jit(solution)/shard_map/ppermute | solution.py:254
  81.3 2.9 %copy-start.1 = (bf16[640,5120]{1,0:T(8,128)(2,1)S(1)}, bf16[640,5120]{1,0:T(8,128)(2,1)}, u32[]{:S(2)}) copy-start(bf16[640,5120]{1,0:T(8,128)(2,1)} %copy-done) | copy-start | bytes 19660804
  86.4 19.8 %copy-start.8 = (f32[5120]{0:T(1024)S(1)}, f32[5120]{0:T(1024)}, u32[]{:S(2)}) copy-start(f32[5120]{0:T(1024)} %param.16) | copy-start | bytes 61444
  (5 other events, 11.2 us)

commit v6 on v5

v6 whole, which is shorter than its diff:
```python
import functools
import math

import jax
import jax.numpy as jnp
from jax import lax
from jax.experimental import pallas as pl
from jax.experimental.pallas import tpu as pltpu
from jax.sharding import Mesh, PartitionSpec as P

HD = 128
BLK = 128
CHUNK = 4
CTX = ("z", "y", "core")
F32 = jnp.float32
BF16 = jnp.bfloat16
SCALE2 = math.log2(math.e) / math.sqrt(HD)
SPLIT = ((0, 3), (3, 5))
KERNEL_VMEM = 58 << 20
BLOCK_VMEM = 30 << 20
SMALL_COST = pl.CostEstimate(flops=1 << 20, bytes_accessed=1 << 20, transcendentals=0)
NT = (((1,), (1,)), ((), ()))


def kv_kernel(x_ref, wk_ref, wv_ref, o_ref, xbuf, wbuf, sems):
    parts, tile, _ = wbuf.shape
    copies = []
    for k in range(parts):
        cut = pl.ds(k * tile, tile)
        group = [
            pltpu.make_async_copy(x_ref.at[:, cut], xbuf.at[:, cut], sems.at[0, k]),
            pltpu.make_async_copy(wk_ref.at[cut], wbuf.at[k, :, pl.ds(0, HD)], sems.at[1, k]),
            pltpu.make_async_copy(wv_ref.at[cut], wbuf.at[k, :, pl.ds(HD, HD)], sems.at[2, k]),
        ]
        for copy in group:
            copy.start()
        copies.append(group)
    total = None
    for k in range(parts):
        for copy in copies[k]:
            copy.wait()
        part = jnp.dot(
            xbuf[:, k * tile:(k + 1) * tile], wbuf[k], preferred_element_type=F32
        )
        total = part if total is None else total + part
    o_ref[...] = total.astype(BF16)


def kv_project(x, wk, wv):
    rows, depth = x.shape
    parts = 5
    hbm = pl.BlockSpec(memory_space=pltpu.HBM)
    return pl.pallas_call(
        kv_kernel,
        name="kv_project",
        out_shape=jax.ShapeDtypeStruct((rows, 2 * HD), BF16),
        in_specs=[hbm] * 3,
        out_specs=pl.BlockSpec(memory_space=pltpu.VMEM),
        scratch_shapes=[
            pltpu.VMEM((rows, depth), BF16),
            pltpu.VMEM((parts, depth // parts, 2 * HD), BF16),
            pltpu.SemaphoreType.DMA((3, parts)),
        ],
        compiler_params=pltpu.CompilerParams(vmem_limit_bytes=KERNEL_VMEM),
        cost_estimate=SMALL_COST,
    )(x, wk, wv)


def q_kernel(x_ref, w_ref, o_ref, wbuf, sems):
    parts, tile, _ = wbuf.shape
    copies = [
        pltpu.make_async_copy(w_ref.at[pl.ds(k * tile, tile)], wbuf.at[k], sems.at[k])
        for k in range(parts)
    ]
    for copy in copies:
        copy.start()
    total = None
    for k in range(parts):
        copies[k].wait()
        part = jnp.dot(x_ref[:, k * tile:(k + 1) * tile], wbuf[k], preferred_element_type=F32)
        total = part if total is None else total + part
    o_ref[...] = total.astype(BF16)


def q_project(x, w):
    parts = 5
    vmem = pl.BlockSpec(memory_space=pltpu.VMEM)
    return pl.pallas_call(
        q_kernel,
        name="q_project",
        out_shape=jax.ShapeDtypeStruct((x.shape[0], w.shape[1]), BF16),
        in_specs=[vmem, pl.BlockSpec(memory_space=pltpu.HBM)],
        out_specs=vmem,
        scratch_shapes=[
            pltpu.VMEM((parts, w.shape[0] // parts, w.shape[1]), BF16),
            pltpu.SemaphoreType.DMA((parts,)),
        ],
        compiler_params=pltpu.CompilerParams(vmem_limit_bytes=20 << 20),
        cost_estimate=SMALL_COST,
    )(x, w)


def tie(values):
    spec = pl.BlockSpec(memory_space=pl.ANY)
    return pl.pallas_call(
        lambda *refs: None,
        name="tie",
        out_shape=[jax.ShapeDtypeStruct(x.shape, x.dtype) for x in values],
        in_specs=[spec] * len(values),
        out_specs=[spec] * len(values),
        input_output_aliases={k: k for k in range(len(values))},
        compiler_params=pltpu.CompilerParams(vmem_limit_bytes=1 << 20),
        cost_estimate=SMALL_COST,
    )(*values)


def collect_kernel(moves, based, *refs):
    pieces, out, sems = refs[based:based + len(moves)], refs[-2], refs[-1]
    copies = []
    for piece, cuts in zip(pieces, moves):
        for source, target, size in cuts:
            copies.append(
                pltpu.make_async_copy(
                    piece.at[pl.ds(source, size)],
                    out.at[pl.ds(target, size)],
                    sems.at[len(copies)],
                )
            )
    for copy in copies:
        copy.start()
    for copy in copies:
        copy.wait()


def collect(parts, shape, base=None, after=()):
    pieces, moves = zip(*parts)
    based = 0 if base is None else 1
    return pl.pallas_call(
        functools.partial(collect_kernel, moves, based),
        name="collect",
        out_shape=jax.ShapeDtypeStruct(shape, BF16),
        in_specs=[pl.BlockSpec(memory_space=pl.ANY)] * (based + len(pieces) + len(after)),
        out_specs=pl.BlockSpec(memory_space=pl.ANY),
        scratch_shapes=[pltpu.SemaphoreType.DMA((sum(len(x) for x in moves),))],
        input_output_aliases={0: 0} if based else {},
        compiler_params=pltpu.CompilerParams(vmem_limit_bytes=2 << 20),
        cost_estimate=SMALL_COST,
    )(*([base] if based else []), *pieces, *after)


def attend(q, kv_ref, own_row, rows, count):
    slots = len(rows)
    take = [kv_ref[pl.ds(pl.multiple_of(r, BLK), BLK), :] for r in rows]
    own = kv_ref[pl.ds(pl.multiple_of(own_row, BLK), BLK), :]
    groups = [take[c:c + CHUNK] for c in range(0, slots, CHUNK)]
    keys = [jnp.concatenate([x[:, :HD] for x in g], axis=0) for g in groups]
    values = [jnp.concatenate([x[:, HD:] for x in g], axis=0) for g in groups]
    results = []
    for lo, hi in SPLIT:
        part = q[lo * BLK:hi * BLK]
        s = lax.dot_general(part, own[:, :HD], NT, preferred_element_type=F32)
        row = lax.broadcasted_iota(jnp.int32, s.shape, 0) % BLK
        col = lax.broadcasted_iota(jnp.int32, s.shape, 1)
        pieces = [jnp.where(col <= row, s, -jnp.inf)]
        for c, key in enumerate(keys):
            s = lax.dot_general(part, key, NT, preferred_element_type=F32)
            for j in range(CHUNK):
                pieces.append(
                    jnp.where(c * CHUNK + j < count, s[:, j * BLK:(j + 1) * BLK], -jnp.inf)
                )
        top = pieces[0]
        for piece in pieces[1:]:
            top = jnp.maximum(top, piece)
        top = jnp.max(top, axis=1, keepdims=True)
        weights = [jnp.exp2((piece - top) * SCALE2) for piece in pieces]
        total = weights[0]
        for w in weights[1:]:
            total = total + w
        out = jnp.dot(weights[0].astype(BF16), own[:, HD:], preferred_element_type=F32)
        for c, value in enumerate(values):
            w = jnp.concatenate(
                [x.astype(BF16) for x in weights[1 + c * CHUNK:1 + (c + 1) * CHUNK]], axis=1
            )
            out = out + jnp.dot(w, value, preferred_element_type=F32)
        out = (out / jnp.sum(total, axis=1, keepdims=True)).astype(BF16)
        results += [out[h * BLK:(h + 1) * BLK] for h in range(hi - lo)]
    return jnp.concatenate(results, axis=1)


def block_row(entry, per):
    owner = entry // per
    dz = (owner // 4 - lax.axis_index("z") + 4) % 4
    dy = (owner // 2 + lax.axis_index("y")) % 2
    dc = (owner + lax.axis_index("core")) % 2
    return ((dz * 4 + dy * 2 + dc) * per + entry % per) * BLK


def block_kernel(turn, anc_ref, q_ref, kv_ref, w_ref, *rest):
    res_ref, outs = (rest[0], rest[1:3]) if len(rest) % 2 else (None, rest[:2])
    per, slots = anc_ref.shape
    local = (lax.axis_index("tp") + turn) % per
    rows, count = [], jnp.int32(0)
    for l in range(slots):
        entry = anc_ref[local, l]
        count += jnp.where(entry >= 0, 1, 0).astype(jnp.int32)
        rows.append(block_row(jnp.maximum(entry, 0), per))
    q_all = q_ref[pl.ds(pl.multiple_of(local * BLK, BLK), BLK), :]
    heads = q_all.shape[1] // HD
    q = jnp.concatenate([q_all[:, h * HD:(h + 1) * HD] for h in range(heads)], axis=0)
    head_out = attend(q, kv_ref, local * BLK, rows, count)
    half = outs[0].shape[1]
    tile = half // 2
    for side in range(2):
        for c in range(0, half, tile):
            cut = slice(side * half + c, side * half + c + tile)
            part = jnp.dot(head_out, w_ref[:, cut], preferred_element_type=F32).astype(BF16)
            if res_ref is not None:
                part = part.astype(F32) + res_ref[:, cut].astype(F32)
            outs[side][:, c:c + tile] = part


def block_terms(turn, ancestors, q, kv, w_out, residual=None):
    cols = w_out.shape[1]
    vmem = pl.BlockSpec(memory_space=pltpu.VMEM)
    extra = [] if residual is None else [residual]
    kind = BF16 if residual is None else F32
    outs = pl.pallas_call(
        functools.partial(block_kernel, turn),
        name="block_terms",
        out_shape=[jax.ShapeDtypeStruct((BLK, cols // 2), kind)] * 2
        + [jax.ShapeDtypeStruct(x.shape, x.dtype) for x in (kv, w_out)],
        in_specs=[pl.BlockSpec(memory_space=pltpu.SMEM)] + [vmem] * (3 + len(extra)),
        out_specs=[vmem] * 2 + [pl.BlockSpec(memory_space=pl.ANY)] * 2,
        input_output_aliases={2: 2, 3: 3},
        compiler_params=pltpu.CompilerParams(vmem_limit_bytes=BLOCK_VMEM),
        cost_estimate=SMALL_COST,
    )(ancestors, q, kv, w_out, *extra)
    return outs[:2], outs[2:]


def norm_kernel(b1_ref, b2_ref, u_ref, v_ref, gain_ref, keep_ref, o_ref):
    half = u_ref.shape[1]
    total = [b1_ref[...] + u_ref[...].astype(F32), b2_ref[...] + v_ref[...].astype(F32)]
    square = sum(jnp.sum(x * x, axis=1, keepdims=True) for x in total)
    factor = lax.rsqrt(square * (1.0 / (2 * half)) + 1e-06) * keep_ref[lax.axis_index("tp")].astype(F32)
    for lo, x in zip((0, half), total):
        o_ref[:, lo:lo + half] = (x * factor * gain_ref[:, lo:lo + half]).astype(BF16)


def final_norm(base, last, gain, keep):
    rows, half = base[0].shape
    vm = pl.BlockSpec(memory_space=pltpu.VMEM)
    return pl.pallas_call(
        norm_kernel,
        name="final_norm",
        out_shape=jax.ShapeDtypeStruct((rows, 2 * half), BF16),
        in_specs=[vm] * 5 + [pl.BlockSpec(memory_space=pltpu.SMEM)],
        out_specs=vm,
        compiler_params=pltpu.CompilerParams(vmem_limit_bytes=30 << 20),
    )(*base, *last, gain[None, :], keep)


def ring(n, s):
    return [(i, (i + s) % n) for i in range(n)]


def shift(x, axis, s):
    return lax.ppermute(x, axis, ring({"y": 2, "core": 2, "z": 4, "tp": 4}[axis], s))


def gather_blocks(own, first, second):
    rows = own.shape[0]
    half = rows // 2

    def fetch(x, dz, dy):
        pairs = [(i, ((i // 2 - dz) % 4) * 2 + (i + dy) % 2) for i in range(8)]
        return lax.ppermute(x, ("z", "y"), pairs)

    def both(piece, *moves):
        result, source = ([], []), 0
        for dz, dy, skip, size in moves:
            spot = (dz * 4 + dy * 2) * rows + skip
            for core in range(2):
                result[core].append((source, spot + core * rows, size))
            source += size
        return [(piece, tuple(result[0])), (shift(piece, "core", 1), tuple(result[1]))]

    y_far = fetch(own, 2, 1)
    y = fetch(own, 0, 1)
    up = fetch(own, 1, 0)
    down = fetch(own, 3, 0)
    y_far, y, up, down, first = tie((y_far, y, up, down, first()))
    more_up = fetch(jnp.concatenate([y, up[:half]], axis=0), 1, 0)
    more_down = fetch(jnp.concatenate([y, down[half:]], axis=0), 3, 0)
    early = (
        both(own, (0, 0, 0, rows))
        + both(y, (0, 1, 0, rows))
        + both(up, (1, 0, 0, rows))
        + both(down, (3, 0, 0, rows))
        + both(y_far, (2, 1, 0, rows))
    )
    shape = (16 * rows, own.shape[1])
    more_up, more_down, base, second = tie((more_up, more_down, collect(early, shape), second(y)))
    late = both(more_up, (1, 1, 0, rows), (2, 0, 0, half)) + both(
        more_down, (3, 1, 0, rows), (2, 0, half, half)
    )
    return collect(late, shape, base), first, second


def on_device(activations, residual, w_query, w_key, w_value, w_out, gain, ancestors, kept):
    kv_own = kv_project(activations, w_key, w_value)
    kv, queries, w_held = gather_blocks(
        kv_own,
        lambda: q_project(activations, w_query),
        lambda there: collect([(w_out, ((0, 0, w_out.shape[0]),))], w_out.shape, None, (there,)),
    )

    def send(x, s):
        return shift(x, "tp", s % 4)

    (lo2, hi2), held = block_terms(2, ancestors, queries, kv, w_held)
    a = send(lo2, 1)
    b = send(hi2, 3)
    (lo1, hi1), held = block_terms(1, ancestors, queries, *held)
    u2 = send(hi1, 1)
    (lo3, hi3), held = block_terms(3, ancestors, queries, *held)
    v1 = send(lo3, 3)
    (left, right), _ = block_terms(0, ancestors, queries, *held, residual)
    u1 = send(lo1 + a, 1)
    v2 = send(hi3 + b, 3)
    base = (left + v1.astype(F32), right + u2.astype(F32))
    return final_norm(base, (u1, v2), gain, kept)


def solution(mesh):
    fine = Mesh(mesh.devices.reshape(2, 4, 2, 2, 4), ("dp", "z", "y", "core", "tp"))
    ctx = ("dp",) + CTX
    in_specs = (
        P(ctx, None),
        P(ctx + ("tp",), None),
        P(None, "tp"),
        P(None, "tp"),
        P(None, "tp"),
        P("tp", None),
        P(),
        P(ctx, None),
        P(ctx),
    )
    out_specs = P(ctx + ("tp",), None)
    return jax.shard_map(
        on_device, mesh=fine, in_specs=in_specs, out_specs=out_specs, check_vma=False
    )
```

time: 110 us -> 93.6 us (0.85)
  local copies, waits for them, and re-layouts: 11.4 us -> 2.91 us
  Pallas kernels: 40.4 us -> 32.6 us
  waiting for transfers between devices: 33.8 us -> 36 us
  starting transfers between devices: 22.3 us -> 20.7 us
  other arithmetic: 2.06 us -> 0.65 us
    ppermute x14 -> x13, waiting for transfers between devices: 16.5 us -> 27.4 us  [shift(): lax.ppermute(x, axis, ring({'y': 2, 'core': 2, 'z': 4, 'tp': 4}[axis], s))]
    ppermute x7 -> x6, waiting for transfers between devices: 17.2 us -> 8.69 us  [fetch(): return lax.ppermute(x, ('z', 'y'), pairs)]
    unnamed x32 -> x16, local copies, waits for them, and re-layouts: 10.1 us -> 2.89 us
    pallas_call x7 -> x10, Pallas kernels: 29.8 us -> 23.6 us  [the longest x4 16.4 us: block_terms(): pl.pallas_call(functools.partial(block_kernel, turn), name='block_terms',...]
    pallas_call x1, Pallas kernels: 3.96 us -> 2.4 us  [final_norm(): pl.pallas_call(norm_kernel, name='final_norm', out_shape=jax.ShapeDtypeSt...]
    ppermute x14 -> x13, starting transfers between devices: 11 us -> 9.97 us  [shift(): lax.ppermute(x, axis, ring({'y': 2, 'core': 2, 'z': 4, 'tp': 4}[axis], s))]
    ppermute x7 -> x6, starting transfers between devices: 11.3 us -> 10.7 us  [fetch(): return lax.ppermute(x, ('z', 'y'), pairs)]
  transfers between devices with their start and end apart: 21 -> 19, of which waited for: 8 -> 10; matrix products, arithmetic and copies ran while one was open for 3% -> 1% of each run, Pallas kernels for 21% -> 21%
where the time goes in v6:
time: 93.6 us; the launch traced here: 93.1 us
  waiting for transfers between devices  36 us (38%)
  Pallas kernels  32.6 us (35%)
  starting transfers between devices  20.7 us (22%)
  local copies, waits for them, and re-layouts  2.91 us (3%)
    ppermute x13, waiting for transfers between devices, shift(): lax.ppermute(x, axis, ring({'y': 2, 'core': 2, 'z': 4, 'tp': 4}[axis], s))  27.4 us
    pallas_call x4, Pallas kernels, block_terms(): pl.pallas_call(functools.partial(block_kernel, turn), name='block_terms',...  16.4 us
    ppermute x6, starting transfers between devices, fetch(): return lax.ppermute(x, ('z', 'y'), pairs)  10.7 us
    ppermute x13, starting transfers between devices, shift(): lax.ppermute(x, axis, ring({'y': 2, 'core': 2, 'z': 4, 'tp': 4}[axis], s))  9.97 us
    ppermute x6, waiting for transfers between devices, fetch(): return lax.ppermute(x, ('z', 'y'), pairs)  8.69 us
    pallas_call x1, Pallas kernels, q_project(): pl.pallas_call(q_kernel, name='q_project', out_shape=jax.ShapeDtypeStruct...  6.6 us
    pallas_call x1, Pallas kernels, kv_project(): pl.pallas_call(kv_kernel, name='kv_project', out_shape=jax.ShapeDtypeStru...  5.62 us
    unnamed x16, local copies, waits for them, and re-layouts  2.89 us
  transfers between devices with their start and end apart: 19, of which 10 were waited for; matrix products, arithmetic and copies ran while one was open for 1% of the time, Pallas kernels for 21%

profile of v6, /device:TPU:24, one launch (start us, length us, event | category | flops | bytes accessed | tf_op | source)
XLA Modules:
  0.0 93.1 jit_solution(1474896219778918081)
XLA Ops:
  0.0 5.6 %kv_project.1.refs_0_ = bf16[512,256]{1,0:T(8,128)(2,1)} custom-call(bf16[512,5120]{1,0:T(8,128)(2,1)} %x_ref.3, bf16[5120,128]{1,0:T(8,128)(2,1)} %wk_ref.1, bf16[5120,128]{1,0:T(8,128)(2,1)} %wv_ref.1), custom_call_target="tpu_custom_call" | custom-call | flops 1048576 | bytes 1048576 | tf_op jit(solution)/shard_map/kv_project/pallas_call | solution.py:53
  5.6 2.0 %collective-permute-start.3 = (bf16[512,256]{1,0:T(8,128)(2,1)}, bf16[512,256]{1,0:T(8,128)(2,1)S(1)}, u32[]{:S(2)}, u32[]{:S(2)}) collective-permute-start(bf16[512,256]{1,0:T(8,128)(2,1)} %kv_project.1.refs_0_), channel_id=1, source_target_pairs={{0,16},{8,24},{16,32},{24,40},{32,48},{40,56},{48,0},{56,8},{1,17}... | collective-permute-start | bytes 786440 | tf_op jit(solution)/shard_map/ppermute | solution.py:277
  7.6 2.2 %collective-permute-start.2 = (bf16[512,256]{1,0:T(8,128)(2,1)}, bf16[512,256]{1,0:T(8,128)(2,1)S(1)}, u32[]{:S(2)}, u32[]{:S(2)}) collective-permute-start(bf16[512,256]{1,0:T(8,128)(2,1)} %kv_project.1.refs_0_), channel_id=1, source_target_pairs={{0,48},{8,56},{16,0},{24,8},{32,16},{40,24},{48,32},{56,40},{1,49}... | collective-permute-start | bytes 786440 | tf_op jit(solution)/shard_map/ppermute | solution.py:277
  9.8 0.7 collective-permute-start.1
  10.6 2.5 %collective-permute-start = (bf16[512,256]{1,0:T(8,128)(2,1)}, bf16[512,256]{1,0:T(8,128)(2,1)S(1)}, u32[]{:S(2)}, u32[]{:S(2)}) collective-permute-start(bf16[512,256]{1,0:T(8,128)(2,1)} %kv_project.1.refs_0_), channel_id=1, source_target_pairs={{0,40},{8,32},{16,56},{24,48},{32,8},{40,0},{48,24},{56,16},{1,41}... | collective-permute-start | bytes 786440 | tf_op jit(solution)/shard_map/ppermute | solution.py:277
  13.1 2.9 %copy-done.1 = bf16[5120,640]{1,0:T(8,128)(2,1)S(1)} copy-done((bf16[5120,640]{1,0:T(8,128)(2,1)S(1)}, bf16[5120,640]{1,0:T(8,128)(2,1)}, u32[]{:S(2)}) %copy-start.1) | copy-done | bytes 6553624
  15.9 6.6 %q_project.1.refs_4_ = bf16[512,640]{1,0:T(8,128)(2,1)S(1)} custom-call(bf16[512,5120]{1,0:T(8,128)(2,1)S(1)} %copy-done, bf16[5120,640]{1,0:T(8,128)(2,1)S(1)} %copy-done.1), custom_call_target="tpu_custom_call" | custom-call | flops 1048576 | bytes 1048576 | tf_op jit(solution)/shard_map/q_project/pallas_call | solution.py:88
  22.6 1.8 %collective-permute-done.refs_0_ = bf16[512,256]{1,0:T(8,128)(2,1)S(1)} collective-permute-done((bf16[512,256]{1,0:T(8,128)(2,1)}, bf16[512,256]{1,0:T(8,128)(2,1)S(1)}, u32[]{:S(2)}, u32[]{:S(2)}) %collective-permute-start) | collective-permute-done | bytes 262176 | tf_op jit(solution)/shard_map/ppermute | solution.py:277
  24.5 1.1 %collective-permute-start.5 = (bf16[768,256]{1,0:T(8,128)(2,1)S(1)}, bf16[768,256]{1,0:T(8,128)(2,1)S(1)}, u32[]{:S(2)}, u32[]{:S(2)}) collective-permute-start(bf16[768,256]{1,0:T(8,128)(2,1)S(1)} %get-tuple-element.51), channel_id=1, source_target_pairs={{0,16},{8,24},{16,32},{24,40},{32,48},{40,56},{48,0},{56,8},{1,17}... | collective-permute-start | bytes 1179656 | tf_op jit(solution)/shard_map/ppermute | solution.py:277
  25.6 2.2 %collective-permute-start.4 = (bf16[768,256]{1,0:T(8,128)(2,1)S(1)}, bf16[768,256]{1,0:T(8,128)(2,1)S(1)}, u32[]{:S(2)}, u32[]{:S(2)}) collective-permute-start(bf16[768,256]{1,0:T(8,128)(2,1)S(1)} %get-tuple-element.52), channel_id=1, source_target_pairs={{0,48},{8,56},{16,0},{24,8},{32,16},{40,24},{48,32},{56,40},{1,49}... | collective-permute-start | bytes 1179656 | tf_op jit(solution)/shard_map/ppermute | solution.py:277
  27.9 0.5 collective-permute-start.9
  28.5 0.4 collect.4.refs_3_
  28.9 0.5 collective-permute-done.8.refs_5_
  29.8 0.4 collective-permute-done.7.refs_3_
  30.4 6.9 %collective-permute-done.5.refs_1_ = bf16[768,256]{1,0:T(8,128)(2,1)S(1)} collective-permute-done((bf16[768,256]{1,0:T(8,128)(2,1)S(1)}, bf16[768,256]{1,0:T(8,128)(2,1)S(1)}, u32[]{:S(2)}, u32[]{:S(2)}) %collective-permute-start.5) | collective-permute-done | bytes 393248 | tf_op jit(solution)/shard_map/ppermute | solution.py:277
  37.3 0.5 collective-permute-start.12
  37.9 1.2 %collective-permute-done.11.refs_2_ = bf16[768,256]{1,0:T(8,128)(2,1)S(1)} collective-permute-done((bf16[768,256]{1,0:T(8,128)(2,1)S(1)}, bf16[768,256]{1,0:T(8,128)(2,1)S(1)}, u32[]{:S(2)}, u32[]{:S(2)}) %collective-permute-start.11) | collective-permute-done | bytes 393248 | tf_op jit(solution)/shard_map/ppermute | solution.py:268
  39.1 0.6 collective-permute-done.12.refs_4_
  39.6 0.8 collect.5.kv_ref
  40.5 4.1 %block_terms.4 = (bf16[128,2560]{1,0:T(8,128)(2,1)S(1)}, bf16[128,2560]{1,0:T(8,128)(2,1)S(1)}, bf16[8192,256]{1,0:T(8,128)(2,1)S(1)}, bf16[640,5120]{1,0:T(8,128)(2,1)S(1)}) custom-call(s32[4,16]{1,0:T(4,128)S(1)} %copy-done.5, bf16[512,640]{1,0:T(8,128)(2,1)S(1)} %get-tuple-element.28.q_ref, ...), custom_call_target="tpu_custom_call", output_to_operand_aliasing={{2}: (2, {}), {3}: (3, {})} | custom-call | flops 1048576 | bytes 1048576 | tf_op jit(solution)/shard_map/block_terms/pallas_call | solution.py:227
  44.6 1.6 %collective-permute-start.15 = (bf16[128,2560]{1,0:T(8,128)(2,1)S(1)}, bf16[128,2560]{1,0:T(8,128)(2,1)S(1)}, u32[]{:S(2)}, u32[]{:S(2)}) collective-permute-start(bf16[128,2560]{1,0:T(8,128)(2,1)S(1)} %get-tuple-element.48), channel_id=1, source_target_pairs={{0,1},{1,2},{2,3},{3,0},{4,5},{5,6},{6,7},{7,4},{8,9},{9,10},{10,1... | collective-permute-start | bytes 1966088 | tf_op jit(solution)/shard_map/ppermute | solution.py:268
  46.1 1.7 %collective-permute-start.17 = (bf16[128,2560]{1,0:T(8,128)(2,1)S(1)}, bf16[128,2560]{1,0:T(8,128)(2,1)S(1)}, u32[]{:S(2)}, u32[]{:S(2)}) collective-permute-start(bf16[128,2560]{1,0:T(8,128)(2,1)S(1)} %get-tuple-element.50), channel_id=1, source_target_pairs={{0,3},{1,0},{2,1},{3,2},{4,7},{5,4},{6,5},{7,6},{8,11},{9,8},{10,9... | collective-permute-start | bytes 1966088 | tf_op jit(solution)/shard_map/ppermute | solution.py:268
  47.9 4.1 %block_terms.5 = (bf16[128,2560]{1,0:T(8,128)(2,1)S(1)}, bf16[128,2560]{1,0:T(8,128)(2,1)S(1)}, bf16[8192,256]{1,0:T(8,128)(2,1)S(1)}, bf16[640,5120]{1,0:T(8,128)(2,1)S(1)}) custom-call(s32[4,16]{1,0:T(4,128)S(1)} %copy-done.5, bf16[512,640]{1,0:T(8,128)(2,1)S(1)} %get-tuple-element.28.q_ref, ...), custom_call_target="tpu_custom_call", output_to_operand_aliasing={{2}: (2, {}), {3}: (3, {})} | custom-call | flops 1048576 | bytes 1048576 | tf_op jit(solution)/shard_map/block_terms/pallas_call | solution.py:227
  52.0 4.1 %block_terms.6 = (bf16[128,2560]{1,0:T(8,128)(2,1)S(1)}, bf16[128,2560]{1,0:T(8,128)(2,1)S(1)}, bf16[8192,256]{1,0:T(8,128)(2,1)S(1)}, bf16[640,5120]{1,0:T(8,128)(2,1)S(1)}) custom-call(s32[4,16]{1,0:T(4,128)S(1)} %copy-done.5, bf16[512,640]{1,0:T(8,128)(2,1)S(1)} %get-tuple-element.28.q_ref, ...), custom_call_target="tpu_custom_call", output_to_operand_aliasing={{2}: (2, {}), {3}: (3, {})} | custom-call | flops 1048576 | bytes 1048576 | tf_op jit(solution)/shard_map/block_terms/pallas_call | solution.py:227
  56.1 1.6 %collective-permute-start.13 = (bf16[128,2560]{1,0:T(8,128)(2,1)S(1)}, bf16[128,2560]{1,0:T(8,128)(2,1)S(1)}, u32[]{:S(2)}, u32[]{:S(2)}) collective-permute-start(bf16[128,2560]{1,0:T(8,128)(2,1)S(1)} %get-tuple-element.44), channel_id=1, source_target_pairs={{0,3},{1,0},{2,1},{3,2},{4,7},{5,4},{6,5},{7,6},{8,11},{9,8},{10,9... | collective-permute-start | bytes 1966088 | tf_op jit(solution)/shard_map/ppermute | solution.py:268
  57.7 0.5 collective-permute-start.14
  58.2 4.2 %block_terms.7 = (f32[128,2560]{1,0:T(8,128)S(1)}, f32[128,2560]{1,0:T(8,128)S(1)}, bf16[8192,256]{1,0:T(8,128)(2,1)S(1)}, bf16[640,5120]{1,0:T(8,128)(2,1)S(1)}) custom-call(s32[4,16]{1,0:T(4,128)S(1)} %copy-done.5, bf16[512,640]{1,0:T(8,128)(2,1)S(1)} %get-tuple-element.28.q_ref, ...), custom_call_target="tpu_custom_call", output_to_operand_aliasing={{2}: (2, {}), {3}: (3, {})} | custom-call | flops 1048576 | bytes 1048576 | tf_op jit(solution)/shard_map/block_terms/pallas_call | solution.py:227
  62.4 1.1 %collective-permute-done.15 = bf16[128,2560]{1,0:T(8,128)(2,1)S(1)} collective-permute-done((bf16[128,2560]{1,0:T(8,128)(2,1)S(1)}, bf16[128,2560]{1,0:T(8,128)(2,1)S(1)}, u32[]{:S(2)}, u32[]{:S(2)}) %collective-permute-start.15) | collective-permute-done | bytes 655392 | tf_op jit(solution)/shard_map/ppermute | solution.py:268
  64.1 3.0 %collective-permute-start.18 = (bf16[128,2560]{1,0:T(8,128)(2,1)S(1)}, bf16[128,2560]{1,0:T(8,128)(2,1)S(1)}, u32[]{:S(2)}, u32[]{:S(2)}) collective-permute-start(bf16[128,2560]{1,0:T(8,128)(2,1)S(1)} %add.15), channel_id=1, source_target_pairs={{0,3},{1,0},{2,1},{3,2},{4,7},{5,4},{6,5},{7,6},{8,11},{9,8},{10,9... | collective-permute-start | bytes 1966088 | tf_op jit(solution)/shard_map/ppermute | solution.py:268
  67.1 10.7 %collective-permute-done.13 = bf16[128,2560]{1,0:T(8,128)(2,1)S(1)} collective-permute-done((bf16[128,2560]{1,0:T(8,128)(2,1)S(1)}, bf16[128,2560]{1,0:T(8,128)(2,1)S(1)}, u32[]{:S(2)}, u32[]{:S(2)}) %collective-permute-start.13) | collective-permute-done | bytes 655392 | tf_op jit(solution)/shard_map/ppermute | solution.py:268
  78.1 12.6 %collective-permute-done.16.u_ref = bf16[128,2560]{1,0:T(8,128)(2,1)S(1)} collective-permute-done((bf16[128,2560]{1,0:T(8,128)(2,1)S(1)}, bf16[128,2560]{1,0:T(8,128)(2,1)S(1)}, u32[]{:S(2)}, u32[]{:S(2)}) %collective-permute-start.16) | collective-permute-done | bytes 655392 | tf_op jit(solution)/shard_map/ppermute | solution.py:268
  90.7 2.4 %final_norm.1 = bf16[128,5120]{1,0:T(8,128)(2,1)} custom-call(f32[128,2560]{1,0:T(8,128)S(1)} %convert_add_fusion.1.b1_ref, f32[128,2560]{1,0:T(8,128)S(1)} %convert_add_fusion.b2_ref, bf16[128,2560]{1,0:T(8,128)(2,1)S(1)} %collective-permute-done.16.u_ref, bf16[128,2560]{1,0:T(8,128)(2,1)S(1)} %collective-permute-done.18.v_ref, f32[1,5120]{1,0:T(1,128)S(1)} %bitcast.1, ...), custom_call_target="tpu_custom_call" | custom-call | tf_op jit(solution)/shard_map/final_norm/pallas_call | solution.py:253
  (41 shorter events, 1.9 us)
Async XLA Ops:
  0.0 13.1 %copy-start = (bf16[512,5120]{1,0:T(8,128)(2,1)S(1)}, bf16[512,5120]{1,0:T(8,128)(2,1)}, u32[]{:S(2)}) copy-start(bf16[512,5120]{1,0:T(8,128)(2,1)} %x_ref.3) | copy-start | bytes 15728644
  5.6 16.9 %collective-permute-start.3 = (bf16[512,256]{1,0:T(8,128)(2,1)}, bf16[512,256]{1,0:T(8,128)(2,1)S(1)}, u32[]{:S(2)}, u32[]{:S(2)}) collective-permute-start(bf16[512,256]{1,0:T(8,128)(2,1)} %kv_project.1.refs_0_), channel_id=1, source_target_pairs={{0,16},{8,24},{16,32},{24,40},{32,48},{40,56},{48,0},{56,8},{1,17}... | collective-permute-start | bytes 786440 | tf_op jit(solution)/shard_map/ppermute | solution.py:277
  7.6 14.9 %collective-permute-start.2 = (bf16[512,256]{1,0:T(8,128)(2,1)}, bf16[512,256]{1,0:T(8,128)(2,1)S(1)}, u32[]{:S(2)}, u32[]{:S(2)}) collective-permute-start(bf16[512,256]{1,0:T(8,128)(2,1)} %kv_project.1.refs_0_), channel_id=1, source_target_pairs={{0,48},{8,56},{16,0},{24,8},{32,16},{40,24},{48,32},{56,40},{1,49}... | collective-permute-start | bytes 786440 | tf_op jit(solution)/shard_map/ppermute | solution.py:277
  9.8 12.7 %collective-permute-start.1 = (bf16[512,256]{1,0:T(8,128)(2,1)}, bf16[512,256]{1,0:T(8,128)(2,1)S(1)}, u32[]{:S(2)}, u32[]{:S(2)}) collective-permute-start(bf16[512,256]{1,0:T(8,128)(2,1)} %kv_project.1.refs_0_), channel_id=1, source_target_pairs={{0,8},{8,0},{16,24},{24,16},{32,40},{40,32},{48,56},{56,48},{1,9},... | collective-permute-start | bytes 786440 | tf_op jit(solution)/shard_map/ppermute | solution.py:277
  10.6 13.8 %collective-permute-start = (bf16[512,256]{1,0:T(8,128)(2,1)}, bf16[512,256]{1,0:T(8,128)(2,1)S(1)}, u32[]{:S(2)}, u32[]{:S(2)}) collective-permute-start(bf16[512,256]{1,0:T(8,128)(2,1)} %kv_project.1.refs_0_), channel_id=1, source_target_pairs={{0,40},{8,32},{16,56},{24,48},{32,8},{40,0},{48,24},{56,16},{1,41}... | collective-permute-start | bytes 786440 | tf_op jit(solution)/shard_map/ppermute | solution.py:277
  13.1 14.8 %collective-permute-start.6 = (bf16[512,256]{1,0:T(8,128)(2,1)}, bf16[512,256]{1,0:T(8,128)(2,1)S(1)}, u32[]{:S(2)}, u32[]{:S(2)}) collective-permute-start(bf16[512,256]{1,0:T(8,128)(2,1)} %kv_project.1.refs_0_), channel_id=1, source_target_pairs={{0,4},{4,0},{1,5},{5,1},{2,6},{6,2},{3,7},{7,3},{8,12},{12,8},{9,1... | collective-permute-start | bytes 786440 | tf_op jit(solution)/shard_map/ppermute | solution.py:268
  13.1 2.9 %copy-start.1 = (bf16[5120,640]{1,0:T(8,128)(2,1)S(1)}, bf16[5120,640]{1,0:T(8,128)(2,1)}, u32[]{:S(2)}) copy-start(bf16[5120,640]{1,0:T(8,128)(2,1)} %w_ref.1) | copy-start | bytes 19660804
  15.9 12.5 %copy-start.2 = (bf16[640,5120]{1,0:T(8,128)(2,1)S(1)}, bf16[640,5120]{1,0:T(8,128)(2,1)}, u32[]{:S(2)}) copy-start(bf16[640,5120]{1,0:T(8,128)(2,1)} %refs_0_.1) | copy-start | bytes 19660804
  24.4 4.0 %collective-permute-start.10 = (bf16[512,256]{1,0:T(8,128)(2,1)S(1)}, bf16[512,256]{1,0:T(8,128)(2,1)S(1)}, u32[]{:S(2)}, u32[]{:S(2)}) collective-permute-start(bf16[512,256]{1,0:T(8,128)(2,1)S(1)} %get-tuple-element.32.refs_8_), channel_id=1, source_target_pairs={{0,4},{4,0},{1,5},{5,1},{2,6},{6,2},{3,7},{7,3},{8,12},{12,8},{9,1... | collective-permute-start | bytes 786440 | tf_op jit(solution)/shard_map/ppermute | solution.py:268
  24.5 12.8 %collective-permute-start.5 = (bf16[768,256]{1,0:T(8,128)(2,1)S(1)}, bf16[768,256]{1,0:T(8,128)(2,1)S(1)}, u32[]{:S(2)}, u32[]{:S(2)}) collective-permute-start(bf16[768,256]{1,0:T(8,128)(2,1)S(1)} %get-tuple-element.51), channel_id=1, source_target_pairs={{0,16},{8,24},{16,32},{24,40},{32,48},{40,56},{48,0},{56,8},{1,17}... | collective-permute-start | bytes 1179656 | tf_op jit(solution)/shard_map/ppermute | solution.py:277
  25.6 4.5 %copy-start.4 = (bf16[512,256]{1,0:T(8,128)(2,1)S(1)}, bf16[512,256]{1,0:T(8,128)(2,1)}, u32[]{:S(2)}) copy-start(bf16[512,256]{1,0:T(8,128)(2,1)} %kv_project.1.refs_0_) | copy-start | bytes 786436
  25.6 11.7 %collective-permute-start.4 = (bf16[768,256]{1,0:T(8,128)(2,1)S(1)}, bf16[768,256]{1,0:T(8,128)(2,1)S(1)}, u32[]{:S(2)}, u32[]{:S(2)}) collective-permute-start(bf16[768,256]{1,0:T(8,128)(2,1)S(1)} %get-tuple-element.52), channel_id=1, source_target_pairs={{0,48},{8,56},{16,0},{24,8},{32,16},{40,24},{48,32},{56,40},{1,49}... | collective-permute-start | bytes 1179656 | tf_op jit(solution)/shard_map/ppermute | solution.py:277
  27.9 1.5 %collective-permute-start.8 = (bf16[512,256]{1,0:T(8,128)(2,1)S(1)}, bf16[512,256]{1,0:T(8,128)(2,1)S(1)}, u32[]{:S(2)}, u32[]{:S(2)}) collective-permute-start(bf16[512,256]{1,0:T(8,128)(2,1)S(1)} %get-tuple-element.30.refs_4_), channel_id=1, source_target_pairs={{0,4},{4,0},{1,5},{5,1},{2,6},{6,2},{3,7},{7,3},{8,12},{12,8},{9,1... | collective-permute-start | bytes 786440 | tf_op jit(solution)/shard_map/ppermute | solution.py:268
  27.9 1.9 %collective-permute-start.9 = (bf16[512,256]{1,0:T(8,128)(2,1)S(1)}, bf16[512,256]{1,0:T(8,128)(2,1)S(1)}, u32[]{:S(2)}, u32[]{:S(2)}) collective-permute-start(bf16[512,256]{1,0:T(8,128)(2,1)S(1)} %get-tuple-element.31.refs_6_), channel_id=1, source_target_pairs={{0,4},{4,0},{1,5},{5,1},{2,6},{6,2},{3,7},{7,3},{8,12},{12,8},{9,1... | collective-permute-start | bytes 786440 | tf_op jit(solution)/shard_map/ppermute | solution.py:268
  28.4 1.8 %collective-permute-start.7 = (bf16[512,256]{1,0:T(8,128)(2,1)S(1)}, bf16[512,256]{1,0:T(8,128)(2,1)S(1)}, u32[]{:S(2)}, u32[]{:S(2)}) collective-permute-start(bf16[512,256]{1,0:T(8,128)(2,1)S(1)} %get-tuple-element.29.refs_2_.refs_1_), channel_id=1, source_target_pairs={{0,4},{4,0},{1,5},{5,1},{2,6},{6,2},{3,7},{7,3},{8,12},{12,8},{9,1... | collective-permute-start | bytes 786440 | tf_op jit(solution)/shard_map/ppermute | solution.py:268
  37.3 1.7 %collective-permute-start.11 = (bf16[768,256]{1,0:T(8,128)(2,1)S(1)}, bf16[768,256]{1,0:T(8,128)(2,1)S(1)}, u32[]{:S(2)}, u32[]{:S(2)}) collective-permute-start(bf16[768,256]{1,0:T(8,128)(2,1)S(1)} %get-tuple-element.34.refs_1_), channel_id=1, source_target_pairs={{0,4},{4,0},{1,5},{5,1},{2,6},{6,2},{3,7},{7,3},{8,12},{12,8},{9,1... | collective-permute-start | bytes 1179656 | tf_op jit(solution)/shard_map/ppermute | solution.py:268
  37.3 2.3 %collective-permute-start.12 = (bf16[768,256]{1,0:T(8,128)(2,1)S(1)}, bf16[768,256]{1,0:T(8,128)(2,1)S(1)}, u32[]{:S(2)}, u32[]{:S(2)}) collective-permute-start(bf16[768,256]{1,0:T(8,128)(2,1)S(1)} %get-tuple-element.35.refs_3_), channel_id=1, source_target_pairs={{0,4},{4,0},{1,5},{5,1},{2,6},{6,2},{3,7},{7,3},{8,12},{12,8},{9,1... | collective-permute-start | bytes 1179656 | tf_op jit(solution)/shard_map/ppermute | solution.py:268
  39.6 0.8 copy-start.5
  44.6 18.9 %collective-permute-start.15 = (bf16[128,2560]{1,0:T(8,128)(2,1)S(1)}, bf16[128,2560]{1,0:T(8,128)(2,1)S(1)}, u32[]{:S(2)}, u32[]{:S(2)}) collective-permute-start(bf16[128,2560]{1,0:T(8,128)(2,1)S(1)} %get-tuple-element.48), channel_id=1, source_target_pairs={{0,1},{1,2},{2,3},{3,0},{4,5},{5,6},{6,7},{7,4},{8,9},{9,10},{10,1... | collective-permute-start | bytes 1966088 | tf_op jit(solution)/shard_map/ppermute | solution.py:268
  46.1 17.8 %collective-permute-start.17 = (bf16[128,2560]{1,0:T(8,128)(2,1)S(1)}, bf16[128,2560]{1,0:T(8,128)(2,1)S(1)}, u32[]{:S(2)}, u32[]{:S(2)}) collective-permute-start(bf16[128,2560]{1,0:T(8,128)(2,1)S(1)} %get-tuple-element.50), channel_id=1, source_target_pairs={{0,3},{1,0},{2,1},{3,2},{4,7},{5,4},{6,5},{7,6},{8,11},{9,8},{10,9... | collective-permute-start | bytes 1966088 | tf_op jit(solution)/shard_map/ppermute | solution.py:268
  52.0 6.2 %copy-start.3 = (bf16[128,5120]{1,0:T(8,128)(2,1)S(1)}, bf16[128,5120]{1,0:T(8,128)(2,1)}, u32[]{:S(2)}) copy-start(bf16[128,5120]{1,0:T(8,128)(2,1)} %rest_0_.1) | copy-start | bytes 3932164
  56.1 21.7 %collective-permute-start.13 = (bf16[128,2560]{1,0:T(8,128)(2,1)S(1)}, bf16[128,2560]{1,0:T(8,128)(2,1)S(1)}, u32[]{:S(2)}, u32[]{:S(2)}) collective-permute-start(bf16[128,2560]{1,0:T(8,128)(2,1)S(1)} %get-tuple-element.44), channel_id=1, source_target_pairs={{0,3},{1,0},{2,1},{3,2},{4,7},{5,4},{6,5},{7,6},{8,11},{9,8},{10,9... | collective-permute-start | bytes 1966088 | tf_op jit(solution)/shard_map/ppermute | solution.py:268
  57.7 20.2 %collective-permute-start.14 = (bf16[128,2560]{1,0:T(8,128)(2,1)S(1)}, bf16[128,2560]{1,0:T(8,128)(2,1)S(1)}, u32[]{:S(2)}, u32[]{:S(2)}) collective-permute-start(bf16[128,2560]{1,0:T(8,128)(2,1)S(1)} %get-tuple-element.46), channel_id=1, source_target_pairs={{0,1},{1,2},{2,3},{3,0},{4,5},{5,6},{6,7},{7,4},{8,9},{9,10},{10,1... | collective-permute-start | bytes 1966088 | tf_op jit(solution)/shard_map/ppermute | solution.py:268
  63.6 27.1 %collective-permute-start.16 = (bf16[128,2560]{1,0:T(8,128)(2,1)S(1)}, bf16[128,2560]{1,0:T(8,128)(2,1)S(1)}, u32[]{:S(2)}, u32[]{:S(2)}) collective-permute-start(bf16[128,2560]{1,0:T(8,128)(2,1)S(1)} %add.14), channel_id=1, source_target_pairs={{0,1},{1,2},{2,3},{3,0},{4,5},{5,6},{6,7},{7,4},{8,9},{9,10},{10,1... | collective-permute-start | bytes 1966088 | tf_op jit(solution)/shard_map/ppermute | solution.py:268
  64.0 26.8 %copy-start.6 = (f32[5120]{0:T(1024)S(1)}, f32[5120]{0:T(1024)}, u32[]{:S(2)}) copy-start(f32[5120]{0:T(1024)} %param.15) | copy-start | bytes 61444
  64.0 26.8 %copy-start.7 = (s32[4]{0:T(128)S(1)}, s32[4]{0:T(128)}, u32[]{:S(2)}) copy-start(s32[4]{0:T(128)} %keep_ref.1) | copy-start | bytes 52
  64.1 26.6 %collective-permute-start.18 = (bf16[128,2560]{1,0:T(8,128)(2,1)S(1)}, bf16[128,2560]{1,0:T(8,128)(2,1)S(1)}, u32[]{:S(2)}, u32[]{:S(2)}) collective-permute-start(bf16[128,2560]{1,0:T(8,128)(2,1)S(1)} %add.15), channel_id=1, source_target_pairs={{0,3},{1,0},{2,1},{3,2},{4,7},{5,4},{6,5},{7,6},{8,11},{9,8},{10,9... | collective-permute-start | bytes 1966088 | tf_op jit(solution)/shard_map/ppermute | solution.py:268

commit v7 on v6

--- a/solution.py
+++ b/solution.py
@@ -66,7 +66,7 @@
     )(x, wk, wv)
 
 
-def q_kernel(x_ref, w_ref, o_ref, wbuf, sems):
+def q_kernel(x_ref, w_ref, after_ref, o_ref, wbuf, sems):
     parts, tile, _ = wbuf.shape
     copies = [
         pltpu.make_async_copy(w_ref.at[pl.ds(k * tile, tile)], wbuf.at[k], sems.at[k])
@@ -82,14 +82,14 @@
     o_ref[...] = total.astype(BF16)
 
 
-def q_project(x, w):
+def q_project(x, w, after):
     parts = 5
     vmem = pl.BlockSpec(memory_space=pltpu.VMEM)
     return pl.pallas_call(
         q_kernel,
         name="q_project",
         out_shape=jax.ShapeDtypeStruct((x.shape[0], w.shape[1]), BF16),
-        in_specs=[vmem, pl.BlockSpec(memory_space=pltpu.HBM)],
+        in_specs=[vmem, pl.BlockSpec(memory_space=pltpu.HBM), pl.BlockSpec(memory_space=pl.ANY)],
         out_specs=vmem,
         scratch_shapes=[
             pltpu.VMEM((parts, w.shape[0] // parts, w.shape[1]), BF16),
@@ -97,7 +97,7 @@
         ],
         compiler_params=pltpu.CompilerParams(vmem_limit_bytes=20 << 20),
         cost_estimate=SMALL_COST,
-    )(x, w)
+    )(x, w, after)
 
 
 def tie(values):
@@ -289,9 +289,9 @@
     y = fetch(own, 0, 1)
     up = fetch(own, 1, 0)
     down = fetch(own, 3, 0)
-    y_far, y, up, down, first = tie((y_far, y, up, down, first()))
     more_up = fetch(jnp.concatenate([y, up[:half]], axis=0), 1, 0)
     more_down = fetch(jnp.concatenate([y, down[half:]], axis=0), 3, 0)
+    y_far, first, second = tie((y_far, first(y), second(y)))
     early = (
         both(own, (0, 0, 0, rows))
         + both(y, (0, 1, 0, rows))
@@ -300,7 +300,9 @@
         + both(y_far, (2, 1, 0, rows))
     )
     shape = (16 * rows, own.shape[1])
-    more_up, more_down, base, second = tie((more_up, more_down, collect(early, shape), second(y)))
+    more_up, more_down, base, first, second = tie(
+        (more_up, more_down, collect(early, shape), first, second)
+    )
     late = both(more_up, (1, 1, 0, rows), (2, 0, 0, half)) + both(
         more_down, (3, 1, 0, rows), (2, 0, half, half)
     )
@@ -311,7 +313,7 @@
     kv_own = kv_project(activations, w_key, w_value)
     kv, queries, w_held = gather_blocks(
         kv_own,
-        lambda: q_project(activations, w_query),
+        lambda there: q_project(activations, w_query, there),
         lambda there: collect([(w_out, ((0, 0, w_out.shape[0]),))], w_out.shape, None, (there,)),
     )
 

time: 93.6 us -> 91.6 us (0.979)
  waiting for transfers between devices: 36 us -> 33.9 us
    ppermute x6, waiting for transfers between devices: 8.69 us -> 6.08 us  [fetch(): return lax.ppermute(x, ('z', 'y'), pairs)]
  transfers between devices with their start and end apart: 19 -> 19, of which waited for: 10 -> 11; matrix products, arithmetic and copies ran while one was open for 1% -> 1% of each run, Pallas kernels for 21% -> 22%
where the time goes in v7:
time: 91.6 us; the launch traced here: 91.2 us
  waiting for transfers between devices  33.9 us (37%)
  Pallas kernels  32.6 us (36%)
  starting transfers between devices  20.9 us (23%)
  local copies, waits for them, and re-layouts  2.91 us (3%)
    ppermute x13, waiting for transfers between devices, shift(): lax.ppermute(x, axis, ring({'y': 2, 'core': 2, 'z': 4, 'tp': 4}[axis], s))  27.8 us
    pallas_call x4, Pallas kernels, block_terms(): pl.pallas_call(functools.partial(block_kernel, turn), name='block_terms',...  16.4 us
    ppermute x6, starting transfers between devices, fetch(): return lax.ppermute(x, ('z', 'y'), pairs)  10.7 us
    ppermute x13, starting transfers between devices, shift(): lax.ppermute(x, axis, ring({'y': 2, 'core': 2, 'z': 4, 'tp': 4}[axis], s))  10.1 us
    pallas_call x1, Pallas kernels, q_project(): pl.pallas_call(q_kernel, name='q_project', out_shape=jax.ShapeDtypeStruct...  6.6 us
    ppermute x6, waiting for transfers between devices, fetch(): return lax.ppermute(x, ('z', 'y'), pairs)  6.08 us
    pallas_call x1, Pallas kernels, kv_project(): pl.pallas_call(kv_kernel, name='kv_project', out_shape=jax.ShapeDtypeStru...  5.62 us
    unnamed x16, local copies, waits for them, and re-layouts  2.89 us
  transfers between devices with their start and end apart: 19, of which 11 were waited for; matrix products, arithmetic and copies ran while one was open for 1% of the time, Pallas kernels for 22%

profile of v7, /device:TPU:24, one launch (start us, length us, event | category | flops | bytes accessed | tf_op | source)
XLA Modules:
  0.0 91.2 jit_solution(3189804464519747776)
XLA Ops:
  0.0 5.6 %kv_project.1.refs_0_ = bf16[512,256]{1,0:T(8,128)(2,1)} custom-call(bf16[512,5120]{1,0:T(8,128)(2,1)} %x_ref.3, bf16[5120,128]{1,0:T(8,128)(2,1)} %wk_ref.1, bf16[5120,128]{1,0:T(8,128)(2,1)} %wv_ref.1), custom_call_target="tpu_custom_call" | custom-call | flops 1048576 | bytes 1048576 | tf_op jit(solution)/shard_map/kv_project/pallas_call | solution.py:53
  5.6 2.0 %collective-permute-start.3 = (bf16[512,256]{1,0:T(8,128)(2,1)}, bf16[512,256]{1,0:T(8,128)(2,1)S(1)}, u32[]{:S(2)}, u32[]{:S(2)}) collective-permute-start(bf16[512,256]{1,0:T(8,128)(2,1)} %kv_project.1.refs_0_), channel_id=1, source_target_pairs={{0,16},{8,24},{16,32},{24,40},{32,48},{40,56},{48,0},{56,8},{1,17}... | collective-permute-start | bytes 786440 | tf_op jit(solution)/shard_map/ppermute | solution.py:277
  7.6 2.2 %collective-permute-start.1 = (bf16[512,256]{1,0:T(8,128)(2,1)}, bf16[512,256]{1,0:T(8,128)(2,1)S(1)}, u32[]{:S(2)}, u32[]{:S(2)}) collective-permute-start(bf16[512,256]{1,0:T(8,128)(2,1)} %kv_project.1.refs_0_), channel_id=1, source_target_pairs={{0,48},{8,56},{16,0},{24,8},{32,16},{40,24},{48,32},{56,40},{1,49}... | collective-permute-start | bytes 786440 | tf_op jit(solution)/shard_map/ppermute | solution.py:277
  9.8 0.7 collective-permute-start
  10.6 2.5 %collective-permute-start.9 = (bf16[512,256]{1,0:T(8,128)(2,1)}, bf16[512,256]{1,0:T(8,128)(2,1)S(1)}, u32[]{:S(2)}, u32[]{:S(2)}) collective-permute-start(bf16[512,256]{1,0:T(8,128)(2,1)} %kv_project.1.refs_0_), channel_id=1, source_target_pairs={{0,40},{8,32},{16,56},{24,48},{32,8},{40,0},{48,24},{56,16},{1,41}... | collective-permute-start | bytes 786440 | tf_op jit(solution)/shard_map/ppermute | solution.py:277
  13.1 3.2 %collective-permute-done.3.refs_6_ = bf16[512,256]{1,0:T(8,128)(2,1)S(1)} collective-permute-done((bf16[512,256]{1,0:T(8,128)(2,1)}, bf16[512,256]{1,0:T(8,128)(2,1)S(1)}, u32[]{:S(2)}, u32[]{:S(2)}) %collective-permute-start.3) | collective-permute-done | bytes 262176 | tf_op jit(solution)/shard_map/ppermute | solution.py:277
  16.4 0.4 collective-permute-done.1.refs_4_
  16.8 2.5 %collective-permute-done.after_ref.refs_1_.refs_2_ = bf16[512,256]{1,0:T(8,128)(2,1)S(1)} collective-permute-done((bf16[512,256]{1,0:T(8,128)(2,1)}, bf16[512,256]{1,0:T(8,128)(2,1)S(1)}, u32[]{:S(2)}, u32[]{:S(2)}) %collective-permute-start) | collective-permute-done | bytes 262176 | tf_op jit(solution)/shard_map/ppermute | solution.py:277
  19.4 3.2 %collective-permute-start.2 = (bf16[768,256]{1,0:T(8,128)(2,1)S(1)}, bf16[768,256]{1,0:T(8,128)(2,1)S(1)}, u32[]{:S(2)}, u32[]{:S(2)}) collective-permute-start(bf16[768,256]{1,0:T(8,128)(2,1)S(1)} %get-tuple-element.50), channel_id=1, source_target_pairs={{0,48},{8,56},{16,0},{24,8},{32,16},{40,24},{48,32},{56,40},{1,49}... | collective-permute-start | bytes 1179656 | tf_op jit(solution)/shard_map/ppermute | solution.py:277
  22.6 2.9 %copy-done.1 = bf16[5120,640]{1,0:T(8,128)(2,1)S(1)} copy-done((bf16[5120,640]{1,0:T(8,128)(2,1)S(1)}, bf16[5120,640]{1,0:T(8,128)(2,1)}, u32[]{:S(2)}) %copy-start.1) | copy-done | bytes 6553624
  25.5 6.6 %q_project.1.refs_1_ = bf16[512,640]{1,0:T(8,128)(2,1)S(1)} custom-call(bf16[512,5120]{1,0:T(8,128)(2,1)S(1)} %copy-done, bf16[5120,640]{1,0:T(8,128)(2,1)S(1)} %copy-done.1, bf16[512,256]{1,0:T(8,128)(2,1)S(1)} %collective-permute-done.after_ref.refs_1_.refs_2_), custom_call_target="tpu_custom_call" | custom-call | flops 1048576 | bytes 1048576 | tf_op jit(solution)/shard_map/q_project/pallas_call | solution.py:88
  32.1 0.4 collect.3.refs_2_
  32.7 0.5 collective-permute-start.6
  33.3 0.9 collective-permute-done.7.refs_5_
  34.2 0.4 collective-permute-done.6.refs_3_
  34.6 0.4 collective-permute-done.10.refs_9_
  35.9 1.2 %collective-permute-done.11.refs_2_ = bf16[768,256]{1,0:T(8,128)(2,1)S(1)} collective-permute-done((bf16[768,256]{1,0:T(8,128)(2,1)S(1)}, bf16[768,256]{1,0:T(8,128)(2,1)S(1)}, u32[]{:S(2)}, u32[]{:S(2)}) %collective-permute-start.11) | collective-permute-done | bytes 393248 | tf_op jit(solution)/shard_map/ppermute | solution.py:268
  37.1 0.6 collective-permute-done.12.refs_4_
  37.6 0.8 collect.5.kv_ref
  38.5 4.1 %block_terms.4 = (bf16[128,2560]{1,0:T(8,128)(2,1)S(1)}, bf16[128,2560]{1,0:T(8,128)(2,1)S(1)}, bf16[8192,256]{1,0:T(8,128)(2,1)S(1)}, bf16[640,5120]{1,0:T(8,128)(2,1)S(1)}) custom-call(s32[4,16]{1,0:T(4,128)S(1)} %copy-done.5, bf16[512,640]{1,0:T(8,128)(2,1)S(1)} %get-tuple-element.30.q_ref, ...), custom_call_target="tpu_custom_call", output_to_operand_aliasing={{2}: (2, {}), {3}: (3, {})} | custom-call | flops 1048576 | bytes 1048576 | tf_op jit(solution)/shard_map/block_terms/pallas_call | solution.py:227
  42.6 1.6 %collective-permute-start.15 = (bf16[128,2560]{1,0:T(8,128)(2,1)S(1)}, bf16[128,2560]{1,0:T(8,128)(2,1)S(1)}, u32[]{:S(2)}, u32[]{:S(2)}) collective-permute-start(bf16[128,2560]{1,0:T(8,128)(2,1)S(1)} %get-tuple-element.46), channel_id=1, source_target_pairs={{0,1},{1,2},{2,3},{3,0},{4,5},{5,6},{6,7},{7,4},{8,9},{9,10},{10,1... | collective-permute-start | bytes 1966088 | tf_op jit(solution)/shard_map/ppermute | solution.py:268
  44.2 1.7 %collective-permute-start.17 = (bf16[128,2560]{1,0:T(8,128)(2,1)S(1)}, bf16[128,2560]{1,0:T(8,128)(2,1)S(1)}, u32[]{:S(2)}, u32[]{:S(2)}) collective-permute-start(bf16[128,2560]{1,0:T(8,128)(2,1)S(1)} %get-tuple-element.48), channel_id=1, source_target_pairs={{0,3},{1,0},{2,1},{3,2},{4,7},{5,4},{6,5},{7,6},{8,11},{9,8},{10,9... | collective-permute-start | bytes 1966088 | tf_op jit(solution)/shard_map/ppermute | solution.py:268
  45.9 4.1 %block_terms.5 = (bf16[128,2560]{1,0:T(8,128)(2,1)S(1)}, bf16[128,2560]{1,0:T(8,128)(2,1)S(1)}, bf16[8192,256]{1,0:T(8,128)(2,1)S(1)}, bf16[640,5120]{1,0:T(8,128)(2,1)S(1)}) custom-call(s32[4,16]{1,0:T(4,128)S(1)} %copy-done.5, bf16[512,640]{1,0:T(8,128)(2,1)S(1)} %get-tuple-element.30.q_ref, ...), custom_call_target="tpu_custom_call", output_to_operand_aliasing={{2}: (2, {}), {3}: (3, {})} | custom-call | flops 1048576 | bytes 1048576 | tf_op jit(solution)/shard_map/block_terms/pallas_call | solution.py:227
  50.0 4.1 %block_terms.6 = (bf16[128,2560]{1,0:T(8,128)(2,1)S(1)}, bf16[128,2560]{1,0:T(8,128)(2,1)S(1)}, bf16[8192,256]{1,0:T(8,128)(2,1)S(1)}, bf16[640,5120]{1,0:T(8,128)(2,1)S(1)}) custom-call(s32[4,16]{1,0:T(4,128)S(1)} %copy-done.5, bf16[512,640]{1,0:T(8,128)(2,1)S(1)} %get-tuple-element.30.q_ref, ...), custom_call_target="tpu_custom_call", output_to_operand_aliasing={{2}: (2, {}), {3}: (3, {})} | custom-call | flops 1048576 | bytes 1048576 | tf_op jit(solution)/shard_map/block_terms/pallas_call | solution.py:227
  54.1 1.6 %collective-permute-start.13 = (bf16[128,2560]{1,0:T(8,128)(2,1)S(1)}, bf16[128,2560]{1,0:T(8,128)(2,1)S(1)}, u32[]{:S(2)}, u32[]{:S(2)}) collective-permute-start(bf16[128,2560]{1,0:T(8,128)(2,1)S(1)} %get-tuple-element.42), channel_id=1, source_target_pairs={{0,3},{1,0},{2,1},{3,2},{4,7},{5,4},{6,5},{7,6},{8,11},{9,8},{10,9... | collective-permute-start | bytes 1966088 | tf_op jit(solution)/shard_map/ppermute | solution.py:268
  55.7 0.5 collective-permute-start.14
  56.2 4.2 %block_terms.7 = (f32[128,2560]{1,0:T(8,128)S(1)}, f32[128,2560]{1,0:T(8,128)S(1)}, bf16[8192,256]{1,0:T(8,128)(2,1)S(1)}, bf16[640,5120]{1,0:T(8,128)(2,1)S(1)}) custom-call(s32[4,16]{1,0:T(4,128)S(1)} %copy-done.5, bf16[512,640]{1,0:T(8,128)(2,1)S(1)} %get-tuple-element.30.q_ref, ...), custom_call_target="tpu_custom_call", output_to_operand_aliasing={{2}: (2, {}), {3}: (3, {})} | custom-call | flops 1048576 | bytes 1048576 | tf_op jit(solution)/shard_map/block_terms/pallas_call | solution.py:227
  60.4 1.1 %collective-permute-done.15 = bf16[128,2560]{1,0:T(8,128)(2,1)S(1)} collective-permute-done((bf16[128,2560]{1,0:T(8,128)(2,1)S(1)}, bf16[128,2560]{1,0:T(8,128)(2,1)S(1)}, u32[]{:S(2)}, u32[]{:S(2)}) %collective-permute-start.15) | collective-permute-done | bytes 655392 | tf_op jit(solution)/shard_map/ppermute | solution.py:268
  62.1 3.0 %collective-permute-start.18 = (bf16[128,2560]{1,0:T(8,128)(2,1)S(1)}, bf16[128,2560]{1,0:T(8,128)(2,1)S(1)}, u32[]{:S(2)}, u32[]{:S(2)}) collective-permute-start(bf16[128,2560]{1,0:T(8,128)(2,1)S(1)} %add.15), channel_id=1, source_target_pairs={{0,3},{1,0},{2,1},{3,2},{4,7},{5,4},{6,5},{7,6},{8,11},{9,8},{10,9... | collective-permute-start | bytes 1966088 | tf_op jit(solution)/shard_map/ppermute | solution.py:268
  65.2 10.7 %collective-permute-done.13 = bf16[128,2560]{1,0:T(8,128)(2,1)S(1)} collective-permute-done((bf16[128,2560]{1,0:T(8,128)(2,1)S(1)}, bf16[128,2560]{1,0:T(8,128)(2,1)S(1)}, u32[]{:S(2)}, u32[]{:S(2)}) %collective-permute-start.13) | collective-permute-done | bytes 655392 | tf_op jit(solution)/shard_map/ppermute | solution.py:268
  76.1 12.6 %collective-permute-done.16.u_ref = bf16[128,2560]{1,0:T(8,128)(2,1)S(1)} collective-permute-done((bf16[128,2560]{1,0:T(8,128)(2,1)S(1)}, bf16[128,2560]{1,0:T(8,128)(2,1)S(1)}, u32[]{:S(2)}, u32[]{:S(2)}) %collective-permute-start.16) | collective-permute-done | bytes 655392 | tf_op jit(solution)/shard_map/ppermute | solution.py:268
  88.8 2.4 %final_norm.1 = bf16[128,5120]{1,0:T(8,128)(2,1)} custom-call(f32[128,2560]{1,0:T(8,128)S(1)} %convert_add_fusion.1.b1_ref, f32[128,2560]{1,0:T(8,128)S(1)} %convert_add_fusion.b2_ref, bf16[128,2560]{1,0:T(8,128)(2,1)S(1)} %collective-permute-done.16.u_ref, bf16[128,2560]{1,0:T(8,128)(2,1)S(1)} %collective-permute-done.18.v_ref, f32[1,5120]{1,0:T(1,128)S(1)} %bitcast.1, ...), custom_call_target="tpu_custom_call" | custom-call | tf_op jit(solution)/shard_map/final_norm/pallas_call | solution.py:253
  (41 shorter events, 2.3 us)
Async XLA Ops:
  0.0 22.6 %copy-start = (bf16[512,5120]{1,0:T(8,128)(2,1)S(1)}, bf16[512,5120]{1,0:T(8,128)(2,1)}, u32[]{:S(2)}) copy-start(bf16[512,5120]{1,0:T(8,128)(2,1)} %x_ref.3) | copy-start | bytes 15728644
  5.6 10.6 %collective-permute-start.3 = (bf16[512,256]{1,0:T(8,128)(2,1)}, bf16[512,256]{1,0:T(8,128)(2,1)S(1)}, u32[]{:S(2)}, u32[]{:S(2)}) collective-permute-start(bf16[512,256]{1,0:T(8,128)(2,1)} %kv_project.1.refs_0_), channel_id=1, source_target_pairs={{0,16},{8,24},{16,32},{24,40},{32,48},{40,56},{48,0},{56,8},{1,17}... | collective-permute-start | bytes 786440 | tf_op jit(solution)/shard_map/ppermute | solution.py:277
  7.6 9.2 %collective-permute-start.1 = (bf16[512,256]{1,0:T(8,128)(2,1)}, bf16[512,256]{1,0:T(8,128)(2,1)S(1)}, u32[]{:S(2)}, u32[]{:S(2)}) collective-permute-start(bf16[512,256]{1,0:T(8,128)(2,1)} %kv_project.1.refs_0_), channel_id=1, source_target_pairs={{0,48},{8,56},{16,0},{24,8},{32,16},{40,24},{48,32},{56,40},{1,49}... | collective-permute-start | bytes 786440 | tf_op jit(solution)/shard_map/ppermute | solution.py:277
  9.8 9.4 %collective-permute-start = (bf16[512,256]{1,0:T(8,128)(2,1)}, bf16[512,256]{1,0:T(8,128)(2,1)S(1)}, u32[]{:S(2)}, u32[]{:S(2)}) collective-permute-start(bf16[512,256]{1,0:T(8,128)(2,1)} %kv_project.1.refs_0_), channel_id=1, source_target_pairs={{0,8},{8,0},{16,24},{24,16},{32,40},{40,32},{48,56},{56,48},{1,9},... | collective-permute-start | bytes 786440 | tf_op jit(solution)/shard_map/ppermute | solution.py:277
  10.6 22.0 %collective-permute-start.9 = (bf16[512,256]{1,0:T(8,128)(2,1)}, bf16[512,256]{1,0:T(8,128)(2,1)S(1)}, u32[]{:S(2)}, u32[]{:S(2)}) collective-permute-start(bf16[512,256]{1,0:T(8,128)(2,1)} %kv_project.1.refs_0_), channel_id=1, source_target_pairs={{0,40},{8,32},{16,56},{24,48},{32,8},{40,0},{48,24},{56,16},{1,41}... | collective-permute-start | bytes 786440 | tf_op jit(solution)/shard_map/ppermute | solution.py:277
  13.1 19.6 %collective-permute-start.5 = (bf16[512,256]{1,0:T(8,128)(2,1)}, bf16[512,256]{1,0:T(8,128)(2,1)S(1)}, u32[]{:S(2)}, u32[]{:S(2)}) collective-permute-start(bf16[512,256]{1,0:T(8,128)(2,1)} %kv_project.1.refs_0_), channel_id=1, source_target_pairs={{0,4},{4,0},{1,5},{5,1},{2,6},{6,2},{3,7},{7,3},{8,12},{12,8},{9,1... | collective-permute-start | bytes 786440 | tf_op jit(solution)/shard_map/ppermute | solution.py:268
  16.3 16.9 %collective-permute-start.8 = (bf16[512,256]{1,0:T(8,128)(2,1)S(1)}, bf16[512,256]{1,0:T(8,128)(2,1)S(1)}, u32[]{:S(2)}, u32[]{:S(2)}) collective-permute-start(bf16[512,256]{1,0:T(8,128)(2,1)S(1)} %collective-permute-done.3.refs_6_), channel_id=1, source_target_pairs={{0,4},{4,0},{1,5},{5,1},{2,6},{6,2},{3,7},{7,3},{8,12},{12,8},{9,1... | collective-permute-start | bytes 786440 | tf_op jit(solution)/shard_map/ppermute | solution.py:268
  19.3 15.9 %collective-permute-start.4 = (bf16[768,256]{1,0:T(8,128)(2,1)S(1)}, bf16[768,256]{1,0:T(8,128)(2,1)S(1)}, u32[]{:S(2)}, u32[]{:S(2)}) collective-permute-start(bf16[768,256]{1,0:T(8,128)(2,1)S(1)} %get-tuple-element.49), channel_id=1, source_target_pairs={{0,16},{8,24},{16,32},{24,40},{32,48},{40,56},{48,0},{56,8},{1,17}... | collective-permute-start | bytes 1179656 | tf_op jit(solution)/shard_map/ppermute | solution.py:277
  19.4 15.9 %collective-permute-start.2 = (bf16[768,256]{1,0:T(8,128)(2,1)S(1)}, bf16[768,256]{1,0:T(8,128)(2,1)S(1)}, u32[]{:S(2)}, u32[]{:S(2)}) collective-permute-start(bf16[768,256]{1,0:T(8,128)(2,1)S(1)} %get-tuple-element.50), channel_id=1, source_target_pairs={{0,48},{8,56},{16,0},{24,8},{32,16},{40,24},{48,32},{56,40},{1,49}... | collective-permute-start | bytes 1179656 | tf_op jit(solution)/shard_map/ppermute | solution.py:277
  22.6 2.9 %copy-start.1 = (bf16[5120,640]{1,0:T(8,128)(2,1)S(1)}, bf16[5120,640]{1,0:T(8,128)(2,1)}, u32[]{:S(2)}) copy-start(bf16[5120,640]{1,0:T(8,128)(2,1)} %w_ref.1) | copy-start | bytes 19660804
  25.5 6.6 %copy-start.2 = (bf16[640,5120]{1,0:T(8,128)(2,1)S(1)}, bf16[640,5120]{1,0:T(8,128)(2,1)}, u32[]{:S(2)}) copy-start(bf16[640,5120]{1,0:T(8,128)(2,1)} %refs_0_.1) | copy-start | bytes 19660804
  32.6 2.4 %copy-start.4 = (bf16[512,256]{1,0:T(8,128)(2,1)S(1)}, bf16[512,256]{1,0:T(8,128)(2,1)}, u32[]{:S(2)}) copy-start(bf16[512,256]{1,0:T(8,128)(2,1)} %kv_project.1.refs_0_) | copy-start | bytes 786436
  32.6 1.6 %collective-permute-start.7 = (bf16[512,256]{1,0:T(8,128)(2,1)S(1)}, bf16[512,256]{1,0:T(8,128)(2,1)S(1)}, u32[]{:S(2)}, u32[]{:S(2)}) collective-permute-start(bf16[512,256]{1,0:T(8,128)(2,1)S(1)} %collective-permute-done.1.refs_4_), channel_id=1, source_target_pairs={{0,4},{4,0},{1,5},{5,1},{2,6},{6,2},{3,7},{7,3},{8,12},{12,8},{9,1... | collective-permute-start | bytes 786440 | tf_op jit(solution)/shard_map/ppermute | solution.py:268
  32.7 1.9 %collective-permute-start.6 = (bf16[512,256]{1,0:T(8,128)(2,1)S(1)}, bf16[512,256]{1,0:T(8,128)(2,1)S(1)}, u32[]{:S(2)}, u32[]{:S(2)}) collective-permute-start(bf16[512,256]{1,0:T(8,128)(2,1)S(1)} %collective-permute-done.after_ref.refs_1_.refs_2_), channel_id=1, source_target_pairs={{0,4},{4,0},{1,5},{5,1},{2,6},{6,2},{3,7},{7,3},{8,12},{12,8},{9,1... | collective-permute-start | bytes 786440 | tf_op jit(solution)/shard_map/ppermute | solution.py:268
  33.2 1.8 %collective-permute-start.10 = (bf16[512,256]{1,0:T(8,128)(2,1)S(1)}, bf16[512,256]{1,0:T(8,128)(2,1)S(1)}, u32[]{:S(2)}, u32[]{:S(2)}) collective-permute-start(bf16[512,256]{1,0:T(8,128)(2,1)S(1)} %get-tuple-element.27.refs_8_), channel_id=1, source_target_pairs={{0,4},{4,0},{1,5},{5,1},{2,6},{6,2},{3,7},{7,3},{8,12},{12,8},{9,1... | collective-permute-start | bytes 786440 | tf_op jit(solution)/shard_map/ppermute | solution.py:268
  35.3 1.8 %collective-permute-start.11 = (bf16[768,256]{1,0:T(8,128)(2,1)S(1)}, bf16[768,256]{1,0:T(8,128)(2,1)S(1)}, u32[]{:S(2)}, u32[]{:S(2)}) collective-permute-start(bf16[768,256]{1,0:T(8,128)(2,1)S(1)} %get-tuple-element.32.refs_1_), channel_id=1, source_target_pairs={{0,4},{4,0},{1,5},{5,1},{2,6},{6,2},{3,7},{7,3},{8,12},{12,8},{9,1... | collective-permute-start | bytes 1179656 | tf_op jit(solution)/shard_map/ppermute | solution.py:268
  35.5 2.1 %collective-permute-start.12 = (bf16[768,256]{1,0:T(8,128)(2,1)S(1)}, bf16[768,256]{1,0:T(8,128)(2,1)S(1)}, u32[]{:S(2)}, u32[]{:S(2)}) collective-permute-start(bf16[768,256]{1,0:T(8,128)(2,1)S(1)} %get-tuple-element.33.refs_3_), channel_id=1, source_target_pairs={{0,4},{4,0},{1,5},{5,1},{2,6},{6,2},{3,7},{7,3},{8,12},{12,8},{9,1... | collective-permute-start | bytes 1179656 | tf_op jit(solution)/shard_map/ppermute | solution.py:268
  37.6 0.8 copy-start.5
  42.6 18.9 %collective-permute-start.15 = (bf16[128,2560]{1,0:T(8,128)(2,1)S(1)}, bf16[128,2560]{1,0:T(8,128)(2,1)S(1)}, u32[]{:S(2)}, u32[]{:S(2)}) collective-permute-start(bf16[128,2560]{1,0:T(8,128)(2,1)S(1)} %get-tuple-element.46), channel_id=1, source_target_pairs={{0,1},{1,2},{2,3},{3,0},{4,5},{5,6},{6,7},{7,4},{8,9},{9,10},{10,1... | collective-permute-start | bytes 1966088 | tf_op jit(solution)/shard_map/ppermute | solution.py:268
  44.2 17.8 %collective-permute-start.17 = (bf16[128,2560]{1,0:T(8,128)(2,1)S(1)}, bf16[128,2560]{1,0:T(8,128)(2,1)S(1)}, u32[]{:S(2)}, u32[]{:S(2)}) collective-permute-start(bf16[128,2560]{1,0:T(8,128)(2,1)S(1)} %get-tuple-element.48), channel_id=1, source_target_pairs={{0,3},{1,0},{2,1},{3,2},{4,7},{5,4},{6,5},{7,6},{8,11},{9,8},{10,9... | collective-permute-start | bytes 1966088 | tf_op jit(solution)/shard_map/ppermute | solution.py:268
  50.0 6.2 %copy-start.3 = (bf16[128,5120]{1,0:T(8,128)(2,1)S(1)}, bf16[128,5120]{1,0:T(8,128)(2,1)}, u32[]{:S(2)}) copy-start(bf16[128,5120]{1,0:T(8,128)(2,1)} %rest_0_.1) | copy-start | bytes 3932164
  54.1 21.7 %collective-permute-start.13 = (bf16[128,2560]{1,0:T(8,128)(2,1)S(1)}, bf16[128,2560]{1,0:T(8,128)(2,1)S(1)}, u32[]{:S(2)}, u32[]{:S(2)}) collective-permute-start(bf16[128,2560]{1,0:T(8,128)(2,1)S(1)} %get-tuple-element.42), channel_id=1, source_target_pairs={{0,3},{1,0},{2,1},{3,2},{4,7},{5,4},{6,5},{7,6},{8,11},{9,8},{10,9... | collective-permute-start | bytes 1966088 | tf_op jit(solution)/shard_map/ppermute | solution.py:268
  55.7 20.3 %collective-permute-start.14 = (bf16[128,2560]{1,0:T(8,128)(2,1)S(1)}, bf16[128,2560]{1,0:T(8,128)(2,1)S(1)}, u32[]{:S(2)}, u32[]{:S(2)}) collective-permute-start(bf16[128,2560]{1,0:T(8,128)(2,1)S(1)} %get-tuple-element.44), channel_id=1, source_target_pairs={{0,1},{1,2},{2,3},{3,0},{4,5},{5,6},{6,7},{7,4},{8,9},{9,10},{10,1... | collective-permute-start | bytes 1966088 | tf_op jit(solution)/shard_map/ppermute | solution.py:268
  61.6 27.1 %collective-permute-start.16 = (bf16[128,2560]{1,0:T(8,128)(2,1)S(1)}, bf16[128,2560]{1,0:T(8,128)(2,1)S(1)}, u32[]{:S(2)}, u32[]{:S(2)}) collective-permute-start(bf16[128,2560]{1,0:T(8,128)(2,1)S(1)} %add.14), channel_id=1, source_target_pairs={{0,1},{1,2},{2,3},{3,0},{4,5},{5,6},{6,7},{7,4},{8,9},{9,10},{10,1... | collective-permute-start | bytes 1966088 | tf_op jit(solution)/shard_map/ppermute | solution.py:268
  62.0 26.8 %copy-start.6 = (f32[5120]{0:T(1024)S(1)}, f32[5120]{0:T(1024)}, u32[]{:S(2)}) copy-start(f32[5120]{0:T(1024)} %param.15) | copy-start | bytes 61444
  62.0 26.8 %copy-start.7 = (s32[4]{0:T(128)S(1)}, s32[4]{0:T(128)}, u32[]{:S(2)}) copy-start(s32[4]{0:T(128)} %keep_ref.1) | copy-start | bytes 52
  62.1 26.6 %collective-permute-start.18 = (bf16[128,2560]{1,0:T(8,128)(2,1)S(1)}, bf16[128,2560]{1,0:T(8,128)(2,1)S(1)}, u32[]{:S(2)}, u32[]{:S(2)}) collective-permute-start(bf16[128,2560]{1,0:T(8,128)(2,1)S(1)} %add.15), channel_id=1, source_target_pairs={{0,3},{1,0},{2,1},{3,2},{4,7},{5,4},{6,5},{7,6},{8,11},{9,8},{10,9... | collective-permute-start | bytes 1966088 | tf_op jit(solution)/shard_map/ppermute | solution.py:268

commit v8 on v7

--- a/solution.py
+++ b/solution.py
@@ -95,7 +95,7 @@
             pltpu.VMEM((parts, w.shape[0] // parts, w.shape[1]), BF16),
             pltpu.SemaphoreType.DMA((parts,)),
         ],
-        compiler_params=pltpu.CompilerParams(vmem_limit_bytes=20 << 20),
+        compiler_params=pltpu.CompilerParams(vmem_limit_bytes=46 << 20),
         cost_estimate=SMALL_COST,
     )(x, w, after)
 
@@ -196,7 +196,7 @@
 
 
 def block_kernel(turn, anc_ref, q_ref, kv_ref, w_ref, *rest):
-    res_ref, outs = (rest[0], rest[1:3]) if len(rest) % 2 else (None, rest[:2])
+    res_ref, outs = (rest[0], rest[1:3]) if len(rest) == 4 else (None, rest[:2])
     per, slots = anc_ref.shape
     local = (lax.axis_index("tp") + turn) % per
     rows, count = [], jnp.int32(0)
@@ -228,23 +228,37 @@
         functools.partial(block_kernel, turn),
         name="block_terms",
         out_shape=[jax.ShapeDtypeStruct((BLK, cols // 2), kind)] * 2
-        + [jax.ShapeDtypeStruct(x.shape, x.dtype) for x in (kv, w_out)],
+        + [jax.ShapeDtypeStruct(kv.shape, kv.dtype)],
         in_specs=[pl.BlockSpec(memory_space=pltpu.SMEM)] + [vmem] * (3 + len(extra)),
-        out_specs=[vmem] * 2 + [pl.BlockSpec(memory_space=pl.ANY)] * 2,
-        input_output_aliases={2: 2, 3: 3},
+        out_specs=[vmem] * 2 + [pl.BlockSpec(memory_space=pl.ANY)],
+        input_output_aliases={2: 2},
         compiler_params=pltpu.CompilerParams(vmem_limit_bytes=BLOCK_VMEM),
         cost_estimate=SMALL_COST,
     )(ancestors, q, kv, w_out, *extra)
-    return outs[:2], outs[2:]
-
-
-def norm_kernel(b1_ref, b2_ref, u_ref, v_ref, gain_ref, keep_ref, o_ref):
+    return outs[:2], outs[2]
+
+
+def norm_kernel(b1_ref, b2_ref, u_ref, v_ref, gain_ref, keep_ref, o_ref, obuf, sems):
     half = u_ref.shape[1]
-    total = [b1_ref[...] + u_ref[...].astype(F32), b2_ref[...] + v_ref[...].astype(F32)]
-    square = sum(jnp.sum(x * x, axis=1, keepdims=True) for x in total)
-    factor = lax.rsqrt(square * (1.0 / (2 * half)) + 1e-06) * keep_ref[lax.axis_index("tp")].astype(F32)
-    for lo, x in zip((0, half), total):
-        o_ref[:, lo:lo + half] = (x * factor * gain_ref[:, lo:lo + half]).astype(BF16)
+    tiles = sems.shape[0]
+    size = u_ref.shape[0] // tiles
+    keep = keep_ref[lax.axis_index("tp")].astype(F32)
+    copies = []
+    for k in range(tiles):
+        cut = slice(k * size, (k + 1) * size)
+        total = [
+            b1_ref[cut, :] + u_ref[cut, :].astype(F32),
+            b2_ref[cut, :] + v_ref[cut, :].astype(F32),
+        ]
+        square = sum(jnp.sum(x * x, axis=1, keepdims=True) for x in total)
+        factor = lax.rsqrt(square * (1.0 / (2 * half)) + 1e-06) * keep
+        for lo, x in zip((0, half), total):
+            obuf[cut, lo:lo + half] = (x * factor * gain_ref[:, lo:lo + half]).astype(BF16)
+        rows = pl.ds(k * size, size)
+        copies.append(pltpu.make_async_copy(obuf.at[rows], o_ref.at[rows], sems.at[k]))
+        copies[-1].start()
+    for copy in copies:
+        copy.wait()
 
 
 def final_norm(base, last, gain, keep):
@@ -255,7 +269,8 @@
         name="final_norm",
         out_shape=jax.ShapeDtypeStruct((rows, 2 * half), BF16),
         in_specs=[vm] * 5 + [pl.BlockSpec(memory_space=pltpu.SMEM)],
-        out_specs=vm,
+        out_specs=pl.BlockSpec(memory_space=pltpu.HBM),
+        scratch_shapes=[pltpu.VMEM((rows, 2 * half), BF16), pltpu.SemaphoreType.DMA((4,))],
         compiler_params=pltpu.CompilerParams(vmem_limit_bytes=30 << 20),
     )(*base, *last, gain[None, :], keep)
 
@@ -268,7 +283,7 @@
     return lax.ppermute(x, axis, ring({"y": 2, "core": 2, "z": 4, "tp": 4}[axis], s))
 
 
-def gather_blocks(own, first, second):
+def gather_blocks(own, first):
     rows = own.shape[0]
     half = rows // 2
 
@@ -286,12 +301,12 @@
         return [(piece, tuple(result[0])), (shift(piece, "core", 1), tuple(result[1]))]
 
     y_far = fetch(own, 2, 1)
-    y = fetch(own, 0, 1)
     up = fetch(own, 1, 0)
     down = fetch(own, 3, 0)
+    y = fetch(own, 0, 1)
     more_up = fetch(jnp.concatenate([y, up[:half]], axis=0), 1, 0)
     more_down = fetch(jnp.concatenate([y, down[half:]], axis=0), 3, 0)
-    y_far, first, second = tie((y_far, first(y), second(y)))
+    y_far, first = tie((y_far, first(y)))
     early = (
         both(own, (0, 0, 0, rows))
         + both(y, (0, 1, 0, rows))
@@ -300,34 +315,28 @@
         + both(y_far, (2, 1, 0, rows))
     )
     shape = (16 * rows, own.shape[1])
-    more_up, more_down, base, first, second = tie(
-        (more_up, more_down, collect(early, shape), first, second)
-    )
+    more_up, more_down, base, first = tie((more_up, more_down, collect(early, shape), first))
     late = both(more_up, (1, 1, 0, rows), (2, 0, 0, half)) + both(
         more_down, (3, 1, 0, rows), (2, 0, half, half)
     )
-    return collect(late, shape, base), first, second
+    return collect(late, shape, base), first
 
 
 def on_device(activations, residual, w_query, w_key, w_value, w_out, gain, ancestors, kept):
     kv_own = kv_project(activations, w_key, w_value)
-    kv, queries, w_held = gather_blocks(
-        kv_own,
-        lambda there: q_project(activations, w_query, there),
-        lambda there: collect([(w_out, ((0, 0, w_out.shape[0]),))], w_out.shape, None, (there,)),
-    )
+    kv, queries = gather_blocks(kv_own, lambda there: q_project(activations, w_query, there))
 
     def send(x, s):
         return shift(x, "tp", s % 4)
 
-    (lo2, hi2), held = block_terms(2, ancestors, queries, kv, w_held)
+    (lo2, hi2), kv = block_terms(2, ancestors, queries, kv, w_out)
     a = send(lo2, 1)
     b = send(hi2, 3)
-    (lo1, hi1), held = block_terms(1, ancestors, queries, *held)
+    (lo1, hi1), kv = block_terms(1, ancestors, queries, kv, w_out)
     u2 = send(hi1, 1)
-    (lo3, hi3), held = block_terms(3, ancestors, queries, *held)
+    (lo3, hi3), kv = block_terms(3, ancestors, queries, kv, w_out)
     v1 = send(lo3, 3)
-    (left, right), _ = block_terms(0, ancestors, queries, *held, residual)
+    (left, right), _ = block_terms(0, ancestors, queries, kv, w_out, residual)
     u1 = send(lo1 + a, 1)
     v2 = send(hi3 + b, 3)
     base = (left + v1.astype(F32), right + u2.astype(F32))

time: 91.6 us -> 90 us (0.983)
  local copies, waits for them, and re-layouts: 2.91 us -> 0.87 us
    unnamed x16, local copies, waits for them, and re-layouts: 2.89 us -> 0.86 us
    pallas_call x1, Pallas kernels: 6.6 us -> 7.7 us  [q_project(): pl.pallas_call(q_kernel, name='q_project', out_shape=jax.ShapeDtypeStruct...]
  transfers between devices with their start and end apart: 19 -> 19, of which waited for: 11 -> 11; matrix products, arithmetic and copies ran while one was open for 1% -> 1% of each run, Pallas kernels for 22% -> 23%
where the time goes in v8:
time: 90 us; the launch traced here: 89.6 us
  waiting for transfers between devices  33.9 us (38%)
  Pallas kernels  33 us (37%)
  starting transfers between devices  20.8 us (23%)
    ppermute x13, waiting for transfers between devices, shift(): lax.ppermute(x, axis, ring({'y': 2, 'core': 2, 'z': 4, 'tp': 4}[axis], s))  27.8 us
    pallas_call x4, Pallas kernels, block_terms(): pl.pallas_call(functools.partial(block_kernel, turn), name='block_terms',...  16.4 us
    ppermute x6, starting transfers between devices, fetch(): return lax.ppermute(x, ('z', 'y'), pairs)  10.7 us
    ppermute x13, starting transfers between devices, shift(): lax.ppermute(x, axis, ring({'y': 2, 'core': 2, 'z': 4, 'tp': 4}[axis], s))  10.1 us
    pallas_call x1, Pallas kernels, q_project(): pl.pallas_call(q_kernel, name='q_project', out_shape=jax.ShapeDtypeStruct...  7.7 us
    ppermute x6, waiting for transfers between devices, fetch(): return lax.ppermute(x, ('z', 'y'), pairs)  6.08 us
    pallas_call x1, Pallas kernels, kv_project(): pl.pallas_call(kv_kernel, name='kv_project', out_shape=jax.ShapeDtypeStru...  5.62 us
    pallas_call x1, Pallas kernels, final_norm(): pl.pallas_call(norm_kernel, name='final_norm', out_shape=jax.ShapeDtypeSt...  2.07 us
  transfers between devices with their start and end apart: 19, of which 11 were waited for; matrix products, arithmetic and copies ran while one was open for 1% of the time, Pallas kernels for 23%

profile of v8, /device:TPU:24, one launch (start us, length us, event | category | flops | bytes accessed | tf_op | source)
XLA Modules:
  0.0 89.6 jit_solution(10257838925938943357)
XLA Ops:
  0.0 5.6 %kv_project.1.refs_0_ = bf16[512,256]{1,0:T(8,128)(2,1)} custom-call(bf16[512,5120]{1,0:T(8,128)(2,1)} %x_ref.3, bf16[5120,128]{1,0:T(8,128)(2,1)} %wk_ref.1, bf16[5120,128]{1,0:T(8,128)(2,1)} %wv_ref.1), custom_call_target="tpu_custom_call" | custom-call | flops 1048576 | bytes 1048576 | tf_op jit(solution)/shard_map/kv_project/pallas_call | solution.py:53
  5.6 2.0 %collective-permute-start.3 = (bf16[512,256]{1,0:T(8,128)(2,1)}, bf16[512,256]{1,0:T(8,128)(2,1)S(1)}, u32[]{:S(2)}, u32[]{:S(2)}) collective-permute-start(bf16[512,256]{1,0:T(8,128)(2,1)} %kv_project.1.refs_0_), channel_id=1, source_target_pairs={{0,16},{8,24},{16,32},{24,40},{32,48},{40,56},{48,0},{56,8},{1,17}... | collective-permute-start | bytes 786440 | tf_op jit(solution)/shard_map/ppermute | solution.py:292
  7.6 2.2 %collective-permute-start.1 = (bf16[512,256]{1,0:T(8,128)(2,1)}, bf16[512,256]{1,0:T(8,128)(2,1)S(1)}, u32[]{:S(2)}, u32[]{:S(2)}) collective-permute-start(bf16[512,256]{1,0:T(8,128)(2,1)} %kv_project.1.refs_0_), channel_id=1, source_target_pairs={{0,48},{8,56},{16,0},{24,8},{32,16},{40,24},{48,32},{56,40},{1,49}... | collective-permute-start | bytes 786440 | tf_op jit(solution)/shard_map/ppermute | solution.py:292
  9.8 0.7 collective-permute-start
  10.6 2.5 %collective-permute-start.9 = (bf16[512,256]{1,0:T(8,128)(2,1)}, bf16[512,256]{1,0:T(8,128)(2,1)S(1)}, u32[]{:S(2)}, u32[]{:S(2)}) collective-permute-start(bf16[512,256]{1,0:T(8,128)(2,1)} %kv_project.1.refs_0_), channel_id=1, source_target_pairs={{0,40},{8,32},{16,56},{24,48},{32,8},{40,0},{48,24},{56,16},{1,41}... | collective-permute-start | bytes 786440 | tf_op jit(solution)/shard_map/ppermute | solution.py:292
  13.1 3.2 %collective-permute-done.3.refs_6_ = bf16[512,256]{1,0:T(8,128)(2,1)S(1)} collective-permute-done((bf16[512,256]{1,0:T(8,128)(2,1)}, bf16[512,256]{1,0:T(8,128)(2,1)S(1)}, u32[]{:S(2)}, u32[]{:S(2)}) %collective-permute-start.3) | collective-permute-done | bytes 262176 | tf_op jit(solution)/shard_map/ppermute | solution.py:292
  16.4 0.4 collective-permute-done.1.refs_4_
  16.8 2.5 %collective-permute-done.after_ref.refs_2_ = bf16[512,256]{1,0:T(8,128)(2,1)S(1)} collective-permute-done((bf16[512,256]{1,0:T(8,128)(2,1)}, bf16[512,256]{1,0:T(8,128)(2,1)S(1)}, u32[]{:S(2)}, u32[]{:S(2)}) %collective-permute-start) | collective-permute-done | bytes 262176 | tf_op jit(solution)/shard_map/ppermute | solution.py:292
  19.4 3.2 %collective-permute-start.2 = (bf16[768,256]{1,0:T(8,128)(2,1)S(1)}, bf16[768,256]{1,0:T(8,128)(2,1)S(1)}, u32[]{:S(2)}, u32[]{:S(2)}) collective-permute-start(bf16[768,256]{1,0:T(8,128)(2,1)S(1)} %get-tuple-element.40), channel_id=1, source_target_pairs={{0,48},{8,56},{16,0},{24,8},{32,16},{40,24},{48,32},{56,40},{1,49}... | collective-permute-start | bytes 1179656 | tf_op jit(solution)/shard_map/ppermute | solution.py:292
  22.6 7.7 %q_project.1.refs_1_ = bf16[512,640]{1,0:T(8,128)(2,1)S(1)} custom-call(bf16[512,5120]{1,0:T(8,128)(2,1)S(1)} %copy-done, bf16[5120,640]{1,0:T(8,128)(2,1)} %w_ref.5, bf16[512,256]{1,0:T(8,128)(2,1)S(1)} %collective-permute-done.after_ref.refs_2_), custom_call_target="tpu_custom_call" | custom-call | flops 1048576 | bytes 1048576 | tf_op jit(solution)/shard_map/q_project/pallas_call | solution.py:88
  30.5 0.5 collective-permute-start.6
  31.1 0.9 %collective-permute-done.7.refs_5_ = bf16[512,256]{1,0:T(8,128)(2,1)S(1)} collective-permute-done((bf16[512,256]{1,0:T(8,128)(2,1)S(1)}, bf16[512,256]{1,0:T(8,128)(2,1)S(1)}, u32[]{:S(2)}, u32[]{:S(2)}) %collective-permute-start.7) | collective-permute-done | bytes 262176 | tf_op jit(solution)/shard_map/ppermute | solution.py:283
  32.0 0.4 collective-permute-done.6.refs_3_
  32.3 0.4 collective-permute-done.10.refs_9_
  33.3 0.4 collective-permute-start.12
  33.6 1.2 %collective-permute-done.11.refs_2_ = bf16[768,256]{1,0:T(8,128)(2,1)S(1)} collective-permute-done((bf16[768,256]{1,0:T(8,128)(2,1)S(1)}, bf16[768,256]{1,0:T(8,128)(2,1)S(1)}, u32[]{:S(2)}, u32[]{:S(2)}) %collective-permute-start.11) | collective-permute-done | bytes 393248 | tf_op jit(solution)/shard_map/ppermute | solution.py:283
  34.9 0.6 collective-permute-done.12.refs_4_
  35.4 0.8 collect.3.kv_ref
  36.3 0.8 slice-done.1
  37.1 4.1 %block_terms.4 = (bf16[128,2560]{1,0:T(8,128)(2,1)S(1)}, bf16[128,2560]{1,0:T(8,128)(2,1)S(1)}, bf16[8192,256]{1,0:T(8,128)(2,1)S(1)}) custom-call(s32[4,16]{1,0:T(4,128)S(1)} %copy-done.3, bf16[512,640]{1,0:T(8,128)(2,1)S(1)} %get-tuple-element.24.q_ref, bf16[8192,256]{1,0:T(8,128)(2,1)S(1)} %collect.3.kv_ref, ...), custom_call_target="tpu_custom_call", output_to_operand_aliasing={{2}: (2, {})} | custom-call | flops 1048576 | bytes 1048576 | tf_op jit(solution)/shard_map/block_terms/pallas_call | solution.py:227
  41.2 1.6 %collective-permute-start.15 = (bf16[128,2560]{1,0:T(8,128)(2,1)S(1)}, bf16[128,2560]{1,0:T(8,128)(2,1)S(1)}, u32[]{:S(2)}, u32[]{:S(2)}) collective-permute-start(bf16[128,2560]{1,0:T(8,128)(2,1)S(1)} %get-tuple-element.36), channel_id=1, source_target_pairs={{0,1},{1,2},{2,3},{3,0},{4,5},{5,6},{6,7},{7,4},{8,9},{9,10},{10,1... | collective-permute-start | bytes 1966088 | tf_op jit(solution)/shard_map/ppermute | solution.py:283
  42.8 1.7 %collective-permute-start.17 = (bf16[128,2560]{1,0:T(8,128)(2,1)S(1)}, bf16[128,2560]{1,0:T(8,128)(2,1)S(1)}, u32[]{:S(2)}, u32[]{:S(2)}) collective-permute-start(bf16[128,2560]{1,0:T(8,128)(2,1)S(1)} %get-tuple-element.38), channel_id=1, source_target_pairs={{0,3},{1,0},{2,1},{3,2},{4,7},{5,4},{6,5},{7,6},{8,11},{9,8},{10,9... | collective-permute-start | bytes 1966088 | tf_op jit(solution)/shard_map/ppermute | solution.py:283
  44.5 4.1 %block_terms.5 = (bf16[128,2560]{1,0:T(8,128)(2,1)S(1)}, bf16[128,2560]{1,0:T(8,128)(2,1)S(1)}, bf16[8192,256]{1,0:T(8,128)(2,1)S(1)}) custom-call(s32[4,16]{1,0:T(4,128)S(1)} %copy-done.3, bf16[512,640]{1,0:T(8,128)(2,1)S(1)} %get-tuple-element.24.q_ref, bf16[8192,256]{1,0:T(8,128)(2,1)S(1)} %get-tuple-element.28.kv_ref, ...), custom_call_target="tpu_custom_call", output_to_operand_aliasing={{2}: (2, {})} | custom-call | flops 1048576 | bytes 1048576 | tf_op jit(solution)/shard_map/block_terms/pallas_call | solution.py:227
  48.6 4.1 %block_terms.6 = (bf16[128,2560]{1,0:T(8,128)(2,1)S(1)}, bf16[128,2560]{1,0:T(8,128)(2,1)S(1)}, bf16[8192,256]{1,0:T(8,128)(2,1)S(1)}) custom-call(s32[4,16]{1,0:T(4,128)S(1)} %copy-done.3, bf16[512,640]{1,0:T(8,128)(2,1)S(1)} %get-tuple-element.24.q_ref, bf16[8192,256]{1,0:T(8,128)(2,1)S(1)} %get-tuple-element.29.kv_ref, ...), custom_call_target="tpu_custom_call", output_to_operand_aliasing={{2}: (2, {})} | custom-call | flops 1048576 | bytes 1048576 | tf_op jit(solution)/shard_map/block_terms/pallas_call | solution.py:227
  52.7 1.6 %collective-permute-start.13 = (bf16[128,2560]{1,0:T(8,128)(2,1)S(1)}, bf16[128,2560]{1,0:T(8,128)(2,1)S(1)}, u32[]{:S(2)}, u32[]{:S(2)}) collective-permute-start(bf16[128,2560]{1,0:T(8,128)(2,1)S(1)} %get-tuple-element.32), channel_id=1, source_target_pairs={{0,3},{1,0},{2,1},{3,2},{4,7},{5,4},{6,5},{7,6},{8,11},{9,8},{10,9... | collective-permute-start | bytes 1966088 | tf_op jit(solution)/shard_map/ppermute | solution.py:283
  54.3 0.5 collective-permute-start.14
  54.8 4.2 %block_terms.7 = (f32[128,2560]{1,0:T(8,128)S(1)}, f32[128,2560]{1,0:T(8,128)S(1)}, bf16[8192,256]{1,0:T(8,128)(2,1)S(1)}) custom-call(s32[4,16]{1,0:T(4,128)S(1)} %copy-done.3, bf16[512,640]{1,0:T(8,128)(2,1)S(1)} %get-tuple-element.24.q_ref, bf16[8192,256]{1,0:T(8,128)(2,1)S(1)} %get-tuple-element.30.kv_ref, ...), custom_call_target="tpu_custom_call", output_to_operand_aliasing={{2}: (2, {})} | custom-call | flops 1048576 | bytes 1048576 | tf_op jit(solution)/shard_map/block_terms/pallas_call | solution.py:227
  59.0 1.1 %collective-permute-done.15 = bf16[128,2560]{1,0:T(8,128)(2,1)S(1)} collective-permute-done((bf16[128,2560]{1,0:T(8,128)(2,1)S(1)}, bf16[128,2560]{1,0:T(8,128)(2,1)S(1)}, u32[]{:S(2)}, u32[]{:S(2)}) %collective-permute-start.15) | collective-permute-done | bytes 655392 | tf_op jit(solution)/shard_map/ppermute | solution.py:283
  60.7 3.0 %collective-permute-start.18 = (bf16[128,2560]{1,0:T(8,128)(2,1)S(1)}, bf16[128,2560]{1,0:T(8,128)(2,1)S(1)}, u32[]{:S(2)}, u32[]{:S(2)}) collective-permute-start(bf16[128,2560]{1,0:T(8,128)(2,1)S(1)} %add.15), channel_id=1, source_target_pairs={{0,3},{1,0},{2,1},{3,2},{4,7},{5,4},{6,5},{7,6},{8,11},{9,8},{10,9... | collective-permute-start | bytes 1966088 | tf_op jit(solution)/shard_map/ppermute | solution.py:283
  63.7 10.7 %collective-permute-done.13 = bf16[128,2560]{1,0:T(8,128)(2,1)S(1)} collective-permute-done((bf16[128,2560]{1,0:T(8,128)(2,1)S(1)}, bf16[128,2560]{1,0:T(8,128)(2,1)S(1)}, u32[]{:S(2)}, u32[]{:S(2)}) %collective-permute-start.13) | collective-permute-done | bytes 655392 | tf_op jit(solution)/shard_map/ppermute | solution.py:283
  74.7 12.6 %collective-permute-done.16.u_ref = bf16[128,2560]{1,0:T(8,128)(2,1)S(1)} collective-permute-done((bf16[128,2560]{1,0:T(8,128)(2,1)S(1)}, bf16[128,2560]{1,0:T(8,128)(2,1)S(1)}, u32[]{:S(2)}, u32[]{:S(2)}) %collective-permute-start.16) | collective-permute-done | bytes 655392 | tf_op jit(solution)/shard_map/ppermute | solution.py:283
  87.4 2.1 %final_norm.1 = bf16[128,5120]{1,0:T(8,128)(2,1)} custom-call(f32[128,2560]{1,0:T(8,128)S(1)} %convert_add_fusion.1.b1_ref, f32[128,2560]{1,0:T(8,128)S(1)} %convert_add_fusion.b2_ref, bf16[128,2560]{1,0:T(8,128)(2,1)S(1)} %collective-permute-done.16.u_ref, bf16[128,2560]{1,0:T(8,128)(2,1)S(1)} %collective-permute-done.18.v_ref, f32[1,5120]{1,0:T(1,128)S(1)} %bitcast.3, ...), custom_call_target="tpu_custom_call" | custom-call | tf_op jit(solution)/shard_map/final_norm/pallas_call | solution.py:267
  (41 shorter events, 1.9 us)
Async XLA Ops:
  0.0 22.6 %copy-start = (bf16[512,5120]{1,0:T(8,128)(2,1)S(1)}, bf16[512,5120]{1,0:T(8,128)(2,1)}, u32[]{:S(2)}) copy-start(bf16[512,5120]{1,0:T(8,128)(2,1)} %x_ref.3) | copy-start | bytes 15728644
  5.6 10.6 %collective-permute-start.3 = (bf16[512,256]{1,0:T(8,128)(2,1)}, bf16[512,256]{1,0:T(8,128)(2,1)S(1)}, u32[]{:S(2)}, u32[]{:S(2)}) collective-permute-start(bf16[512,256]{1,0:T(8,128)(2,1)} %kv_project.1.refs_0_), channel_id=1, source_target_pairs={{0,16},{8,24},{16,32},{24,40},{32,48},{40,56},{48,0},{56,8},{1,17}... | collective-permute-start | bytes 786440 | tf_op jit(solution)/shard_map/ppermute | solution.py:292
  7.6 9.2 %collective-permute-start.1 = (bf16[512,256]{1,0:T(8,128)(2,1)}, bf16[512,256]{1,0:T(8,128)(2,1)S(1)}, u32[]{:S(2)}, u32[]{:S(2)}) collective-permute-start(bf16[512,256]{1,0:T(8,128)(2,1)} %kv_project.1.refs_0_), channel_id=1, source_target_pairs={{0,48},{8,56},{16,0},{24,8},{32,16},{40,24},{48,32},{56,40},{1,49}... | collective-permute-start | bytes 786440 | tf_op jit(solution)/shard_map/ppermute | solution.py:292
  9.8 9.4 %collective-permute-start = (bf16[512,256]{1,0:T(8,128)(2,1)}, bf16[512,256]{1,0:T(8,128)(2,1)S(1)}, u32[]{:S(2)}, u32[]{:S(2)}) collective-permute-start(bf16[512,256]{1,0:T(8,128)(2,1)} %kv_project.1.refs_0_), channel_id=1, source_target_pairs={{0,8},{8,0},{16,24},{24,16},{32,40},{40,32},{48,56},{56,48},{1,9},... | collective-permute-start | bytes 786440 | tf_op jit(solution)/shard_map/ppermute | solution.py:292
  10.6 19.8 %collective-permute-start.9 = (bf16[512,256]{1,0:T(8,128)(2,1)}, bf16[512,256]{1,0:T(8,128)(2,1)S(1)}, u32[]{:S(2)}, u32[]{:S(2)}) collective-permute-start(bf16[512,256]{1,0:T(8,128)(2,1)} %kv_project.1.refs_0_), channel_id=1, source_target_pairs={{0,40},{8,32},{16,56},{24,48},{32,8},{40,0},{48,24},{56,16},{1,41}... | collective-permute-start | bytes 786440 | tf_op jit(solution)/shard_map/ppermute | solution.py:292
  13.1 17.4 %collective-permute-start.5 = (bf16[512,256]{1,0:T(8,128)(2,1)}, bf16[512,256]{1,0:T(8,128)(2,1)S(1)}, u32[]{:S(2)}, u32[]{:S(2)}) collective-permute-start(bf16[512,256]{1,0:T(8,128)(2,1)} %kv_project.1.refs_0_), channel_id=1, source_target_pairs={{0,4},{4,0},{1,5},{5,1},{2,6},{6,2},{3,7},{7,3},{8,12},{12,8},{9,1... | collective-permute-start | bytes 786440 | tf_op jit(solution)/shard_map/ppermute | solution.py:283
  16.3 14.7 %collective-permute-start.8 = (bf16[512,256]{1,0:T(8,128)(2,1)S(1)}, bf16[512,256]{1,0:T(8,128)(2,1)S(1)}, u32[]{:S(2)}, u32[]{:S(2)}) collective-permute-start(bf16[512,256]{1,0:T(8,128)(2,1)S(1)} %collective-permute-done.3.refs_6_), channel_id=1, source_target_pairs={{0,4},{4,0},{1,5},{5,1},{2,6},{6,2},{3,7},{7,3},{8,12},{12,8},{9,1... | collective-permute-start | bytes 786440 | tf_op jit(solution)/shard_map/ppermute | solution.py:283
  19.3 13.7 %collective-permute-start.4 = (bf16[768,256]{1,0:T(8,128)(2,1)S(1)}, bf16[768,256]{1,0:T(8,128)(2,1)S(1)}, u32[]{:S(2)}, u32[]{:S(2)}) collective-permute-start(bf16[768,256]{1,0:T(8,128)(2,1)S(1)} %get-tuple-element.39), channel_id=1, source_target_pairs={{0,16},{8,24},{16,32},{24,40},{32,48},{40,56},{48,0},{56,8},{1,17}... | collective-permute-start | bytes 1179656 | tf_op jit(solution)/shard_map/ppermute | solution.py:292
  19.4 13.3 %copy-start.2 = (bf16[512,256]{1,0:T(8,128)(2,1)S(1)}, bf16[512,256]{1,0:T(8,128)(2,1)}, u32[]{:S(2)}) copy-start(bf16[512,256]{1,0:T(8,128)(2,1)} %kv_project.1.refs_0_) | copy-start | bytes 786436
  19.4 13.6 %collective-permute-start.2 = (bf16[768,256]{1,0:T(8,128)(2,1)S(1)}, bf16[768,256]{1,0:T(8,128)(2,1)S(1)}, u32[]{:S(2)}, u32[]{:S(2)}) collective-permute-start(bf16[768,256]{1,0:T(8,128)(2,1)S(1)} %get-tuple-element.40), channel_id=1, source_target_pairs={{0,48},{8,56},{16,0},{24,8},{32,16},{40,24},{48,32},{56,40},{1,49}... | collective-permute-start | bytes 1179656 | tf_op jit(solution)/shard_map/ppermute | solution.py:292
  30.3 1.6 %collective-permute-start.7 = (bf16[512,256]{1,0:T(8,128)(2,1)S(1)}, bf16[512,256]{1,0:T(8,128)(2,1)S(1)}, u32[]{:S(2)}, u32[]{:S(2)}) collective-permute-start(bf16[512,256]{1,0:T(8,128)(2,1)S(1)} %collective-permute-done.1.refs_4_), channel_id=1, source_target_pairs={{0,4},{4,0},{1,5},{5,1},{2,6},{6,2},{3,7},{7,3},{8,12},{12,8},{9,1... | collective-permute-start | bytes 786440 | tf_op jit(solution)/shard_map/ppermute | solution.py:283
  30.5 1.9 %collective-permute-start.6 = (bf16[512,256]{1,0:T(8,128)(2,1)S(1)}, bf16[512,256]{1,0:T(8,128)(2,1)S(1)}, u32[]{:S(2)}, u32[]{:S(2)}) collective-permute-start(bf16[512,256]{1,0:T(8,128)(2,1)S(1)} %collective-permute-done.after_ref.refs_2_), channel_id=1, source_target_pairs={{0,4},{4,0},{1,5},{5,1},{2,6},{6,2},{3,7},{7,3},{8,12},{12,8},{9,1... | collective-permute-start | bytes 786440 | tf_op jit(solution)/shard_map/ppermute | solution.py:283
  30.9 1.8 %collective-permute-start.10 = (bf16[512,256]{1,0:T(8,128)(2,1)S(1)}, bf16[512,256]{1,0:T(8,128)(2,1)S(1)}, u32[]{:S(2)}, u32[]{:S(2)}) collective-permute-start(bf16[512,256]{1,0:T(8,128)(2,1)S(1)} %get-tuple-element.22.refs_8_), channel_id=1, source_target_pairs={{0,4},{4,0},{1,5},{5,1},{2,6},{6,2},{3,7},{7,3},{8,12},{12,8},{9,1... | collective-permute-start | bytes 786440 | tf_op jit(solution)/shard_map/ppermute | solution.py:283
  33.0 3.2 %slice-start = ((s8[6553600]{0:T(1024)(128)(4,1)}), s8[4194304]{0:T(1024)(128)(4,1)S(1)}, s32[]{:S(2)}) async-start(s8[6553600]{0:T(1024)(128)(4,1)} %bitcast.1), calls=%async_computation | async-start | bytes 8388608
  33.1 1.8 %collective-permute-start.11 = (bf16[768,256]{1,0:T(8,128)(2,1)S(1)}, bf16[768,256]{1,0:T(8,128)(2,1)S(1)}, u32[]{:S(2)}, u32[]{:S(2)}) collective-permute-start(bf16[768,256]{1,0:T(8,128)(2,1)S(1)} %get-tuple-element.26.refs_1_), channel_id=1, source_target_pairs={{0,4},{4,0},{1,5},{5,1},{2,6},{6,2},{3,7},{7,3},{8,12},{12,8},{9,1... | collective-permute-start | bytes 1179656 | tf_op jit(solution)/shard_map/ppermute | solution.py:283
  33.3 2.1 %collective-permute-start.12 = (bf16[768,256]{1,0:T(8,128)(2,1)S(1)}, bf16[768,256]{1,0:T(8,128)(2,1)S(1)}, u32[]{:S(2)}, u32[]{:S(2)}) collective-permute-start(bf16[768,256]{1,0:T(8,128)(2,1)S(1)} %get-tuple-element.27.refs_3_), channel_id=1, source_target_pairs={{0,4},{4,0},{1,5},{5,1},{2,6},{6,2},{3,7},{7,3},{8,12},{12,8},{9,1... | collective-permute-start | bytes 1179656 | tf_op jit(solution)/shard_map/ppermute | solution.py:283
  35.4 1.7 %slice-start.1 = ((s8[6553600]{0:T(1024)(128)(4,1)}), s8[2359296]{0:T(1024)(128)(4,1)S(1)}, s32[]{:S(2)}) async-start(s8[6553600]{0:T(1024)(128)(4,1)} %bitcast.1), calls=%async_computation.1 | async-start | bytes 4718592
  35.4 1.7 %copy-start.3 = (s32[4,16]{1,0:T(4,128)S(1)}, s32[4,16]{1,0:T(4,128)}, u32[]{:S(2)}) copy-start(s32[4,16]{1,0:T(4,128)} %anc_ref.7) | copy-start | bytes 772
  41.2 18.9 %collective-permute-start.15 = (bf16[128,2560]{1,0:T(8,128)(2,1)S(1)}, bf16[128,2560]{1,0:T(8,128)(2,1)S(1)}, u32[]{:S(2)}, u32[]{:S(2)}) collective-permute-start(bf16[128,2560]{1,0:T(8,128)(2,1)S(1)} %get-tuple-element.36), channel_id=1, source_target_pairs={{0,1},{1,2},{2,3},{3,0},{4,5},{5,6},{6,7},{7,4},{8,9},{9,10},{10,1... | collective-permute-start | bytes 1966088 | tf_op jit(solution)/shard_map/ppermute | solution.py:283
  42.8 17.8 %collective-permute-start.17 = (bf16[128,2560]{1,0:T(8,128)(2,1)S(1)}, bf16[128,2560]{1,0:T(8,128)(2,1)S(1)}, u32[]{:S(2)}, u32[]{:S(2)}) collective-permute-start(bf16[128,2560]{1,0:T(8,128)(2,1)S(1)} %get-tuple-element.38), channel_id=1, source_target_pairs={{0,3},{1,0},{2,1},{3,2},{4,7},{5,4},{6,5},{7,6},{8,11},{9,8},{10,9... | collective-permute-start | bytes 1966088 | tf_op jit(solution)/shard_map/ppermute | solution.py:283
  48.6 6.2 %copy-start.1 = (bf16[128,5120]{1,0:T(8,128)(2,1)S(1)}, bf16[128,5120]{1,0:T(8,128)(2,1)}, u32[]{:S(2)}) copy-start(bf16[128,5120]{1,0:T(8,128)(2,1)} %rest_0_.1) | copy-start | bytes 3932164
  52.7 21.7 %collective-permute-start.13 = (bf16[128,2560]{1,0:T(8,128)(2,1)S(1)}, bf16[128,2560]{1,0:T(8,128)(2,1)S(1)}, u32[]{:S(2)}, u32[]{:S(2)}) collective-permute-start(bf16[128,2560]{1,0:T(8,128)(2,1)S(1)} %get-tuple-element.32), channel_id=1, source_target_pairs={{0,3},{1,0},{2,1},{3,2},{4,7},{5,4},{6,5},{7,6},{8,11},{9,8},{10,9... | collective-permute-start | bytes 1966088 | tf_op jit(solution)/shard_map/ppermute | solution.py:283
  54.3 20.2 %collective-permute-start.14 = (bf16[128,2560]{1,0:T(8,128)(2,1)S(1)}, bf16[128,2560]{1,0:T(8,128)(2,1)S(1)}, u32[]{:S(2)}, u32[]{:S(2)}) collective-permute-start(bf16[128,2560]{1,0:T(8,128)(2,1)S(1)} %get-tuple-element.34), channel_id=1, source_target_pairs={{0,1},{1,2},{2,3},{3,0},{4,5},{5,6},{6,7},{7,4},{8,9},{9,10},{10,1... | collective-permute-start | bytes 1966088 | tf_op jit(solution)/shard_map/ppermute | solution.py:283
  60.2 27.1 %collective-permute-start.16 = (bf16[128,2560]{1,0:T(8,128)(2,1)S(1)}, bf16[128,2560]{1,0:T(8,128)(2,1)S(1)}, u32[]{:S(2)}, u32[]{:S(2)}) collective-permute-start(bf16[128,2560]{1,0:T(8,128)(2,1)S(1)} %add.14), channel_id=1, source_target_pairs={{0,1},{1,2},{2,3},{3,0},{4,5},{5,6},{6,7},{7,4},{8,9},{9,10},{10,1... | collective-permute-start | bytes 1966088 | tf_op jit(solution)/shard_map/ppermute | solution.py:283
  60.7 26.6 %collective-permute-start.18 = (bf16[128,2560]{1,0:T(8,128)(2,1)S(1)}, bf16[128,2560]{1,0:T(8,128)(2,1)S(1)}, u32[]{:S(2)}, u32[]{:S(2)}) collective-permute-start(bf16[128,2560]{1,0:T(8,128)(2,1)S(1)} %add.15), channel_id=1, source_target_pairs={{0,3},{1,0},{2,1},{3,2},{4,7},{5,4},{6,5},{7,6},{8,11},{9,8},{10,9... | collective-permute-start | bytes 1966088 | tf_op jit(solution)/shard_map/ppermute | solution.py:283
  74.6 12.8 %copy-start.4 = (f32[5120]{0:T(1024)S(1)}, f32[5120]{0:T(1024)}, u32[]{:S(2)}) copy-start(f32[5120]{0:T(1024)} %param.15) | copy-start | bytes 61444
  74.6 12.8 %copy-start.5 = (s32[4]{0:T(128)S(1)}, s32[4]{0:T(128)}, u32[]{:S(2)}) copy-start(s32[4]{0:T(128)} %keep_ref.1) | copy-start | bytes 52

commit v9 on v8

--- a/solution.py
+++ b/solution.py
@@ -10,7 +10,7 @@
 
 HD = 128
 BLK = 128
-CHUNK = 4
+CHUNK = 8
 CTX = ("z", "y", "core")
 F32 = jnp.float32
 BF16 = jnp.bfloat16

time: 90 us -> 90 us (level)
  no operation moved by 1% of the time
where the time goes in v9:
time: 90 us; the launch traced here: 89.6 us
  waiting for transfers between devices  33.9 us (38%)
  Pallas kernels  32.9 us (37%)
  starting transfers between devices  20.8 us (23%)
    ppermute x13, waiting for transfers between devices, shift(): lax.ppermute(x, axis, ring({'y': 2, 'core': 2, 'z': 4, 'tp': 4}[axis], s))  27.9 us
    pallas_call x4, Pallas kernels, block_terms(): pl.pallas_call(functools.partial(block_kernel, turn), name='block_terms',...  16.4 us
    ppermute x6, starting transfers between devices, fetch(): return lax.ppermute(x, ('z', 'y'), pairs)  10.7 us
    ppermute x13, starting transfers between devices, shift(): lax.ppermute(x, axis, ring({'y': 2, 'core': 2, 'z': 4, 'tp': 4}[axis], s))  10.1 us
    pallas_call x1, Pallas kernels, q_project(): pl.pallas_call(q_kernel, name='q_project', out_shape=jax.ShapeDtypeStruct...  7.7 us
    ppermute x6, waiting for transfers between devices, fetch(): return lax.ppermute(x, ('z', 'y'), pairs)  6.08 us
    pallas_call x1, Pallas kernels, kv_project(): pl.pallas_call(kv_kernel, name='kv_project', out_shape=jax.ShapeDtypeStru...  5.62 us
    pallas_call x1, Pallas kernels, final_norm(): pl.pallas_call(norm_kernel, name='final_norm', out_shape=jax.ShapeDtypeSt...  2.07 us
  transfers between devices with their start and end apart: 19, of which 11 were waited for; matrix products, arithmetic and copies ran while one was open for 1% of the time, Pallas kernels for 23%

profile of v9, /device:TPU:24, one launch (start us, length us, event | category | flops | bytes accessed | tf_op | source)
XLA Modules:
  0.0 89.6 jit_solution(15169220146764766146)
XLA Ops:
  0.0 5.6 %kv_project.1.refs_0_ = bf16[512,256]{1,0:T(8,128)(2,1)} custom-call(bf16[512,5120]{1,0:T(8,128)(2,1)} %x_ref.3, bf16[5120,128]{1,0:T(8,128)(2,1)} %wk_ref.1, bf16[5120,128]{1,0:T(8,128)(2,1)} %wv_ref.1), custom_call_target="tpu_custom_call" | custom-call | flops 1048576 | bytes 1048576 | tf_op jit(solution)/shard_map/kv_project/pallas_call | solution.py:53
  5.6 2.0 %collective-permute-start.3 = (bf16[512,256]{1,0:T(8,128)(2,1)}, bf16[512,256]{1,0:T(8,128)(2,1)S(1)}, u32[]{:S(2)}, u32[]{:S(2)}) collective-permute-start(bf16[512,256]{1,0:T(8,128)(2,1)} %kv_project.1.refs_0_), channel_id=1, source_target_pairs={{0,16},{8,24},{16,32},{24,40},{32,48},{40,56},{48,0},{56,8},{1,17}... | collective-permute-start | bytes 786440 | tf_op jit(solution)/shard_map/ppermute | solution.py:292
  7.6 2.2 %collective-permute-start.1 = (bf16[512,256]{1,0:T(8,128)(2,1)}, bf16[512,256]{1,0:T(8,128)(2,1)S(1)}, u32[]{:S(2)}, u32[]{:S(2)}) collective-permute-start(bf16[512,256]{1,0:T(8,128)(2,1)} %kv_project.1.refs_0_), channel_id=1, source_target_pairs={{0,48},{8,56},{16,0},{24,8},{32,16},{40,24},{48,32},{56,40},{1,49}... | collective-permute-start | bytes 786440 | tf_op jit(solution)/shard_map/ppermute | solution.py:292
  9.8 0.7 collective-permute-start
  10.6 2.5 %collective-permute-start.9 = (bf16[512,256]{1,0:T(8,128)(2,1)}, bf16[512,256]{1,0:T(8,128)(2,1)S(1)}, u32[]{:S(2)}, u32[]{:S(2)}) collective-permute-start(bf16[512,256]{1,0:T(8,128)(2,1)} %kv_project.1.refs_0_), channel_id=1, source_target_pairs={{0,40},{8,32},{16,56},{24,48},{32,8},{40,0},{48,24},{56,16},{1,41}... | collective-permute-start | bytes 786440 | tf_op jit(solution)/shard_map/ppermute | solution.py:292
  13.1 3.2 %collective-permute-done.3.refs_6_ = bf16[512,256]{1,0:T(8,128)(2,1)S(1)} collective-permute-done((bf16[512,256]{1,0:T(8,128)(2,1)}, bf16[512,256]{1,0:T(8,128)(2,1)S(1)}, u32[]{:S(2)}, u32[]{:S(2)}) %collective-permute-start.3) | collective-permute-done | bytes 262176 | tf_op jit(solution)/shard_map/ppermute | solution.py:292
  16.4 0.4 collective-permute-done.1.refs_4_
  16.8 2.5 %collective-permute-done.after_ref.refs_2_ = bf16[512,256]{1,0:T(8,128)(2,1)S(1)} collective-permute-done((bf16[512,256]{1,0:T(8,128)(2,1)}, bf16[512,256]{1,0:T(8,128)(2,1)S(1)}, u32[]{:S(2)}, u32[]{:S(2)}) %collective-permute-start) | collective-permute-done | bytes 262176 | tf_op jit(solution)/shard_map/ppermute | solution.py:292
  19.4 3.2 %collective-permute-start.2 = (bf16[768,256]{1,0:T(8,128)(2,1)S(1)}, bf16[768,256]{1,0:T(8,128)(2,1)S(1)}, u32[]{:S(2)}, u32[]{:S(2)}) collective-permute-start(bf16[768,256]{1,0:T(8,128)(2,1)S(1)} %get-tuple-element.40), channel_id=1, source_target_pairs={{0,48},{8,56},{16,0},{24,8},{32,16},{40,24},{48,32},{56,40},{1,49}... | collective-permute-start | bytes 1179656 | tf_op jit(solution)/shard_map/ppermute | solution.py:292
  22.6 7.7 %q_project.1.refs_1_ = bf16[512,640]{1,0:T(8,128)(2,1)S(1)} custom-call(bf16[512,5120]{1,0:T(8,128)(2,1)S(1)} %copy-done, bf16[5120,640]{1,0:T(8,128)(2,1)} %w_ref.5, bf16[512,256]{1,0:T(8,128)(2,1)S(1)} %collective-permute-done.after_ref.refs_2_), custom_call_target="tpu_custom_call" | custom-call | flops 1048576 | bytes 1048576 | tf_op jit(solution)/shard_map/q_project/pallas_call | solution.py:88
  30.5 0.5 collective-permute-start.6
  31.1 0.9 %collective-permute-done.7.refs_5_ = bf16[512,256]{1,0:T(8,128)(2,1)S(1)} collective-permute-done((bf16[512,256]{1,0:T(8,128)(2,1)S(1)}, bf16[512,256]{1,0:T(8,128)(2,1)S(1)}, u32[]{:S(2)}, u32[]{:S(2)}) %collective-permute-start.7) | collective-permute-done | bytes 262176 | tf_op jit(solution)/shard_map/ppermute | solution.py:283
  32.0 0.4 collective-permute-done.6.refs_3_
  32.3 0.4 collective-permute-done.10.refs_9_
  33.3 0.4 collective-permute-start.12
  33.6 1.2 %collective-permute-done.11.refs_2_ = bf16[768,256]{1,0:T(8,128)(2,1)S(1)} collective-permute-done((bf16[768,256]{1,0:T(8,128)(2,1)S(1)}, bf16[768,256]{1,0:T(8,128)(2,1)S(1)}, u32[]{:S(2)}, u32[]{:S(2)}) %collective-permute-start.11) | collective-permute-done | bytes 393248 | tf_op jit(solution)/shard_map/ppermute | solution.py:283
  34.9 0.6 collective-permute-done.12.refs_4_
  35.4 0.8 collect.3.kv_ref
  36.3 0.8 slice-done.1
  37.1 4.1 %block_terms.4 = (bf16[128,2560]{1,0:T(8,128)(2,1)S(1)}, bf16[128,2560]{1,0:T(8,128)(2,1)S(1)}, bf16[8192,256]{1,0:T(8,128)(2,1)S(1)}) custom-call(s32[4,16]{1,0:T(4,128)S(1)} %copy-done.3, bf16[512,640]{1,0:T(8,128)(2,1)S(1)} %get-tuple-element.24.q_ref, bf16[8192,256]{1,0:T(8,128)(2,1)S(1)} %collect.3.kv_ref, ...), custom_call_target="tpu_custom_call", output_to_operand_aliasing={{2}: (2, {})} | custom-call | flops 1048576 | bytes 1048576 | tf_op jit(solution)/shard_map/block_terms/pallas_call | solution.py:227
  41.2 1.6 %collective-permute-start.15 = (bf16[128,2560]{1,0:T(8,128)(2,1)S(1)}, bf16[128,2560]{1,0:T(8,128)(2,1)S(1)}, u32[]{:S(2)}, u32[]{:S(2)}) collective-permute-start(bf16[128,2560]{1,0:T(8,128)(2,1)S(1)} %get-tuple-element.36), channel_id=1, source_target_pairs={{0,1},{1,2},{2,3},{3,0},{4,5},{5,6},{6,7},{7,4},{8,9},{9,10},{10,1... | collective-permute-start | bytes 1966088 | tf_op jit(solution)/shard_map/ppermute | solution.py:283
  42.7 1.7 %collective-permute-start.17 = (bf16[128,2560]{1,0:T(8,128)(2,1)S(1)}, bf16[128,2560]{1,0:T(8,128)(2,1)S(1)}, u32[]{:S(2)}, u32[]{:S(2)}) collective-permute-start(bf16[128,2560]{1,0:T(8,128)(2,1)S(1)} %get-tuple-element.38), channel_id=1, source_target_pairs={{0,3},{1,0},{2,1},{3,2},{4,7},{5,4},{6,5},{7,6},{8,11},{9,8},{10,9... | collective-permute-start | bytes 1966088 | tf_op jit(solution)/shard_map/ppermute | solution.py:283
  44.5 4.1 %block_terms.5 = (bf16[128,2560]{1,0:T(8,128)(2,1)S(1)}, bf16[128,2560]{1,0:T(8,128)(2,1)S(1)}, bf16[8192,256]{1,0:T(8,128)(2,1)S(1)}) custom-call(s32[4,16]{1,0:T(4,128)S(1)} %copy-done.3, bf16[512,640]{1,0:T(8,128)(2,1)S(1)} %get-tuple-element.24.q_ref, bf16[8192,256]{1,0:T(8,128)(2,1)S(1)} %get-tuple-element.28.kv_ref, ...), custom_call_target="tpu_custom_call", output_to_operand_aliasing={{2}: (2, {})} | custom-call | flops 1048576 | bytes 1048576 | tf_op jit(solution)/shard_map/block_terms/pallas_call | solution.py:227
  48.6 4.1 %block_terms.6 = (bf16[128,2560]{1,0:T(8,128)(2,1)S(1)}, bf16[128,2560]{1,0:T(8,128)(2,1)S(1)}, bf16[8192,256]{1,0:T(8,128)(2,1)S(1)}) custom-call(s32[4,16]{1,0:T(4,128)S(1)} %copy-done.3, bf16[512,640]{1,0:T(8,128)(2,1)S(1)} %get-tuple-element.24.q_ref, bf16[8192,256]{1,0:T(8,128)(2,1)S(1)} %get-tuple-element.29.kv_ref, ...), custom_call_target="tpu_custom_call", output_to_operand_aliasing={{2}: (2, {})} | custom-call | flops 1048576 | bytes 1048576 | tf_op jit(solution)/shard_map/block_terms/pallas_call | solution.py:227
  52.7 1.6 %collective-permute-start.13 = (bf16[128,2560]{1,0:T(8,128)(2,1)S(1)}, bf16[128,2560]{1,0:T(8,128)(2,1)S(1)}, u32[]{:S(2)}, u32[]{:S(2)}) collective-permute-start(bf16[128,2560]{1,0:T(8,128)(2,1)S(1)} %get-tuple-element.32), channel_id=1, source_target_pairs={{0,3},{1,0},{2,1},{3,2},{4,7},{5,4},{6,5},{7,6},{8,11},{9,8},{10,9... | collective-permute-start | bytes 1966088 | tf_op jit(solution)/shard_map/ppermute | solution.py:283
  54.3 0.5 collective-permute-start.14
  54.8 4.1 %block_terms.7 = (f32[128,2560]{1,0:T(8,128)S(1)}, f32[128,2560]{1,0:T(8,128)S(1)}, bf16[8192,256]{1,0:T(8,128)(2,1)S(1)}) custom-call(s32[4,16]{1,0:T(4,128)S(1)} %copy-done.3, bf16[512,640]{1,0:T(8,128)(2,1)S(1)} %get-tuple-element.24.q_ref, bf16[8192,256]{1,0:T(8,128)(2,1)S(1)} %get-tuple-element.30.kv_ref, ...), custom_call_target="tpu_custom_call", output_to_operand_aliasing={{2}: (2, {})} | custom-call | flops 1048576 | bytes 1048576 | tf_op jit(solution)/shard_map/block_terms/pallas_call | solution.py:227
  58.9 1.1 %collective-permute-done.15 = bf16[128,2560]{1,0:T(8,128)(2,1)S(1)} collective-permute-done((bf16[128,2560]{1,0:T(8,128)(2,1)S(1)}, bf16[128,2560]{1,0:T(8,128)(2,1)S(1)}, u32[]{:S(2)}, u32[]{:S(2)}) %collective-permute-start.15) | collective-permute-done | bytes 655392 | tf_op jit(solution)/shard_map/ppermute | solution.py:283
  60.7 3.0 %collective-permute-start.18 = (bf16[128,2560]{1,0:T(8,128)(2,1)S(1)}, bf16[128,2560]{1,0:T(8,128)(2,1)S(1)}, u32[]{:S(2)}, u32[]{:S(2)}) collective-permute-start(bf16[128,2560]{1,0:T(8,128)(2,1)S(1)} %add.15), channel_id=1, source_target_pairs={{0,3},{1,0},{2,1},{3,2},{4,7},{5,4},{6,5},{7,6},{8,11},{9,8},{10,9... | collective-permute-start | bytes 1966088 | tf_op jit(solution)/shard_map/ppermute | solution.py:283
  63.7 10.7 %collective-permute-done.13 = bf16[128,2560]{1,0:T(8,128)(2,1)S(1)} collective-permute-done((bf16[128,2560]{1,0:T(8,128)(2,1)S(1)}, bf16[128,2560]{1,0:T(8,128)(2,1)S(1)}, u32[]{:S(2)}, u32[]{:S(2)}) %collective-permute-start.13) | collective-permute-done | bytes 655392 | tf_op jit(solution)/shard_map/ppermute | solution.py:283
  74.7 12.6 %collective-permute-done.16.u_ref = bf16[128,2560]{1,0:T(8,128)(2,1)S(1)} collective-permute-done((bf16[128,2560]{1,0:T(8,128)(2,1)S(1)}, bf16[128,2560]{1,0:T(8,128)(2,1)S(1)}, u32[]{:S(2)}, u32[]{:S(2)}) %collective-permute-start.16) | collective-permute-done | bytes 655392 | tf_op jit(solution)/shard_map/ppermute | solution.py:283
  87.3 2.1 %final_norm.1 = bf16[128,5120]{1,0:T(8,128)(2,1)} custom-call(f32[128,2560]{1,0:T(8,128)S(1)} %convert_add_fusion.1.b1_ref, f32[128,2560]{1,0:T(8,128)S(1)} %convert_add_fusion.b2_ref, bf16[128,2560]{1,0:T(8,128)(2,1)S(1)} %collective-permute-done.16.u_ref, bf16[128,2560]{1,0:T(8,128)(2,1)S(1)} %collective-permute-done.18.v_ref, f32[1,5120]{1,0:T(1,128)S(1)} %bitcast.3, ...), custom_call_target="tpu_custom_call" | custom-call | tf_op jit(solution)/shard_map/final_norm/pallas_call | solution.py:267
  (41 shorter events, 1.9 us)
Async XLA Ops:
  0.0 22.6 %copy-start = (bf16[512,5120]{1,0:T(8,128)(2,1)S(1)}, bf16[512,5120]{1,0:T(8,128)(2,1)}, u32[]{:S(2)}) copy-start(bf16[512,5120]{1,0:T(8,128)(2,1)} %x_ref.3) | copy-start | bytes 15728644
  5.6 10.6 %collective-permute-start.3 = (bf16[512,256]{1,0:T(8,128)(2,1)}, bf16[512,256]{1,0:T(8,128)(2,1)S(1)}, u32[]{:S(2)}, u32[]{:S(2)}) collective-permute-start(bf16[512,256]{1,0:T(8,128)(2,1)} %kv_project.1.refs_0_), channel_id=1, source_target_pairs={{0,16},{8,24},{16,32},{24,40},{32,48},{40,56},{48,0},{56,8},{1,17}... | collective-permute-start | bytes 786440 | tf_op jit(solution)/shard_map/ppermute | solution.py:292
  7.6 9.2 %collective-permute-start.1 = (bf16[512,256]{1,0:T(8,128)(2,1)}, bf16[512,256]{1,0:T(8,128)(2,1)S(1)}, u32[]{:S(2)}, u32[]{:S(2)}) collective-permute-start(bf16[512,256]{1,0:T(8,128)(2,1)} %kv_project.1.refs_0_), channel_id=1, source_target_pairs={{0,48},{8,56},{16,0},{24,8},{32,16},{40,24},{48,32},{56,40},{1,49}... | collective-permute-start | bytes 786440 | tf_op jit(solution)/shard_map/ppermute | solution.py:292
  9.8 9.4 %collective-permute-start = (bf16[512,256]{1,0:T(8,128)(2,1)}, bf16[512,256]{1,0:T(8,128)(2,1)S(1)}, u32[]{:S(2)}, u32[]{:S(2)}) collective-permute-start(bf16[512,256]{1,0:T(8,128)(2,1)} %kv_project.1.refs_0_), channel_id=1, source_target_pairs={{0,8},{8,0},{16,24},{24,16},{32,40},{40,32},{48,56},{56,48},{1,9},... | collective-permute-start | bytes 786440 | tf_op jit(solution)/shard_map/ppermute | solution.py:292
  10.6 19.8 %collective-permute-start.9 = (bf16[512,256]{1,0:T(8,128)(2,1)}, bf16[512,256]{1,0:T(8,128)(2,1)S(1)}, u32[]{:S(2)}, u32[]{:S(2)}) collective-permute-start(bf16[512,256]{1,0:T(8,128)(2,1)} %kv_project.1.refs_0_), channel_id=1, source_target_pairs={{0,40},{8,32},{16,56},{24,48},{32,8},{40,0},{48,24},{56,16},{1,41}... | collective-permute-start | bytes 786440 | tf_op jit(solution)/shard_map/ppermute | solution.py:292
  13.1 17.4 %collective-permute-start.5 = (bf16[512,256]{1,0:T(8,128)(2,1)}, bf16[512,256]{1,0:T(8,128)(2,1)S(1)}, u32[]{:S(2)}, u32[]{:S(2)}) collective-permute-start(bf16[512,256]{1,0:T(8,128)(2,1)} %kv_project.1.refs_0_), channel_id=1, source_target_pairs={{0,4},{4,0},{1,5},{5,1},{2,6},{6,2},{3,7},{7,3},{8,12},{12,8},{9,1... | collective-permute-start | bytes 786440 | tf_op jit(solution)/shard_map/ppermute | solution.py:283
  16.3 14.7 %collective-permute-start.8 = (bf16[512,256]{1,0:T(8,128)(2,1)S(1)}, bf16[512,256]{1,0:T(8,128)(2,1)S(1)}, u32[]{:S(2)}, u32[]{:S(2)}) collective-permute-start(bf16[512,256]{1,0:T(8,128)(2,1)S(1)} %collective-permute-done.3.refs_6_), channel_id=1, source_target_pairs={{0,4},{4,0},{1,5},{5,1},{2,6},{6,2},{3,7},{7,3},{8,12},{12,8},{9,1... | collective-permute-start | bytes 786440 | tf_op jit(solution)/shard_map/ppermute | solution.py:283
  19.3 13.7 %collective-permute-start.4 = (bf16[768,256]{1,0:T(8,128)(2,1)S(1)}, bf16[768,256]{1,0:T(8,128)(2,1)S(1)}, u32[]{:S(2)}, u32[]{:S(2)}) collective-permute-start(bf16[768,256]{1,0:T(8,128)(2,1)S(1)} %get-tuple-element.39), channel_id=1, source_target_pairs={{0,16},{8,24},{16,32},{24,40},{32,48},{40,56},{48,0},{56,8},{1,17}... | collective-permute-start | bytes 1179656 | tf_op jit(solution)/shard_map/ppermute | solution.py:292
  19.4 13.3 %copy-start.2 = (bf16[512,256]{1,0:T(8,128)(2,1)S(1)}, bf16[512,256]{1,0:T(8,128)(2,1)}, u32[]{:S(2)}) copy-start(bf16[512,256]{1,0:T(8,128)(2,1)} %kv_project.1.refs_0_) | copy-start | bytes 786436
  19.4 13.6 %collective-permute-start.2 = (bf16[768,256]{1,0:T(8,128)(2,1)S(1)}, bf16[768,256]{1,0:T(8,128)(2,1)S(1)}, u32[]{:S(2)}, u32[]{:S(2)}) collective-permute-start(bf16[768,256]{1,0:T(8,128)(2,1)S(1)} %get-tuple-element.40), channel_id=1, source_target_pairs={{0,48},{8,56},{16,0},{24,8},{32,16},{40,24},{48,32},{56,40},{1,49}... | collective-permute-start | bytes 1179656 | tf_op jit(solution)/shard_map/ppermute | solution.py:292
  30.3 1.6 %collective-permute-start.7 = (bf16[512,256]{1,0:T(8,128)(2,1)S(1)}, bf16[512,256]{1,0:T(8,128)(2,1)S(1)}, u32[]{:S(2)}, u32[]{:S(2)}) collective-permute-start(bf16[512,256]{1,0:T(8,128)(2,1)S(1)} %collective-permute-done.1.refs_4_), channel_id=1, source_target_pairs={{0,4},{4,0},{1,5},{5,1},{2,6},{6,2},{3,7},{7,3},{8,12},{12,8},{9,1... | collective-permute-start | bytes 786440 | tf_op jit(solution)/shard_map/ppermute | solution.py:283
  30.5 1.9 %collective-permute-start.6 = (bf16[512,256]{1,0:T(8,128)(2,1)S(1)}, bf16[512,256]{1,0:T(8,128)(2,1)S(1)}, u32[]{:S(2)}, u32[]{:S(2)}) collective-permute-start(bf16[512,256]{1,0:T(8,128)(2,1)S(1)} %collective-permute-done.after_ref.refs_2_), channel_id=1, source_target_pairs={{0,4},{4,0},{1,5},{5,1},{2,6},{6,2},{3,7},{7,3},{8,12},{12,8},{9,1... | collective-permute-start | bytes 786440 | tf_op jit(solution)/shard_map/ppermute | solution.py:283
  30.9 1.8 %collective-permute-start.10 = (bf16[512,256]{1,0:T(8,128)(2,1)S(1)}, bf16[512,256]{1,0:T(8,128)(2,1)S(1)}, u32[]{:S(2)}, u32[]{:S(2)}) collective-permute-start(bf16[512,256]{1,0:T(8,128)(2,1)S(1)} %get-tuple-element.22.refs_8_), channel_id=1, source_target_pairs={{0,4},{4,0},{1,5},{5,1},{2,6},{6,2},{3,7},{7,3},{8,12},{12,8},{9,1... | collective-permute-start | bytes 786440 | tf_op jit(solution)/shard_map/ppermute | solution.py:283
  33.0 3.2 %slice-start = ((s8[6553600]{0:T(1024)(128)(4,1)}), s8[4194304]{0:T(1024)(128)(4,1)S(1)}, s32[]{:S(2)}) async-start(s8[6553600]{0:T(1024)(128)(4,1)} %bitcast.1), calls=%async_computation | async-start | bytes 8388608
  33.1 1.8 %collective-permute-start.11 = (bf16[768,256]{1,0:T(8,128)(2,1)S(1)}, bf16[768,256]{1,0:T(8,128)(2,1)S(1)}, u32[]{:S(2)}, u32[]{:S(2)}) collective-permute-start(bf16[768,256]{1,0:T(8,128)(2,1)S(1)} %get-tuple-element.26.refs_1_), channel_id=1, source_target_pairs={{0,4},{4,0},{1,5},{5,1},{2,6},{6,2},{3,7},{7,3},{8,12},{12,8},{9,1... | collective-permute-start | bytes 1179656 | tf_op jit(solution)/shard_map/ppermute | solution.py:283
  33.3 2.1 %collective-permute-start.12 = (bf16[768,256]{1,0:T(8,128)(2,1)S(1)}, bf16[768,256]{1,0:T(8,128)(2,1)S(1)}, u32[]{:S(2)}, u32[]{:S(2)}) collective-permute-start(bf16[768,256]{1,0:T(8,128)(2,1)S(1)} %get-tuple-element.27.refs_3_), channel_id=1, source_target_pairs={{0,4},{4,0},{1,5},{5,1},{2,6},{6,2},{3,7},{7,3},{8,12},{12,8},{9,1... | collective-permute-start | bytes 1179656 | tf_op jit(solution)/shard_map/ppermute | solution.py:283
  35.4 1.7 %slice-start.1 = ((s8[6553600]{0:T(1024)(128)(4,1)}), s8[2359296]{0:T(1024)(128)(4,1)S(1)}, s32[]{:S(2)}) async-start(s8[6553600]{0:T(1024)(128)(4,1)} %bitcast.1), calls=%async_computation.1 | async-start | bytes 4718592
  35.4 1.7 %copy-start.3 = (s32[4,16]{1,0:T(4,128)S(1)}, s32[4,16]{1,0:T(4,128)}, u32[]{:S(2)}) copy-start(s32[4,16]{1,0:T(4,128)} %anc_ref.7) | copy-start | bytes 772
  41.2 18.9 %collective-permute-start.15 = (bf16[128,2560]{1,0:T(8,128)(2,1)S(1)}, bf16[128,2560]{1,0:T(8,128)(2,1)S(1)}, u32[]{:S(2)}, u32[]{:S(2)}) collective-permute-start(bf16[128,2560]{1,0:T(8,128)(2,1)S(1)} %get-tuple-element.36), channel_id=1, source_target_pairs={{0,1},{1,2},{2,3},{3,0},{4,5},{5,6},{6,7},{7,4},{8,9},{9,10},{10,1... | collective-permute-start | bytes 1966088 | tf_op jit(solution)/shard_map/ppermute | solution.py:283
  42.7 17.8 %collective-permute-start.17 = (bf16[128,2560]{1,0:T(8,128)(2,1)S(1)}, bf16[128,2560]{1,0:T(8,128)(2,1)S(1)}, u32[]{:S(2)}, u32[]{:S(2)}) collective-permute-start(bf16[128,2560]{1,0:T(8,128)(2,1)S(1)} %get-tuple-element.38), channel_id=1, source_target_pairs={{0,3},{1,0},{2,1},{3,2},{4,7},{5,4},{6,5},{7,6},{8,11},{9,8},{10,9... | collective-permute-start | bytes 1966088 | tf_op jit(solution)/shard_map/ppermute | solution.py:283
  48.6 6.2 %copy-start.1 = (bf16[128,5120]{1,0:T(8,128)(2,1)S(1)}, bf16[128,5120]{1,0:T(8,128)(2,1)}, u32[]{:S(2)}) copy-start(bf16[128,5120]{1,0:T(8,128)(2,1)} %rest_0_.1) | copy-start | bytes 3932164
  52.7 21.7 %collective-permute-start.13 = (bf16[128,2560]{1,0:T(8,128)(2,1)S(1)}, bf16[128,2560]{1,0:T(8,128)(2,1)S(1)}, u32[]{:S(2)}, u32[]{:S(2)}) collective-permute-start(bf16[128,2560]{1,0:T(8,128)(2,1)S(1)} %get-tuple-element.32), channel_id=1, source_target_pairs={{0,3},{1,0},{2,1},{3,2},{4,7},{5,4},{6,5},{7,6},{8,11},{9,8},{10,9... | collective-permute-start | bytes 1966088 | tf_op jit(solution)/shard_map/ppermute | solution.py:283
  54.3 20.2 %collective-permute-start.14 = (bf16[128,2560]{1,0:T(8,128)(2,1)S(1)}, bf16[128,2560]{1,0:T(8,128)(2,1)S(1)}, u32[]{:S(2)}, u32[]{:S(2)}) collective-permute-start(bf16[128,2560]{1,0:T(8,128)(2,1)S(1)} %get-tuple-element.34), channel_id=1, source_target_pairs={{0,1},{1,2},{2,3},{3,0},{4,5},{5,6},{6,7},{7,4},{8,9},{9,10},{10,1... | collective-permute-start | bytes 1966088 | tf_op jit(solution)/shard_map/ppermute | solution.py:283
  60.2 27.1 %collective-permute-start.16 = (bf16[128,2560]{1,0:T(8,128)(2,1)S(1)}, bf16[128,2560]{1,0:T(8,128)(2,1)S(1)}, u32[]{:S(2)}, u32[]{:S(2)}) collective-permute-start(bf16[128,2560]{1,0:T(8,128)(2,1)S(1)} %add.14), channel_id=1, source_target_pairs={{0,1},{1,2},{2,3},{3,0},{4,5},{5,6},{6,7},{7,4},{8,9},{9,10},{10,1... | collective-permute-start | bytes 1966088 | tf_op jit(solution)/shard_map/ppermute | solution.py:283
  60.7 26.6 %collective-permute-start.18 = (bf16[128,2560]{1,0:T(8,128)(2,1)S(1)}, bf16[128,2560]{1,0:T(8,128)(2,1)S(1)}, u32[]{:S(2)}, u32[]{:S(2)}) collective-permute-start(bf16[128,2560]{1,0:T(8,128)(2,1)S(1)} %add.15), channel_id=1, source_target_pairs={{0,3},{1,0},{2,1},{3,2},{4,7},{5,4},{6,5},{7,6},{8,11},{9,8},{10,9... | collective-permute-start | bytes 1966088 | tf_op jit(solution)/shard_map/ppermute | solution.py:283
  74.5 12.8 %copy-start.4 = (f32[5120]{0:T(1024)S(1)}, f32[5120]{0:T(1024)}, u32[]{:S(2)}) copy-start(f32[5120]{0:T(1024)} %param.15) | copy-start | bytes 61444
  74.6 12.8 %copy-start.5 = (s32[4]{0:T(128)S(1)}, s32[4]{0:T(128)}, u32[]{:S(2)}) copy-start(s32[4]{0:T(128)} %keep_ref.1) | copy-start | bytes 52

commit v10 on v8

--- a/solution.py
+++ b/solution.py
@@ -48,7 +48,7 @@
 
 def kv_project(x, wk, wv):
     rows, depth = x.shape
-    parts = 5
+    parts = 2
     hbm = pl.BlockSpec(memory_space=pltpu.HBM)
     return pl.pallas_call(
         kv_kernel,

time: 90 us -> 90 us (level)
  no operation moved by 1% of the time
where the time goes in v10:
time: 90 us; the launch traced here: 89.6 us
  waiting for transfers between devices  33.9 us (38%)
  Pallas kernels  32.9 us (37%)
  starting transfers between devices  20.8 us (23%)
    ppermute x13, waiting for transfers between devices, shift(): lax.ppermute(x, axis, ring({'y': 2, 'core': 2, 'z': 4, 'tp': 4}[axis], s))  27.8 us
    pallas_call x4, Pallas kernels, block_terms(): pl.pallas_call(functools.partial(block_kernel, turn), name='block_terms',...  16.4 us
    ppermute x6, starting transfers between devices, fetch(): return lax.ppermute(x, ('z', 'y'), pairs)  10.7 us
    ppermute x13, starting transfers between devices, shift(): lax.ppermute(x, axis, ring({'y': 2, 'core': 2, 'z': 4, 'tp': 4}[axis], s))  10.1 us
    pallas_call x1, Pallas kernels, q_project(): pl.pallas_call(q_kernel, name='q_project', out_shape=jax.ShapeDtypeStruct...  7.7 us
    ppermute x6, waiting for transfers between devices, fetch(): return lax.ppermute(x, ('z', 'y'), pairs)  6.08 us
    pallas_call x1, Pallas kernels, kv_project(): pl.pallas_call(kv_kernel, name='kv_project', out_shape=jax.ShapeDtypeStru...  5.63 us
    pallas_call x1, Pallas kernels, final_norm(): pl.pallas_call(norm_kernel, name='final_norm', out_shape=jax.ShapeDtypeSt...  2.06 us
  transfers between devices with their start and end apart: 19, of which 11 were waited for; matrix products, arithmetic and copies ran while one was open for 1% of the time, Pallas kernels for 23%

profile of v10, /device:TPU:24, one launch (start us, length us, event | category | flops | bytes accessed | tf_op | source)
XLA Modules:
  0.0 89.6 jit_solution(16079160175300792716)
XLA Ops:
  0.0 5.6 %kv_project.1.refs_0_ = bf16[512,256]{1,0:T(8,128)(2,1)} custom-call(bf16[512,5120]{1,0:T(8,128)(2,1)} %x_ref.3, bf16[5120,128]{1,0:T(8,128)(2,1)} %wk_ref.1, bf16[5120,128]{1,0:T(8,128)(2,1)} %wv_ref.1), custom_call_target="tpu_custom_call" | custom-call | flops 1048576 | bytes 1048576 | tf_op jit(solution)/shard_map/kv_project/pallas_call | solution.py:53
  5.6 2.0 %collective-permute-start.3 = (bf16[512,256]{1,0:T(8,128)(2,1)}, bf16[512,256]{1,0:T(8,128)(2,1)S(1)}, u32[]{:S(2)}, u32[]{:S(2)}) collective-permute-start(bf16[512,256]{1,0:T(8,128)(2,1)} %kv_project.1.refs_0_), channel_id=1, source_target_pairs={{0,16},{8,24},{16,32},{24,40},{32,48},{40,56},{48,0},{56,8},{1,17}... | collective-permute-start | bytes 786440 | tf_op jit(solution)/shard_map/ppermute | solution.py:292
  7.6 2.2 %collective-permute-start.1 = (bf16[512,256]{1,0:T(8,128)(2,1)}, bf16[512,256]{1,0:T(8,128)(2,1)S(1)}, u32[]{:S(2)}, u32[]{:S(2)}) collective-permute-start(bf16[512,256]{1,0:T(8,128)(2,1)} %kv_project.1.refs_0_), channel_id=1, source_target_pairs={{0,48},{8,56},{16,0},{24,8},{32,16},{40,24},{48,32},{56,40},{1,49}... | collective-permute-start | bytes 786440 | tf_op jit(solution)/shard_map/ppermute | solution.py:292
  9.8 0.7 collective-permute-start
  10.6 2.5 %collective-permute-start.9 = (bf16[512,256]{1,0:T(8,128)(2,1)}, bf16[512,256]{1,0:T(8,128)(2,1)S(1)}, u32[]{:S(2)}, u32[]{:S(2)}) collective-permute-start(bf16[512,256]{1,0:T(8,128)(2,1)} %kv_project.1.refs_0_), channel_id=1, source_target_pairs={{0,40},{8,32},{16,56},{24,48},{32,8},{40,0},{48,24},{56,16},{1,41}... | collective-permute-start | bytes 786440 | tf_op jit(solution)/shard_map/ppermute | solution.py:292
  13.1 3.2 %collective-permute-done.3.refs_6_ = bf16[512,256]{1,0:T(8,128)(2,1)S(1)} collective-permute-done((bf16[512,256]{1,0:T(8,128)(2,1)}, bf16[512,256]{1,0:T(8,128)(2,1)S(1)}, u32[]{:S(2)}, u32[]{:S(2)}) %collective-permute-start.3) | collective-permute-done | bytes 262176 | tf_op jit(solution)/shard_map/ppermute | solution.py:292
  16.4 0.4 collective-permute-done.1.refs_4_
  16.8 2.4 %collective-permute-done.after_ref.refs_2_ = bf16[512,256]{1,0:T(8,128)(2,1)S(1)} collective-permute-done((bf16[512,256]{1,0:T(8,128)(2,1)}, bf16[512,256]{1,0:T(8,128)(2,1)S(1)}, u32[]{:S(2)}, u32[]{:S(2)}) %collective-permute-start) | collective-permute-done | bytes 262176 | tf_op jit(solution)/shard_map/ppermute | solution.py:292
  19.4 3.2 %collective-permute-start.2 = (bf16[768,256]{1,0:T(8,128)(2,1)S(1)}, bf16[768,256]{1,0:T(8,128)(2,1)S(1)}, u32[]{:S(2)}, u32[]{:S(2)}) collective-permute-start(bf16[768,256]{1,0:T(8,128)(2,1)S(1)} %get-tuple-element.40), channel_id=1, source_target_pairs={{0,48},{8,56},{16,0},{24,8},{32,16},{40,24},{48,32},{56,40},{1,49}... | collective-permute-start | bytes 1179656 | tf_op jit(solution)/shard_map/ppermute | solution.py:292
  22.6 7.7 %q_project.1.refs_1_ = bf16[512,640]{1,0:T(8,128)(2,1)S(1)} custom-call(bf16[512,5120]{1,0:T(8,128)(2,1)S(1)} %copy-done, bf16[5120,640]{1,0:T(8,128)(2,1)} %w_ref.5, bf16[512,256]{1,0:T(8,128)(2,1)S(1)} %collective-permute-done.after_ref.refs_2_), custom_call_target="tpu_custom_call" | custom-call | flops 1048576 | bytes 1048576 | tf_op jit(solution)/shard_map/q_project/pallas_call | solution.py:88
  30.5 0.5 collective-permute-start.6
  31.1 0.9 %collective-permute-done.7.refs_5_ = bf16[512,256]{1,0:T(8,128)(2,1)S(1)} collective-permute-done((bf16[512,256]{1,0:T(8,128)(2,1)S(1)}, bf16[512,256]{1,0:T(8,128)(2,1)S(1)}, u32[]{:S(2)}, u32[]{:S(2)}) %collective-permute-start.7) | collective-permute-done | bytes 262176 | tf_op jit(solution)/shard_map/ppermute | solution.py:283
  32.0 0.4 collective-permute-done.6.refs_3_
  32.3 0.4 collective-permute-done.10.refs_9_
  33.3 0.4 collective-permute-start.12
  33.6 1.2 %collective-permute-done.11.refs_2_ = bf16[768,256]{1,0:T(8,128)(2,1)S(1)} collective-permute-done((bf16[768,256]{1,0:T(8,128)(2,1)S(1)}, bf16[768,256]{1,0:T(8,128)(2,1)S(1)}, u32[]{:S(2)}, u32[]{:S(2)}) %collective-permute-start.11) | collective-permute-done | bytes 393248 | tf_op jit(solution)/shard_map/ppermute | solution.py:283
  34.9 0.6 collective-permute-done.12.refs_4_
  35.4 0.8 collect.3.kv_ref
  36.3 0.8 slice-done.1
  37.1 4.1 %block_terms.4 = (bf16[128,2560]{1,0:T(8,128)(2,1)S(1)}, bf16[128,2560]{1,0:T(8,128)(2,1)S(1)}, bf16[8192,256]{1,0:T(8,128)(2,1)S(1)}) custom-call(s32[4,16]{1,0:T(4,128)S(1)} %copy-done.3, bf16[512,640]{1,0:T(8,128)(2,1)S(1)} %get-tuple-element.24.q_ref, bf16[8192,256]{1,0:T(8,128)(2,1)S(1)} %collect.3.kv_ref, ...), custom_call_target="tpu_custom_call", output_to_operand_aliasing={{2}: (2, {})} | custom-call | flops 1048576 | bytes 1048576 | tf_op jit(solution)/shard_map/block_terms/pallas_call | solution.py:227
  41.2 1.6 %collective-permute-start.15 = (bf16[128,2560]{1,0:T(8,128)(2,1)S(1)}, bf16[128,2560]{1,0:T(8,128)(2,1)S(1)}, u32[]{:S(2)}, u32[]{:S(2)}) collective-permute-start(bf16[128,2560]{1,0:T(8,128)(2,1)S(1)} %get-tuple-element.36), channel_id=1, source_target_pairs={{0,1},{1,2},{2,3},{3,0},{4,5},{5,6},{6,7},{7,4},{8,9},{9,10},{10,1... | collective-permute-start | bytes 1966088 | tf_op jit(solution)/shard_map/ppermute | solution.py:283
  42.8 1.7 %collective-permute-start.17 = (bf16[128,2560]{1,0:T(8,128)(2,1)S(1)}, bf16[128,2560]{1,0:T(8,128)(2,1)S(1)}, u32[]{:S(2)}, u32[]{:S(2)}) collective-permute-start(bf16[128,2560]{1,0:T(8,128)(2,1)S(1)} %get-tuple-element.38), channel_id=1, source_target_pairs={{0,3},{1,0},{2,1},{3,2},{4,7},{5,4},{6,5},{7,6},{8,11},{9,8},{10,9... | collective-permute-start | bytes 1966088 | tf_op jit(solution)/shard_map/ppermute | solution.py:283
  44.5 4.1 %block_terms.5 = (bf16[128,2560]{1,0:T(8,128)(2,1)S(1)}, bf16[128,2560]{1,0:T(8,128)(2,1)S(1)}, bf16[8192,256]{1,0:T(8,128)(2,1)S(1)}) custom-call(s32[4,16]{1,0:T(4,128)S(1)} %copy-done.3, bf16[512,640]{1,0:T(8,128)(2,1)S(1)} %get-tuple-element.24.q_ref, bf16[8192,256]{1,0:T(8,128)(2,1)S(1)} %get-tuple-element.28.kv_ref, ...), custom_call_target="tpu_custom_call", output_to_operand_aliasing={{2}: (2, {})} | custom-call | flops 1048576 | bytes 1048576 | tf_op jit(solution)/shard_map/block_terms/pallas_call | solution.py:227
  48.6 4.1 %block_terms.6 = (bf16[128,2560]{1,0:T(8,128)(2,1)S(1)}, bf16[128,2560]{1,0:T(8,128)(2,1)S(1)}, bf16[8192,256]{1,0:T(8,128)(2,1)S(1)}) custom-call(s32[4,16]{1,0:T(4,128)S(1)} %copy-done.3, bf16[512,640]{1,0:T(8,128)(2,1)S(1)} %get-tuple-element.24.q_ref, bf16[8192,256]{1,0:T(8,128)(2,1)S(1)} %get-tuple-element.29.kv_ref, ...), custom_call_target="tpu_custom_call", output_to_operand_aliasing={{2}: (2, {})} | custom-call | flops 1048576 | bytes 1048576 | tf_op jit(solution)/shard_map/block_terms/pallas_call | solution.py:227
  52.7 1.6 %collective-permute-start.13 = (bf16[128,2560]{1,0:T(8,128)(2,1)S(1)}, bf16[128,2560]{1,0:T(8,128)(2,1)S(1)}, u32[]{:S(2)}, u32[]{:S(2)}) collective-permute-start(bf16[128,2560]{1,0:T(8,128)(2,1)S(1)} %get-tuple-element.32), channel_id=1, source_target_pairs={{0,3},{1,0},{2,1},{3,2},{4,7},{5,4},{6,5},{7,6},{8,11},{9,8},{10,9... | collective-permute-start | bytes 1966088 | tf_op jit(solution)/shard_map/ppermute | solution.py:283
  54.3 0.5 collective-permute-start.14
  54.8 4.2 %block_terms.7 = (f32[128,2560]{1,0:T(8,128)S(1)}, f32[128,2560]{1,0:T(8,128)S(1)}, bf16[8192,256]{1,0:T(8,128)(2,1)S(1)}) custom-call(s32[4,16]{1,0:T(4,128)S(1)} %copy-done.3, bf16[512,640]{1,0:T(8,128)(2,1)S(1)} %get-tuple-element.24.q_ref, bf16[8192,256]{1,0:T(8,128)(2,1)S(1)} %get-tuple-element.30.kv_ref, ...), custom_call_target="tpu_custom_call", output_to_operand_aliasing={{2}: (2, {})} | custom-call | flops 1048576 | bytes 1048576 | tf_op jit(solution)/shard_map/block_terms/pallas_call | solution.py:227
  59.0 1.1 %collective-permute-done.15 = bf16[128,2560]{1,0:T(8,128)(2,1)S(1)} collective-permute-done((bf16[128,2560]{1,0:T(8,128)(2,1)S(1)}, bf16[128,2560]{1,0:T(8,128)(2,1)S(1)}, u32[]{:S(2)}, u32[]{:S(2)}) %collective-permute-start.15) | collective-permute-done | bytes 655392 | tf_op jit(solution)/shard_map/ppermute | solution.py:283
  60.7 3.0 %collective-permute-start.18 = (bf16[128,2560]{1,0:T(8,128)(2,1)S(1)}, bf16[128,2560]{1,0:T(8,128)(2,1)S(1)}, u32[]{:S(2)}, u32[]{:S(2)}) collective-permute-start(bf16[128,2560]{1,0:T(8,128)(2,1)S(1)} %add.15), channel_id=1, source_target_pairs={{0,3},{1,0},{2,1},{3,2},{4,7},{5,4},{6,5},{7,6},{8,11},{9,8},{10,9... | collective-permute-start | bytes 1966088 | tf_op jit(solution)/shard_map/ppermute | solution.py:283
  63.8 10.7 %collective-permute-done.13 = bf16[128,2560]{1,0:T(8,128)(2,1)S(1)} collective-permute-done((bf16[128,2560]{1,0:T(8,128)(2,1)S(1)}, bf16[128,2560]{1,0:T(8,128)(2,1)S(1)}, u32[]{:S(2)}, u32[]{:S(2)}) %collective-permute-start.13) | collective-permute-done | bytes 655392 | tf_op jit(solution)/shard_map/ppermute | solution.py:283
  74.7 12.6 %collective-permute-done.16.u_ref = bf16[128,2560]{1,0:T(8,128)(2,1)S(1)} collective-permute-done((bf16[128,2560]{1,0:T(8,128)(2,1)S(1)}, bf16[128,2560]{1,0:T(8,128)(2,1)S(1)}, u32[]{:S(2)}, u32[]{:S(2)}) %collective-permute-start.16) | collective-permute-done | bytes 655392 | tf_op jit(solution)/shard_map/ppermute | solution.py:283
  87.4 2.1 %final_norm.1 = bf16[128,5120]{1,0:T(8,128)(2,1)} custom-call(f32[128,2560]{1,0:T(8,128)S(1)} %convert_add_fusion.1.b1_ref, f32[128,2560]{1,0:T(8,128)S(1)} %convert_add_fusion.b2_ref, bf16[128,2560]{1,0:T(8,128)(2,1)S(1)} %collective-permute-done.16.u_ref, bf16[128,2560]{1,0:T(8,128)(2,1)S(1)} %collective-permute-done.18.v_ref, f32[1,5120]{1,0:T(1,128)S(1)} %bitcast.3, ...), custom_call_target="tpu_custom_call" | custom-call | tf_op jit(solution)/shard_map/final_norm/pallas_call | solution.py:267
  (41 shorter events, 1.9 us)
Async XLA Ops:
  0.0 22.6 %copy-start = (bf16[512,5120]{1,0:T(8,128)(2,1)S(1)}, bf16[512,5120]{1,0:T(8,128)(2,1)}, u32[]{:S(2)}) copy-start(bf16[512,5120]{1,0:T(8,128)(2,1)} %x_ref.3) | copy-start | bytes 15728644
  5.6 10.6 %collective-permute-start.3 = (bf16[512,256]{1,0:T(8,128)(2,1)}, bf16[512,256]{1,0:T(8,128)(2,1)S(1)}, u32[]{:S(2)}, u32[]{:S(2)}) collective-permute-start(bf16[512,256]{1,0:T(8,128)(2,1)} %kv_project.1.refs_0_), channel_id=1, source_target_pairs={{0,16},{8,24},{16,32},{24,40},{32,48},{40,56},{48,0},{56,8},{1,17}... | collective-permute-start | bytes 786440 | tf_op jit(solution)/shard_map/ppermute | solution.py:292
  7.6 9.2 %collective-permute-start.1 = (bf16[512,256]{1,0:T(8,128)(2,1)}, bf16[512,256]{1,0:T(8,128)(2,1)S(1)}, u32[]{:S(2)}, u32[]{:S(2)}) collective-permute-start(bf16[512,256]{1,0:T(8,128)(2,1)} %kv_project.1.refs_0_), channel_id=1, source_target_pairs={{0,48},{8,56},{16,0},{24,8},{32,16},{40,24},{48,32},{56,40},{1,49}... | collective-permute-start | bytes 786440 | tf_op jit(solution)/shard_map/ppermute | solution.py:292
  9.8 9.4 %collective-permute-start = (bf16[512,256]{1,0:T(8,128)(2,1)}, bf16[512,256]{1,0:T(8,128)(2,1)S(1)}, u32[]{:S(2)}, u32[]{:S(2)}) collective-permute-start(bf16[512,256]{1,0:T(8,128)(2,1)} %kv_project.1.refs_0_), channel_id=1, source_target_pairs={{0,8},{8,0},{16,24},{24,16},{32,40},{40,32},{48,56},{56,48},{1,9},... | collective-permute-start | bytes 786440 | tf_op jit(solution)/shard_map/ppermute | solution.py:292
  10.6 19.8 %collective-permute-start.9 = (bf16[512,256]{1,0:T(8,128)(2,1)}, bf16[512,256]{1,0:T(8,128)(2,1)S(1)}, u32[]{:S(2)}, u32[]{:S(2)}) collective-permute-start(bf16[512,256]{1,0:T(8,128)(2,1)} %kv_project.1.refs_0_), channel_id=1, source_target_pairs={{0,40},{8,32},{16,56},{24,48},{32,8},{40,0},{48,24},{56,16},{1,41}... | collective-permute-start | bytes 786440 | tf_op jit(solution)/shard_map/ppermute | solution.py:292
  13.1 17.4 %collective-permute-start.5 = (bf16[512,256]{1,0:T(8,128)(2,1)}, bf16[512,256]{1,0:T(8,128)(2,1)S(1)}, u32[]{:S(2)}, u32[]{:S(2)}) collective-permute-start(bf16[512,256]{1,0:T(8,128)(2,1)} %kv_project.1.refs_0_), channel_id=1, source_target_pairs={{0,4},{4,0},{1,5},{5,1},{2,6},{6,2},{3,7},{7,3},{8,12},{12,8},{9,1... | collective-permute-start | bytes 786440 | tf_op jit(solution)/shard_map/ppermute | solution.py:283
  16.3 14.7 %collective-permute-start.8 = (bf16[512,256]{1,0:T(8,128)(2,1)S(1)}, bf16[512,256]{1,0:T(8,128)(2,1)S(1)}, u32[]{:S(2)}, u32[]{:S(2)}) collective-permute-start(bf16[512,256]{1,0:T(8,128)(2,1)S(1)} %collective-permute-done.3.refs_6_), channel_id=1, source_target_pairs={{0,4},{4,0},{1,5},{5,1},{2,6},{6,2},{3,7},{7,3},{8,12},{12,8},{9,1... | collective-permute-start | bytes 786440 | tf_op jit(solution)/shard_map/ppermute | solution.py:283
  19.3 13.7 %collective-permute-start.4 = (bf16[768,256]{1,0:T(8,128)(2,1)S(1)}, bf16[768,256]{1,0:T(8,128)(2,1)S(1)}, u32[]{:S(2)}, u32[]{:S(2)}) collective-permute-start(bf16[768,256]{1,0:T(8,128)(2,1)S(1)} %get-tuple-element.39), channel_id=1, source_target_pairs={{0,16},{8,24},{16,32},{24,40},{32,48},{40,56},{48,0},{56,8},{1,17}... | collective-permute-start | bytes 1179656 | tf_op jit(solution)/shard_map/ppermute | solution.py:292
  19.4 13.3 %copy-start.2 = (bf16[512,256]{1,0:T(8,128)(2,1)S(1)}, bf16[512,256]{1,0:T(8,128)(2,1)}, u32[]{:S(2)}) copy-start(bf16[512,256]{1,0:T(8,128)(2,1)} %kv_project.1.refs_0_) | copy-start | bytes 786436
  19.4 13.6 %collective-permute-start.2 = (bf16[768,256]{1,0:T(8,128)(2,1)S(1)}, bf16[768,256]{1,0:T(8,128)(2,1)S(1)}, u32[]{:S(2)}, u32[]{:S(2)}) collective-permute-start(bf16[768,256]{1,0:T(8,128)(2,1)S(1)} %get-tuple-element.40), channel_id=1, source_target_pairs={{0,48},{8,56},{16,0},{24,8},{32,16},{40,24},{48,32},{56,40},{1,49}... | collective-permute-start | bytes 1179656 | tf_op jit(solution)/shard_map/ppermute | solution.py:292
  30.3 1.6 %collective-permute-start.7 = (bf16[512,256]{1,0:T(8,128)(2,1)S(1)}, bf16[512,256]{1,0:T(8,128)(2,1)S(1)}, u32[]{:S(2)}, u32[]{:S(2)}) collective-permute-start(bf16[512,256]{1,0:T(8,128)(2,1)S(1)} %collective-permute-done.1.refs_4_), channel_id=1, source_target_pairs={{0,4},{4,0},{1,5},{5,1},{2,6},{6,2},{3,7},{7,3},{8,12},{12,8},{9,1... | collective-permute-start | bytes 786440 | tf_op jit(solution)/shard_map/ppermute | solution.py:283
  30.5 1.9 %collective-permute-start.6 = (bf16[512,256]{1,0:T(8,128)(2,1)S(1)}, bf16[512,256]{1,0:T(8,128)(2,1)S(1)}, u32[]{:S(2)}, u32[]{:S(2)}) collective-permute-start(bf16[512,256]{1,0:T(8,128)(2,1)S(1)} %collective-permute-done.after_ref.refs_2_), channel_id=1, source_target_pairs={{0,4},{4,0},{1,5},{5,1},{2,6},{6,2},{3,7},{7,3},{8,12},{12,8},{9,1... | collective-permute-start | bytes 786440 | tf_op jit(solution)/shard_map/ppermute | solution.py:283
  30.9 1.8 %collective-permute-start.10 = (bf16[512,256]{1,0:T(8,128)(2,1)S(1)}, bf16[512,256]{1,0:T(8,128)(2,1)S(1)}, u32[]{:S(2)}, u32[]{:S(2)}) collective-permute-start(bf16[512,256]{1,0:T(8,128)(2,1)S(1)} %get-tuple-element.22.refs_8_), channel_id=1, source_target_pairs={{0,4},{4,0},{1,5},{5,1},{2,6},{6,2},{3,7},{7,3},{8,12},{12,8},{9,1... | collective-permute-start | bytes 786440 | tf_op jit(solution)/shard_map/ppermute | solution.py:283
  33.0 3.2 %slice-start = ((s8[6553600]{0:T(1024)(128)(4,1)}), s8[4194304]{0:T(1024)(128)(4,1)S(1)}, s32[]{:S(2)}) async-start(s8[6553600]{0:T(1024)(128)(4,1)} %bitcast.1), calls=%async_computation | async-start | bytes 8388608
  33.1 1.8 %collective-permute-start.11 = (bf16[768,256]{1,0:T(8,128)(2,1)S(1)}, bf16[768,256]{1,0:T(8,128)(2,1)S(1)}, u32[]{:S(2)}, u32[]{:S(2)}) collective-permute-start(bf16[768,256]{1,0:T(8,128)(2,1)S(1)} %get-tuple-element.26.refs_1_), channel_id=1, source_target_pairs={{0,4},{4,0},{1,5},{5,1},{2,6},{6,2},{3,7},{7,3},{8,12},{12,8},{9,1... | collective-permute-start | bytes 1179656 | tf_op jit(solution)/shard_map/ppermute | solution.py:283
  33.3 2.1 %collective-permute-start.12 = (bf16[768,256]{1,0:T(8,128)(2,1)S(1)}, bf16[768,256]{1,0:T(8,128)(2,1)S(1)}, u32[]{:S(2)}, u32[]{:S(2)}) collective-permute-start(bf16[768,256]{1,0:T(8,128)(2,1)S(1)} %get-tuple-element.27.refs_3_), channel_id=1, source_target_pairs={{0,4},{4,0},{1,5},{5,1},{2,6},{6,2},{3,7},{7,3},{8,12},{12,8},{9,1... | collective-permute-start | bytes 1179656 | tf_op jit(solution)/shard_map/ppermute | solution.py:283
  35.4 1.7 %slice-start.1 = ((s8[6553600]{0:T(1024)(128)(4,1)}), s8[2359296]{0:T(1024)(128)(4,1)S(1)}, s32[]{:S(2)}) async-start(s8[6553600]{0:T(1024)(128)(4,1)} %bitcast.1), calls=%async_computation.1 | async-start | bytes 4718592
  35.4 1.7 %copy-start.3 = (s32[4,16]{1,0:T(4,128)S(1)}, s32[4,16]{1,0:T(4,128)}, u32[]{:S(2)}) copy-start(s32[4,16]{1,0:T(4,128)} %anc_ref.7) | copy-start | bytes 772
  41.2 18.9 %collective-permute-start.15 = (bf16[128,2560]{1,0:T(8,128)(2,1)S(1)}, bf16[128,2560]{1,0:T(8,128)(2,1)S(1)}, u32[]{:S(2)}, u32[]{:S(2)}) collective-permute-start(bf16[128,2560]{1,0:T(8,128)(2,1)S(1)} %get-tuple-element.36), channel_id=1, source_target_pairs={{0,1},{1,2},{2,3},{3,0},{4,5},{5,6},{6,7},{7,4},{8,9},{9,10},{10,1... | collective-permute-start | bytes 1966088 | tf_op jit(solution)/shard_map/ppermute | solution.py:283
  42.8 17.8 %collective-permute-start.17 = (bf16[128,2560]{1,0:T(8,128)(2,1)S(1)}, bf16[128,2560]{1,0:T(8,128)(2,1)S(1)}, u32[]{:S(2)}, u32[]{:S(2)}) collective-permute-start(bf16[128,2560]{1,0:T(8,128)(2,1)S(1)} %get-tuple-element.38), channel_id=1, source_target_pairs={{0,3},{1,0},{2,1},{3,2},{4,7},{5,4},{6,5},{7,6},{8,11},{9,8},{10,9... | collective-permute-start | bytes 1966088 | tf_op jit(solution)/shard_map/ppermute | solution.py:283
  48.6 6.2 %copy-start.1 = (bf16[128,5120]{1,0:T(8,128)(2,1)S(1)}, bf16[128,5120]{1,0:T(8,128)(2,1)}, u32[]{:S(2)}) copy-start(bf16[128,5120]{1,0:T(8,128)(2,1)} %rest_0_.1) | copy-start | bytes 3932164
  52.7 21.7 %collective-permute-start.13 = (bf16[128,2560]{1,0:T(8,128)(2,1)S(1)}, bf16[128,2560]{1,0:T(8,128)(2,1)S(1)}, u32[]{:S(2)}, u32[]{:S(2)}) collective-permute-start(bf16[128,2560]{1,0:T(8,128)(2,1)S(1)} %get-tuple-element.32), channel_id=1, source_target_pairs={{0,3},{1,0},{2,1},{3,2},{4,7},{5,4},{6,5},{7,6},{8,11},{9,8},{10,9... | collective-permute-start | bytes 1966088 | tf_op jit(solution)/shard_map/ppermute | solution.py:283
  54.3 20.2 %collective-permute-start.14 = (bf16[128,2560]{1,0:T(8,128)(2,1)S(1)}, bf16[128,2560]{1,0:T(8,128)(2,1)S(1)}, u32[]{:S(2)}, u32[]{:S(2)}) collective-permute-start(bf16[128,2560]{1,0:T(8,128)(2,1)S(1)} %get-tuple-element.34), channel_id=1, source_target_pairs={{0,1},{1,2},{2,3},{3,0},{4,5},{5,6},{6,7},{7,4},{8,9},{9,10},{10,1... | collective-permute-start | bytes 1966088 | tf_op jit(solution)/shard_map/ppermute | solution.py:283
  60.2 27.1 %collective-permute-start.16 = (bf16[128,2560]{1,0:T(8,128)(2,1)S(1)}, bf16[128,2560]{1,0:T(8,128)(2,1)S(1)}, u32[]{:S(2)}, u32[]{:S(2)}) collective-permute-start(bf16[128,2560]{1,0:T(8,128)(2,1)S(1)} %add.14), channel_id=1, source_target_pairs={{0,1},{1,2},{2,3},{3,0},{4,5},{5,6},{6,7},{7,4},{8,9},{9,10},{10,1... | collective-permute-start | bytes 1966088 | tf_op jit(solution)/shard_map/ppermute | solution.py:283
  60.7 26.6 %collective-permute-start.18 = (bf16[128,2560]{1,0:T(8,128)(2,1)S(1)}, bf16[128,2560]{1,0:T(8,128)(2,1)S(1)}, u32[]{:S(2)}, u32[]{:S(2)}) collective-permute-start(bf16[128,2560]{1,0:T(8,128)(2,1)S(1)} %add.15), channel_id=1, source_target_pairs={{0,3},{1,0},{2,1},{3,2},{4,7},{5,4},{6,5},{7,6},{8,11},{9,8},{10,9... | collective-permute-start | bytes 1966088 | tf_op jit(solution)/shard_map/ppermute | solution.py:283
  74.6 12.8 %copy-start.4 = (f32[5120]{0:T(1024)S(1)}, f32[5120]{0:T(1024)}, u32[]{:S(2)}) copy-start(f32[5120]{0:T(1024)} %param.15) | copy-start | bytes 61444
  74.6 12.8 %copy-start.5 = (s32[4]{0:T(128)S(1)}, s32[4]{0:T(128)}, u32[]{:S(2)}) copy-start(s32[4]{0:T(128)} %keep_ref.1) | copy-start | bytes 52
